TPU v7x, 32 devices: a whole 2x2x4 slice. The times are simulated.
32 devices in a mesh: groups: 2 (over y), seq: 4 (over z), head: 2 (over x), sub: 2 (over core).
Axes of the slice: x: 2, y: 2, z: 4, core: 2. Of those that a mesh axis runs over, the one named last changes fastest.
Arguments:
- queries: bfloat16 [1024, 4096], P(('groups', 'seq'), ('head', 'sub')), parts along dimension 0, may hold values from -6 to 6
- keys: bfloat16 [1024, 4096], P(('groups', 'seq'), ('head', 'sub')), parts along dimension 0, may hold values from -6 to 6
- values: bfloat16 [1024, 4096], P(('groups', 'seq'), ('head', 'sub')), parts along dimension 0, may hold values from -6 to 6
- level_index: int32 [1024, 21], P(('groups', 'seq')), parts along dimension 0, may hold values from 0 to 15
- level_table: float32 [16, 32], P(None, ('head', 'sub')), may hold values from 0.01 to 0.1
- out_weight: bfloat16 [4096, 2048], P(('head', 'sub')), may hold values from -0.09375 to 0.09375
- residual: bfloat16 [1024, 2048], P(('groups', 'seq', 'sub')), parts along dimension 0, may hold values from -6 to 6
- norm_gain: float32 [2048], replicated, may hold values from 0.5 to 1.5
- expert_ids: int32 [1024, 8], P(('groups', 'seq', 'sub')), parts along dimension 0, may hold values from 0 to 63, as said below
- expert_slots: int32 [1024, 8], P(('groups', 'seq', 'sub')), parts along dimension 0, may hold values from -1 to 11, as said below
- route_weight: float32 [1024, 8], P(('groups', 'seq', 'sub')), parts along dimension 0, may hold values from 0.6 to 1
- w_gate_up: bfloat16 [64, 2048, 2, 768], P(('seq', 'sub'), None, None, 'head'), may hold values from -0.125 to 0.125
- w_down: bfloat16 [64, 768, 2048], P(('seq', 'sub'), 'head'), may hold values from -0.21875 to 0.21875
Outputs:
- layer_out: bfloat16 [1024, 2048], P(('groups', 'seq', 'sub'), 'head'), parts along dimension 0
There are 2 independent parts, one for each index of `groups`. A program takes and returns all parts, laid end to end along the dimension named above; an argument that names none is the same for every part. Nothing has to cross between parts.
Inputs may be any that keep to these rules, and one draw needn't show every extreme that they name: `expert_ids`: the 8 ids of a token are different. `expert_slots`: -1 marks a dropped pair. Within an aligned block of 64 tokens, kept pairs that name the same expert have different slots; in every block some expert has all 12 slots taken.
All inputs are finite; a program needn't handle non-finite values.
Results may differ from a plain program's by a relative error of at most 0.018.
Values may be sent and summed in bfloat16 or wider, within the bound.
No kernel may reach another device: no remote copies, remote signals or barrier semaphores. Data moves between devices by JAX's collectives and lax.ppermute only.
A program may use at most 128 MiB of HBM per device.

v0:
```python
import jax
import jax.numpy as jnp
from jax import lax
from jax.sharding import PartitionSpec as P

D = 2048
HEAD_DIM = 128
EXPERTS = 64
TOPK = 8
LOCAL_LEVELS = 8


def swapped(value, axis, distance):
    mask = 2**distance
    pairs = [(source, source ^ mask) for source in range(lax.axis_size(axis))]
    return lax.ppermute(value, axis, pairs)


def bit_length(numbers, digits):
    counted = jnp.zeros_like(numbers)
    for place_bit in range(digits):
        counted = counted + (numbers >= 1 << place_bit).astype(jnp.int32)
    return counted


def on_device(
    queries,
    keys,
    values,
    level_index,
    level_table,
    out_weight,
    residual,
    norm_gain,
    expert_ids,
    expert_slots,
    route_weight,
    w_gate_up,
    w_down,
):
    block_len = queries.shape[0]
    heads_here = queries.shape[1] // HEAD_DIM
    inv_root = HEAD_DIM ** (-0.5)
    query_cube = queries.reshape(block_len, heads_here, HEAD_DIM)
    key_cube = keys.reshape(block_len, heads_here, HEAD_DIM)
    value_cube = values.reshape(block_len, heads_here, HEAD_DIM)
    table_rows = level_table.shape[0]
    lookup = (
        level_index[:, :, None] == jnp.arange(table_rows, dtype=jnp.int32)[None, None, :]
    ).astype(jnp.float32)
    level_weight = jnp.einsum("tlr,rh->tlh", lookup, level_table, precision=lax.Precision.HIGHEST)
    block_state = jnp.einsum(
        "shd,she->hde", key_cube, value_cube, preferred_element_type=jnp.float32
    ).astype(jnp.bfloat16)
    seq_bits = lax.axis_size("seq").bit_length() - 1
    my_block = lax.axis_index("seq")
    running = block_state.astype(jnp.float32)
    levels_found = []
    for place_bit in range(seq_bits):
        partner = swapped(running.astype(jnp.bfloat16), "seq", place_bit).astype(running.dtype)
        owned_bit = (my_block >> place_bit & 1).astype(jnp.float32)
        levels_found.append(partner * owned_bit)
        running = running + partner
    stacked = jnp.stack(levels_found)
    level_states = stacked.astype(jnp.bfloat16)
    position = jnp.arange(block_len, dtype=jnp.int32)
    bit_depth = bit_length(position[:, None] ^ position[None, :], LOCAL_LEVELS)
    causal = position[None, :] <= position[:, None]
    mixed_weights = jnp.zeros((heads_here, block_len, block_len), jnp.float32)
    for level_id in range(LOCAL_LEVELS):
        mixed_weights = jnp.where(
            (causal & (bit_depth == level_id))[None],
            jnp.transpose(level_weight[:, level_id, :])[:, :, None],
            mixed_weights,
        )
    scores = jnp.einsum("thd,shd->hts", query_cube, key_cube, preferred_element_type=jnp.float32)
    mixed_scores = (scores * mixed_weights).astype(jnp.bfloat16)
    within_block = jnp.einsum(
        "hts,she->the", mixed_scores, value_cube, preferred_element_type=jnp.float32
    )
    level_reads = jnp.einsum(
        "thd,jhde->tjhe", query_cube, level_states, preferred_element_type=jnp.float32
    )
    across_blocks = jnp.sum(
        level_weight[:, LOCAL_LEVELS : LOCAL_LEVELS + seq_bits, :, None] * level_reads, axis=1
    )
    attended = (
        ((within_block + across_blocks) * inv_root)
        .astype(jnp.bfloat16)
        .reshape(block_len, heads_here * HEAD_DIM)
    )
    partial_value = jnp.dot(attended, out_weight, preferred_element_type=jnp.float32)
    summed = lax.psum(partial_value.astype(jnp.bfloat16), ("head", "sub")).astype(jnp.float32)
    my_tokens = residual.shape[0]
    my_rows = lax.dynamic_slice_in_dim(summed, lax.axis_index("sub") * my_tokens, my_tokens, 0)
    stream = residual.astype(jnp.float32) + my_rows
    mean_square = jnp.mean(stream * stream, axis=-1, keepdims=True)
    normed = (stream * lax.rsqrt(mean_square + 1e-06) * norm_gain).astype(jnp.bfloat16)
    capacity = 3 * (my_tokens * TOPK // EXPERTS) // 2
    slot_index = jnp.where(
        expert_slots >= 0, expert_ids * capacity + expert_slots, EXPERTS * capacity
    )
    exp_here = w_gate_up.shape[0]
    hid_part = w_down.shape[1]
    pair_weight = w_gate_up.reshape(exp_here, D, 2 * hid_part)
    kept_weight = jnp.where(expert_slots >= 0, route_weight, 0.0)
    head_count = lax.axis_size("head")
    width_part = D // head_count
    residual_part = lax.dynamic_slice_in_dim(
        stream, lax.axis_index("head") * width_part, width_part, 1
    )
    outgoing = jnp.zeros((EXPERTS * capacity, D), jnp.bfloat16)
    outgoing = outgoing.at[slot_index].set(
        jnp.broadcast_to(normed[:, None, :], (my_tokens, TOPK, D)), mode="drop"
    )
    outgoing = outgoing.reshape(EXPERTS, capacity, D)
    arrived = lax.all_to_all(outgoing, ("seq", "sub"), split_axis=0, concat_axis=0, tiled=True)
    sources = arrived.shape[0] // exp_here
    grouped = arrived.reshape(sources, exp_here, arrived.shape[1], D)
    gate_up = jnp.einsum("sxnd,xdf->sxnf", grouped, pair_weight, preferred_element_type=jnp.float32)
    active = (jax.nn.silu(gate_up[..., :hid_part]) * gate_up[..., hid_part:]).astype(jnp.bfloat16)
    result = jnp.einsum(
        "sxnf,xfd->sxnd", active, w_down, preferred_element_type=jnp.float32
    ).astype(jnp.bfloat16)
    returned = lax.all_to_all(
        result.reshape(arrived.shape), ("seq", "sub"), split_axis=0, concat_axis=0, tiled=True
    )
    returned = returned.reshape(EXPERTS * capacity, D)
    picked = jnp.take(returned, jnp.minimum(slot_index, EXPERTS * capacity - 1), axis=0)
    combined = jnp.sum(kept_weight[:, :, None] * picked, axis=1)
    expert_sum = lax.psum_scatter(
        combined.astype(jnp.bfloat16), "head", scatter_dimension=1, tiled=True
    ).astype(jnp.float32)
    return (residual_part + expert_sum).astype(jnp.bfloat16)


def solution(mesh):
    return jax.shard_map(
        on_device,
        mesh=mesh,
        in_specs=(
            P(("groups", "seq"), ("head", "sub")),
            P(("groups", "seq"), ("head", "sub")),
            P(("groups", "seq"), ("head", "sub")),
            P(("groups", "seq"), None),
            P(None, ("head", "sub")),
            P(("head", "sub"), None),
            P(("groups", "seq", "sub"), None),
            P(),
            P(("groups", "seq", "sub"), None),
            P(("groups", "seq", "sub"), None),
            P(("groups", "seq", "sub"), None),
            P(("seq", "sub"), None, None, "head"),
            P(("seq", "sub"), "head", None),
        ),
        out_specs=P(("groups", "seq", "sub"), "head"),
        check_vma=False,
    )
```

profile of v0, /device:TPU:0, one launch (start us, length us, event | category | flops | bytes accessed | tf_op | source)
XLA Modules:
  0.0 335.3 jit_solution(3788209799914021042)
XLA Ops:
  6.5 0.0 copy-start
  6.5 0.0 copy-start.4
  6.5 0.0 all-reduce.2.cloned.1.call-start
  6.5 1.2 copy.61
  7.7 0.0 copy-done
  7.7 0.2 convolution_convert_fusion.1
  8.0 3.1 collective-permute-start
  11.1 0.1 fusion.74
  11.2 0.1 fusion.76
  11.2 0.1 fusion.78
  11.3 0.9 fusion.64
  12.2 5.2 %collective-permute-done = bf16[8,128,128]{2,1,0:T(8,128)(2,1)S(1)} collective-permute-done((bf16[8,128,128]{2,1,0:T(8,128)(2,1)S(1)}, bf16[8,128,128]{2,1,0:T(8,128)(2,1)S(1)}, u32[]{:S(2)}, u32[]{:S(2)}) %collective-permute-start) | collective-permute-done | bytes 262176 | tf_op jit(solution)/shard_map/ppermute | solution.py:16
  17.4 0.1 fusion.37
  17.5 2.8 collective-permute-start.1
  20.3 0.1 fusion.80
  20.4 1.0 copy.64
  21.5 10.1 %collective-permute-done.1 = bf16[8,128,128]{2,1,0:T(8,128)(2,1)S(1)} collective-permute-done((bf16[8,128,128]{2,1,0:T(8,128)(2,1)S(1)}, bf16[8,128,128]{2,1,0:T(8,128)(2,1)S(1)}, u32[]{:S(2)}, u32[]{:S(2)}) %collective-permute-start.1) | collective-permute-done | bytes 262176 | tf_op jit(solution)/shard_map/ppermute | solution.py:16
  31.6 0.1 fusion.36
  31.6 0.4 fusion.17
  32.0 0.0 copy-done.4
  32.0 1.4 fusion.20
  33.4 0.0 copy-start.5
  33.4 0.0 copy-start.6
  33.4 0.0 copy-start.3
  33.4 0.0 copy-start.7
  33.5 3.8 %convolution_convert_fusion = bf16[128,2048]{1,0:T(8,128)(2,1)} fusion(bf16[128,1024]{0,1:T(8,128)(2,1)S(1)} %bitcast.114, bf16[1024,2048]{1,0:T(8,128)(2,1)} %param.18), kind=kOutput, calls=%fused_computation.10 | convolution fusion | flops 537133056 | bytes 4980736 | tf_op jit(solution)/shard_map/dot_general | solution.py:92
  37.2 0.0 all-reduce.2.cloned.1.call-update
  37.3 0.0 copy-done.5
  37.3 0.0 copy-done.6
  37.3 0.1 copy.46
  37.4 0.1 reshape.261
  37.5 34.4 %all-reduce.2.cloned.1.call-done = bf16[128,2048]{1,0:T(8,128)(2,1)} async-done(((bf16[128,2048]{1,0:T(8,128)(2,1)}), bf16[128,2048]{1,0:T(8,128)(2,1)}) %all-reduce.2.cloned.1.call-update) | async-done | bytes 524304 | tf_op jit(solution)/shard_map/psum | solution.py:93
  71.9 0.0 copy-done.3
  71.9 1.1 multiply_reduce_fusion.1
  73.0 0.0 copy-start.2
  73.0 0.8 copy-done.2
  73.8 0.0 copy-done.7
  73.8 0.1 multiply_convert_fusion
  73.9 4.6 %scatter_custom_fusion = bf16[768,2048]{1,0:T(8,128)(2,1)S(1)} fusion(s32[512]{0:T(512)S(1)} %reshape.261, bf16[]{:T(256)} %constant.24.clone.1, bf16[64,2048]{1,0:T(8,128)(2,1)S(1)} %multiply_convert_fusion), kind=kCustom, calls=%fused_computation.12 | custom fusion | bytes 3407874 | tf_op jit(solution)/shard_map/scatter | solution.py:113
  78.6 2.7 reshape.246
  81.3 4.8 %all-to-all-start = ((bf16[64,12,2048]{2,1,0:T(8,128)(2,1)}), bf16[64,12,2048]{2,1,0:T(8,128)(2,1)}, u32[]{:S(2)}, u32[]{:S(2)}) async-start(bf16[64,12,2048]{2,1,0:T(8,128)(2,1)} %reshape.246), calls=%async_computation | async-start | bytes 8388608 | tf_op jit(solution)/shard_map/all_to_all | solution.py:117
  86.0 53.9 %reshape.273 = bf16[8,2048,768,1]{2,1,0,3:T(8,128)(2,1)} reshape(bf16[8,2048,2,384]{3,2,1,0:T(2,128)(2,1)} %param.24) | data formatting | bytes 50331648 | tf_op jit(solution)/shard_map/reshape | solution.py:105
  140.0 40.0 %all-to-all-done = bf16[64,12,2048]{2,1,0:T(8,128)(2,1)} async-done(((bf16[64,12,2048]{2,1,0:T(8,128)(2,1)}), bf16[64,12,2048]{2,1,0:T(8,128)(2,1)}, u32[]{:S(2)}, u32[]{:S(2)}) %all-to-all-start) | async-done | bytes 3145760 | tf_op jit(solution)/shard_map/all_to_all | solution.py:117
  180.0 12.9 %fusion.9 = f32[8,8,12,768]{3,2,0,1:T(8,128)S(1)} fusion(bf16[8,2048,768,1]{2,1,0,3:T(8,128)(2,1)} %reshape.273, bf16[8,8,12,2048]{3,2,1,0:T(8,128)(2,1)} %bitcast.24), kind=kOutput, calls=%fused_computation.14 | convolution fusion | flops 2415919104 | bytes 30670848 | tf_op jit(solution)/shard_map/sxnd,xdf->sxnf/dot_general | solution.py:120
  192.9 7.1 %convert_bitcast_fusion = bf16[8,8,12,2048]{3,2,0,1:T(8,128)(2,1)S(1)} fusion(bf16[8,384,2048]{2,1,0:T(8,128)(2,1)} %param.25, f32[8,8,12,768]{3,2,0,1:T(8,128)S(1)} %fusion.9), kind=kOutput, calls=%fused_computation.8 | convolution fusion | flops 1211301888 | bytes 18087936 | tf_op jit(solution)/shard_map/sxnf,xfd->sxnd/dot_general | solution.py:122
  200.0 1.7 copy.87
  201.7 3.7 %copy.50 = bf16[64,12,2048]{2,1,0:T(8,128)(2,1)} copy(bf16[64,12,2048]{2,0,1:T(8,128)(2,1)S(1)} %bitcast.111) | data formatting | bytes 6291456 | tf_op jit(solution)/shard_map/reshape | solution.py:126
  205.4 0.0 copy-start.8
  205.4 4.7 %all-to-all-start.1 = ((bf16[64,12,2048]{2,1,0:T(8,128)(2,1)}), bf16[64,12,2048]{2,1,0:T(8,128)(2,1)}, u32[]{:S(2)}, u32[]{:S(2)}) async-start(bf16[64,12,2048]{2,1,0:T(8,128)(2,1)} %copy.50), calls=%async_computation.1 | async-start | bytes 8388608 | tf_op jit(solution)/shard_map/all_to_all | solution.py:125
  210.1 0.3 reduce-scatter.2.cloned.1.call-start
  210.4 0.1 copy.51
  210.5 0.1 reshape.253
  210.6 0.1 copy.45
  210.7 0.0 copy-done.8
  210.7 0.1 copy.44
  210.8 93.3 %all-to-all-done.1 = bf16[64,12,2048]{2,1,0:T(8,128)(2,1)} async-done(((bf16[64,12,2048]{2,1,0:T(8,128)(2,1)}), bf16[64,12,2048]{2,1,0:T(8,128)(2,1)}, u32[]{:S(2)}, u32[]{:S(2)}) %all-to-all-start.1) | async-done | bytes 3145760 | tf_op jit(solution)/shard_map/all_to_all | solution.py:125
  304.1 4.7 %reshape.250 = bf16[768,2048]{1,0:T(8,128)(2,1)S(1)} reshape(bf16[64,12,2048]{2,1,0:T(8,128)(2,1)} %all-to-all-done.1) | data formatting | bytes 6291456 | tf_op jit(solution)/shard_map/reshape | solution.py:128
  308.8 0.0 copy-start.1
  308.8 3.3 gather_fusion
  312.2 4.7 %multiply_reduce_fusion = bf16[64,2048]{1,0:T(8,128)(2,1)} fusion(bf16[512,2048]{1,0:T(8,128)(2,1)} %gather_fusion, f32[64,8]{1,0:T(8,128)S(1)} %copy.44, pred[64,8]{1,0:T(8,128)(4,1)S(1)} %copy.45), kind=kLoop, calls=%fused_computation.7 | loop fusion | flops 4063232 | bytes 2361856 | tf_op jit(solution)/shard_map/reduce_sum | solution.py:130
  316.8 0.0 reduce-scatter.2.cloned.1.call-update
  316.8 10.0 %reduce-scatter.2.cloned.1.call-done = bf16[64,1024]{1,0:T(8,128)(2,1)} async-done(((bf16[64,2048]{1,0:T(8,128)(2,1)}), bf16[64,1024]{1,0:T(8,128)(2,1)}) %reduce-scatter.2.cloned.1.call-update) | async-done | bytes 131088 | tf_op jit(solution)/shard_map/reduce_scatter | solution.py:131
  326.8 1.7 add_convert_fusion
  328.5 0.0 copy-done.1
  (8 shorter events, 0.1 us)
Async XLA Ops:
  6.5 1.2 copy-start
  6.5 25.4 %copy-start.4 = (bf16[128,1024]{1,0:T(8,128)(2,1)S(1)}, bf16[128,1024]{1,0:T(8,128)(2,1)}, u32[]{:S(2)}) copy-start(bf16[128,1024]{1,0:T(8,128)(2,1)} %param.13) | copy-start | bytes 786436
  6.5 65.3 %all-reduce.2.cloned.1.call-start = ((), (), s32[]{:S(2)}) async-start(), calls=%async_computation.3 | async-start | bytes 1048576 | tf_op jit(solution)/shard_map/psum | solution.py:93
  8.0 9.4 %collective-permute-start = (bf16[8,128,128]{2,1,0:T(8,128)(2,1)S(1)}, bf16[8,128,128]{2,1,0:T(8,128)(2,1)S(1)}, u32[]{:S(2)}, u32[]{:S(2)}) collective-permute-start(bf16[8,128,128]{2,1,0:T(8,128)(2,1)S(1)} %convolution_convert_fusion.1), channel_id=1, source_target_pairs={{0,4},{4,0},{8,12},{12,8},{1,5},{5,1},{9,13},{13,9},{2,6},{6,2},{1... | collective-permute-start | bytes 786440 | tf_op jit(solution)/shard_map/ppermute | solution.py:16
  17.5 14.1 %collective-permute-start.1 = (bf16[8,128,128]{2,1,0:T(8,128)(2,1)S(1)}, bf16[8,128,128]{2,1,0:T(8,128)(2,1)S(1)}, u32[]{:S(2)}, u32[]{:S(2)}) collective-permute-start(bf16[8,128,128]{2,1,0:T(8,128)(2,1)S(1)} %get-tuple-element.10), channel_id=1, source_target_pairs={{0,8},{4,12},{8,0},{12,4},{1,9},{5,13},{9,1},{13,5},{2,10},{6,14},... | collective-permute-start | bytes 786440 | tf_op jit(solution)/shard_map/ppermute | solution.py:16
  33.4 3.9 %copy-start.5 = (s32[64,8]{0,1:T(8,128)S(1)}, s32[64,8]{0,1:T(8,128)}, u32[]{:S(2)}) copy-start(s32[64,8]{0,1:T(8,128)} %param.22) | copy-start | bytes 6148
  33.4 3.8 %copy-start.6 = (s32[64,8]{0,1:T(8,128)S(1)}, s32[64,8]{0,1:T(8,128)}, u32[]{:S(2)}) copy-start(s32[64,8]{0,1:T(8,128)} %param.21) | copy-start | bytes 6148
  33.4 38.4 %copy-start.3 = (bf16[64,2048]{1,0:T(8,128)(2,1)S(1)}, bf16[64,2048]{1,0:T(8,128)(2,1)}, u32[]{:S(2)}) copy-start(bf16[64,2048]{1,0:T(8,128)(2,1)} %param.19) | copy-start | bytes 786436
  33.4 40.4 %copy-start.7 = (f32[2048]{0:T(1024)S(1)}, f32[2048]{0:T(1024)}, u32[]{:S(2)}) copy-start(f32[2048]{0:T(1024)} %param.20) | copy-start | bytes 24580
  73.0 0.8 copy-start.2
  81.3 98.7 %all-to-all-start = ((bf16[64,12,2048]{2,1,0:T(8,128)(2,1)}), bf16[64,12,2048]{2,1,0:T(8,128)(2,1)}, u32[]{:S(2)}, u32[]{:S(2)}) async-start(bf16[64,12,2048]{2,1,0:T(8,128)(2,1)} %reshape.246), calls=%async_computation | async-start | bytes 8388608 | tf_op jit(solution)/shard_map/all_to_all | solution.py:117
  205.4 5.3 %copy-start.8 = (f32[64,8]{0,1:T(8,128)S(1)}, f32[64,8]{0,1:T(8,128)}, u32[]{:S(2)}) copy-start(f32[64,8]{0,1:T(8,128)} %param.23) | copy-start | bytes 6148
  205.4 98.7 %all-to-all-start.1 = ((bf16[64,12,2048]{2,1,0:T(8,128)(2,1)}), bf16[64,12,2048]{2,1,0:T(8,128)(2,1)}, u32[]{:S(2)}, u32[]{:S(2)}) async-start(bf16[64,12,2048]{2,1,0:T(8,128)(2,1)} %copy.50), calls=%async_computation.1 | async-start | bytes 8388608 | tf_op jit(solution)/shard_map/all_to_all | solution.py:125
  210.1 116.7 %reduce-scatter.2.cloned.1.call-start = ((), (), s32[]{:S(2)}) async-start(), calls=%async_computation.4 | async-start | bytes 393216 | tf_op jit(solution)/shard_map/reduce_scatter | solution.py:131
  308.8 19.7 %copy-start.1 = (bf16[128,1024]{1,0:T(8,128)(2,1)S(1)}, bf16[128,1024]{1,0:T(8,128)(2,1)}, u32[]{:S(2)}) copy-start(bf16[128,1024]{1,0:T(8,128)(2,1)} %param.15) | copy-start | bytes 786436
Sparse Core Ops, SparseCore 0:
  37.4 34.4 all-reduce.1
  316.9 9.7 reduce-scatter.1
where the time goes:
time: 337 us; the launch traced here: 335 us
  waiting for transfers between devices  193 us (57%)
  local copies, waits for them, and re-layouts  78.3 us (23%)
  matrix products  26.6 us (8%)
  starting transfers between devices  15.6 us (5%)
  between operations  13.7 us (4%)
  other arithmetic  8.13 us (2%)
    all_to_all x1, waiting for transfers between devices, on_device(): lax.all_to_all(result.reshape(arrived.shape), ('seq', 'sub'), split_axis=...  93.3 us
    reshape x1, local copies, waits for them, and re-layouts, on_device(): pair_weight = w_gate_up.reshape(exp_here, D, 2 * hid_part)  53.9 us
    all_to_all x1, waiting for transfers between devices, on_device(): lax.all_to_all(outgoing, ('seq', 'sub'), split_axis=0, concat_axis=0, til...  40 us
    psum x1, waiting for transfers between devices, on_device(): lax.psum(partial_value.astype(jnp.bfloat16), ('head', 'sub'))  34.4 us
    ppermute x2, waiting for transfers between devices, swapped(): return lax.ppermute(value, axis, pairs)  15.3 us
    dot_general x1, matrix products, on_device(): jnp.einsum('sxnd,xdf->sxnf', grouped, pair_weight, preferred_element_type...  12.9 us
    reduce_scatter x1, waiting for transfers between devices, on_device(): lax.psum_scatter(combined.astype(jnp.bfloat16), 'head', scatter_dimension...  9.96 us
    dot_general x1, matrix products, on_device(): jnp.einsum('sxnf,xfd->sxnd', active, w_down, preferred_element_type=jnp.f...  7.07 us
  transfers between devices with their start and end apart: 6, of which 6 were waited for; matrix products, arithmetic and copies ran while one was open for 17% of the time, Pallas kernels for 0%

commit v1 on v0

--- a/solution.py
+++ b/solution.py
@@ -1,6 +1,8 @@
 import jax
 import jax.numpy as jnp
 from jax import lax
+from jax.experimental import pallas as pl
+from jax.experimental.pallas import tpu as pltpu
 from jax.sharding import PartitionSpec as P
 
 D = 2048
@@ -14,6 +16,39 @@
     mask = 2**distance
     pairs = [(source, source ^ mask) for source in range(lax.axis_size(axis))]
     return lax.ppermute(value, axis, pairs)
+
+
+def moved(value, axis, distance):
+    size = lax.axis_size(axis)
+    pairs = [(source, (source + distance) % size) for source in range(size)]
+    return lax.ppermute(value, axis, pairs)
+
+
+def expert_kernel(rows_ref, gate_up_ref, down_ref, scale_ref, out_ref):
+    pair = jnp.swapaxes(gate_up_ref[0], 0, 1)
+    rows = rows_ref[0]
+    gate = jnp.dot(rows, pair[0], preferred_element_type=jnp.float32)
+    up = jnp.dot(rows, pair[1], preferred_element_type=jnp.float32)
+    active = (gate / (1.0 + jnp.exp(-gate)) * up).astype(jnp.bfloat16)
+    piece = jnp.dot(active, down_ref[0], preferred_element_type=jnp.float32)
+    out_ref[0] = (piece * scale_ref[0]).astype(jnp.bfloat16)
+
+
+def run_experts(rows, w_gate_up, w_down, scale):
+    experts, count, width = rows.shape
+    hidden = w_down.shape[1]
+    return pl.pallas_call(
+        expert_kernel,
+        grid=(experts,),
+        in_specs=[
+            pl.BlockSpec((1, count, width), lambda e: (e, 0, 0)),
+            pl.BlockSpec((1, width, 2, hidden), lambda e: (e, 0, 0, 0)),
+            pl.BlockSpec((1, hidden, width), lambda e: (e, 0, 0)),
+            pl.BlockSpec((1, count, 1), lambda e: (e, 0, 0)),
+        ],
+        out_specs=pl.BlockSpec((1, count, width), lambda e: (e, 0, 0)),
+        out_shape=jax.ShapeDtypeStruct(rows.shape, jnp.bfloat16),
+    )(rows, w_gate_up, w_down, scale)
 
 
 def bit_length(numbers, digits):
@@ -38,6 +73,16 @@
     w_gate_up,
     w_down,
 ):
+    bf16, f32 = jnp.bfloat16, jnp.float32
+    n_seq, n_head, n_sub = (lax.axis_size(name) for name in ("seq", "head", "sub"))
+    my_seq, my_head, my_sub = (lax.axis_index(name) for name in ("seq", "head", "sub"))
+    my_tokens = residual.shape[0]
+    route = jnp.concatenate(
+        [expert_ids.astype(f32), expert_slots.astype(f32), route_weight], axis=1
+    ).T
+    routes = [route] + [moved(route, "seq", hop) for hop in range(1, n_seq)]
+    routes = jnp.concatenate(routes, axis=1)
+    routes = jnp.concatenate([routes] + [moved(routes, "sub", hop) for hop in range(1, n_sub)], axis=1)
     block_len = queries.shape[0]
     heads_here = queries.shape[1] // HEAD_DIM
     inv_root = HEAD_DIM ** (-0.5)
@@ -89,49 +134,79 @@
         .astype(jnp.bfloat16)
         .reshape(block_len, heads_here * HEAD_DIM)
     )
-    partial_value = jnp.dot(attended, out_weight, preferred_element_type=jnp.float32)
-    summed = lax.psum(partial_value.astype(jnp.bfloat16), ("head", "sub")).astype(jnp.float32)
-    my_tokens = residual.shape[0]
-    my_rows = lax.dynamic_slice_in_dim(summed, lax.axis_index("sub") * my_tokens, my_tokens, 0)
-    stream = residual.astype(jnp.float32) + my_rows
+    capacity = 3 * (my_tokens * TOPK // EXPERTS) // 2
+    exp_here = w_gate_up.shape[0]
+    named, slots, weights = jnp.split(routes, 3, axis=0)
+    all_tokens = named.shape[1]
+    blocks = all_tokens // my_tokens
+    first = (my_seq * n_sub + my_sub) * exp_here
+    local = (first + jnp.arange(exp_here, dtype=jnp.int32)).astype(f32)
+    match = (named[None] == local[:, None, None]) & (slots >= 0)[None]
+    block_of = (jnp.arange(all_tokens, dtype=jnp.int32) // my_tokens * capacity).astype(f32)
+    place = jnp.sum(jnp.where(match, slots[None] + block_of + 1.0, 0.0), axis=1) - 1.0
+    share = jnp.sum(jnp.where(match, weights[None], 0.0), axis=1)
+    row = jnp.arange(blocks * capacity, dtype=jnp.int32).astype(f32)
+    chosen = place[:, None, :] == row[None, :, None]
+    scale = jnp.sum(jnp.where(chosen, share[:, None, :], 0.0), axis=2, keepdims=True)
+    pick = chosen.astype(bf16).reshape(exp_here * blocks * capacity, all_tokens)
+
+    partial_value = jnp.dot(attended, out_weight, preferred_element_type=f32)
+    by_sub = partial_value.reshape(n_sub, my_tokens, D)
+    my_rows = lax.dynamic_index_in_dim(by_sub, my_sub, 0, keepdims=False)
+    for hop in range(1, n_sub):
+        outgoing = lax.dynamic_index_in_dim(by_sub, (my_sub + hop) % n_sub, 0, keepdims=False)
+        my_rows = my_rows + moved(outgoing.astype(bf16), "sub", hop).astype(f32)
+    shared = my_rows.astype(bf16)
+    total = shared.astype(f32)
+    for hop in range(1, n_head):
+        total = total + moved(shared, "head", hop).astype(f32)
+    stream = residual.astype(f32) + total
     mean_square = jnp.mean(stream * stream, axis=-1, keepdims=True)
-    normed = (stream * lax.rsqrt(mean_square + 1e-06) * norm_gain).astype(jnp.bfloat16)
-    capacity = 3 * (my_tokens * TOPK // EXPERTS) // 2
-    slot_index = jnp.where(
-        expert_slots >= 0, expert_ids * capacity + expert_slots, EXPERTS * capacity
-    )
-    exp_here = w_gate_up.shape[0]
-    hid_part = w_down.shape[1]
-    pair_weight = w_gate_up.reshape(exp_here, D, 2 * hid_part)
-    kept_weight = jnp.where(expert_slots >= 0, route_weight, 0.0)
-    head_count = lax.axis_size("head")
-    width_part = D // head_count
-    residual_part = lax.dynamic_slice_in_dim(
-        stream, lax.axis_index("head") * width_part, width_part, 1
-    )
-    outgoing = jnp.zeros((EXPERTS * capacity, D), jnp.bfloat16)
-    outgoing = outgoing.at[slot_index].set(
-        jnp.broadcast_to(normed[:, None, :], (my_tokens, TOPK, D)), mode="drop"
-    )
-    outgoing = outgoing.reshape(EXPERTS, capacity, D)
-    arrived = lax.all_to_all(outgoing, ("seq", "sub"), split_axis=0, concat_axis=0, tiled=True)
-    sources = arrived.shape[0] // exp_here
-    grouped = arrived.reshape(sources, exp_here, arrived.shape[1], D)
-    gate_up = jnp.einsum("sxnd,xdf->sxnf", grouped, pair_weight, preferred_element_type=jnp.float32)
-    active = (jax.nn.silu(gate_up[..., :hid_part]) * gate_up[..., hid_part:]).astype(jnp.bfloat16)
-    result = jnp.einsum(
-        "sxnf,xfd->sxnd", active, w_down, preferred_element_type=jnp.float32
-    ).astype(jnp.bfloat16)
-    returned = lax.all_to_all(
-        result.reshape(arrived.shape), ("seq", "sub"), split_axis=0, concat_axis=0, tiled=True
-    )
-    returned = returned.reshape(EXPERTS * capacity, D)
-    picked = jnp.take(returned, jnp.minimum(slot_index, EXPERTS * capacity - 1), axis=0)
-    combined = jnp.sum(kept_weight[:, :, None] * picked, axis=1)
-    expert_sum = lax.psum_scatter(
-        combined.astype(jnp.bfloat16), "head", scatter_dimension=1, tiled=True
-    ).astype(jnp.float32)
-    return (residual_part + expert_sum).astype(jnp.bfloat16)
+    normed = (stream * lax.rsqrt(mean_square + 1e-06) * norm_gain).astype(bf16)
+
+    width = D // n_head
+    mine = lax.dynamic_slice_in_dim(normed, my_head * width, width, 1)
+    gathered = [normed]
+    step = max(1, n_seq // 4)
+    for begin in range(1, n_seq, step):
+        hops = range(begin, min(begin + step, n_seq))
+        part = jnp.concatenate([moved(mine, "seq", hop) for hop in hops], axis=0)
+        whole = jnp.zeros((n_head, part.shape[0], width), bf16)
+        parts = [part] + [moved(part, "head", side) for side in range(1, n_head)]
+        for side, piece in enumerate(parts):
+            whole = lax.dynamic_update_index_in_dim(whole, piece, (my_head - side) % n_head, 0)
+        gathered.append(jnp.transpose(whole, (1, 0, 2)).reshape(-1, D))
+    here = jnp.concatenate(gathered, axis=0)
+    picks = jnp.split(pick, n_sub, axis=1)
+    rows = jnp.dot(picks[0], here, preferred_element_type=f32)
+    for hop in range(1, n_sub):
+        rows = rows + jnp.dot(picks[hop], moved(here, "sub", hop), preferred_element_type=f32)
+    rows = rows.astype(bf16).reshape(exp_here, blocks * capacity, D)
+    pieces = run_experts(rows, w_gate_up, w_down, scale).reshape(-1, D)
+
+    def combined(part):
+        return lax.dot_general(part, pieces, (((0,), (0,)), ((), ())), preferred_element_type=f32)
+
+    sent = [moved(combined(picks[hop]).astype(bf16), "sub", -hop) for hop in range(1, n_sub)]
+    merged = combined(picks[0])
+    for value in sent:
+        merged = merged + value.astype(f32)
+    by_head = merged.reshape(n_seq, my_tokens, n_head, width)
+    expert_sum = 0.0
+    for begin in range(0, n_seq, step):
+        hops = range(begin, min(begin + step, n_seq))
+        group = by_head[begin : hops[-1] + 1]
+        own = lax.dynamic_index_in_dim(group, my_head, 2, keepdims=False)
+        for side in range(1, n_head):
+            away = lax.dynamic_index_in_dim(group, (my_head + side) % n_head, 2, keepdims=False)
+            own = own + moved(away.astype(bf16), "head", side).astype(f32)
+        for place_in, hop in enumerate(hops):
+            value = own[place_in]
+            if hop:
+                value = moved(value.astype(bf16), "seq", -hop).astype(f32)
+            expert_sum = expert_sum + value
+    stream_part = lax.dynamic_slice_in_dim(stream, my_head * width, width, 1)
+    return (stream_part + expert_sum).astype(bf16)
 
 
 def solution(mesh):

time: 337 us -> 134 us (0.40)
  waiting for transfers between devices: 193 us -> 37.1 us
  local copies, waits for them, and re-layouts: 78.3 us -> 20.9 us
  Pallas kernels: 0 us -> 21 us
  starting transfers between devices: 15.6 us -> 30.1 us
  between operations: 13.7 us -> 0.75 us
  matrix products: 26.6 us -> 16 us
    all_to_all x2 -> x0, waiting for transfers between devices: 133 us -> none  [the longest x1 93.3 us: on_device(): lax.all_to_all(result.reshape(arrived.shape), ('seq', 'sub'), split_axis=...]
    reshape x4 -> x0, local copies, waits for them, and re-layouts: 65.1 us -> none  [the longest x1 53.9 us: on_device(): pair_weight = w_gate_up.reshape(exp_here, D, 2 * hid_part)]
    psum x1 -> x0, waiting for transfers between devices: 34.4 us -> none  [on_device(): lax.psum(partial_value.astype(jnp.bfloat16), ('head', 'sub'))]
    ppermute x0 -> x21, starting transfers between devices: none -> 24.2 us  [moved(): return lax.ppermute(value, axis, pairs)]
    pallas_call x0 -> x1, Pallas kernels: none -> 21 us  [run_experts(): pl.pallas_call(expert_kernel, grid=(experts,), in_specs=[pl.BlockSpec((1,...]
    ppermute x0 -> x21, waiting for transfers between devices: none -> 20.9 us  [moved(): return lax.ppermute(value, axis, pairs)]
    dynamic_update_slice x0 -> x6, local copies, waits for them, and re-layouts: none -> 10.7 us  [on_device(): lax.dynamic_update_index_in_dim(whole, piece, (my_head - side) % n_head, 0)]
    dot_general x3 -> x5, matrix products: 23.7 us -> 13.2 us  [the longest x2 6.58 us: combined(): lax.dot_general(part, pieces, (((0,), (0,)), ((), ())), preferred_element...]
  transfers between devices with their start and end apart: 6 -> 23, of which waited for: 6 -> 9; matrix products, arithmetic and copies ran while one was open for 17% -> 17% of each run, Pallas kernels for 0% -> 0%
where the time goes in v1:
time: 134 us; the launch traced here: 133 us
  waiting for transfers between devices  37.1 us (28%)
  starting transfers between devices  30.1 us (22%)
  Pallas kernels  21 us (16%)
  local copies, waits for them, and re-layouts  20.9 us (16%)
  matrix products  16 us (12%)
  other arithmetic  7.72 us (6%)
    ppermute x21, starting transfers between devices, moved(): return lax.ppermute(value, axis, pairs)  24.2 us
    pallas_call x1, Pallas kernels, run_experts(): pl.pallas_call(expert_kernel, grid=(experts,), in_specs=[pl.BlockSpec((1,...  21 us
    ppermute x21, waiting for transfers between devices, moved(): return lax.ppermute(value, axis, pairs)  20.9 us
    ppermute x2, waiting for transfers between devices, swapped(): return lax.ppermute(value, axis, pairs)  16.2 us
    dynamic_update_slice x6, local copies, waits for them, and re-layouts, on_device(): lax.dynamic_update_index_in_dim(whole, piece, (my_head - side) % n_head, 0)  10.7 us
    dot_general x2, matrix products, combined(): lax.dot_general(part, pieces, (((0,), (0,)), ((), ())), preferred_element...  6.58 us
    ppermute x2, starting transfers between devices, swapped(): return lax.ppermute(value, axis, pairs)  5.93 us
    dot_general x1, matrix products, on_device(): partial_value = jnp.dot(attended, out_weight, preferred_element_type=f32)  2.94 us
  transfers between devices with their start and end apart: 23, of which 9 were waited for; matrix products, arithmetic and copies ran while one was open for 17% of the time, Pallas kernels for 0%

profile of v1, /device:TPU:0, one launch (start us, length us, event | category | flops | bytes accessed | tf_op | source)
XLA Modules:
  0.0 133.5 jit_solution(6653834715488884364)
XLA Ops:
  0.0 1.2 copy.99
  1.4 3.1 %collective-permute-start = (bf16[8,128,128]{2,1,0:T(8,128)(2,1)S(1)}, bf16[8,128,128]{2,1,0:T(8,128)(2,1)S(1)}, u32[]{:S(2)}, u32[]{:S(2)}) collective-permute-start(bf16[8,128,128]{2,1,0:T(8,128)(2,1)S(1)} %convolution_convert_fusion.1), channel_id=1, source_target_pairs={{0,4},{4,0},{8,12},{12,8},{1,5},{5,1},{9,13},{13,9},{2,6},{6,2},{1... | collective-permute-start | bytes 786440 | tf_op jit(solution)/shard_map/ppermute | solution.py:18
  4.8 0.9 fusion.66
  5.7 5.2 %collective-permute-done = bf16[8,128,128]{2,1,0:T(8,128)(2,1)S(1)} collective-permute-done((bf16[8,128,128]{2,1,0:T(8,128)(2,1)S(1)}, bf16[8,128,128]{2,1,0:T(8,128)(2,1)S(1)}, u32[]{:S(2)}, u32[]{:S(2)}) %collective-permute-start) | collective-permute-done | bytes 262176 | tf_op jit(solution)/shard_map/ppermute | solution.py:18
  11.0 2.8 %collective-permute-start.1 = (bf16[8,128,128]{2,1,0:T(8,128)(2,1)S(1)}, bf16[8,128,128]{2,1,0:T(8,128)(2,1)S(1)}, u32[]{:S(2)}, u32[]{:S(2)}) collective-permute-start(bf16[8,128,128]{2,1,0:T(8,128)(2,1)S(1)} %get-tuple-element.14), channel_id=1, source_target_pairs={{0,8},{4,12},{8,0},{12,4},{1,9},{5,13},{9,1},{13,5},{2,10},{6,14},... | collective-permute-start | bytes 786440 | tf_op jit(solution)/shard_map/ppermute | solution.py:18
  14.0 11.0 %collective-permute-done.1 = bf16[8,128,128]{2,1,0:T(8,128)(2,1)S(1)} collective-permute-done((bf16[8,128,128]{2,1,0:T(8,128)(2,1)S(1)}, bf16[8,128,128]{2,1,0:T(8,128)(2,1)S(1)}, u32[]{:S(2)}, u32[]{:S(2)}) %collective-permute-start.1) | collective-permute-done | bytes 262176 | tf_op jit(solution)/shard_map/ppermute | solution.py:18
  25.1 0.4 fusion.3
  25.6 1.3 fusion.6
  27.3 2.9 %fusion = f32[2,64,2048]{2,1,0:T(8,128)S(1)} fusion(bf16[2,64,1024]{2,1,0:T(8,128)(2,1)S(1)} %dot_general.37, bf16[1024,2048]{1,0:T(8,128)(2,1)} %param.18), kind=kOutput, calls=%fused_computation.1 | convolution fusion | flops 536870912 | bytes 5505024 | tf_op jit(solution)/shard_map/dot_general | solution.py:153
  30.5 1.5 %collective-permute-done.2 = bf16[64,2048]{1,0:T(8,128)(2,1)S(1)} collective-permute-done((bf16[64,2048]{1,0:T(8,128)(2,1)S(1)}, bf16[64,2048]{1,0:T(8,128)(2,1)S(1)}, u32[]{:S(2)}, u32[]{:S(2)}) %collective-permute-start.2) | collective-permute-done | bytes 262176 | tf_op jit(solution)/shard_map/ppermute | solution.py:24
  32.0 1.4 %collective-permute-start.3 = (bf16[64,2048]{1,0:T(8,128)(2,1)S(1)}, bf16[64,2048]{1,0:T(8,128)(2,1)S(1)}, u32[]{:S(2)}, u32[]{:S(2)}) collective-permute-start(bf16[64,2048]{1,0:T(8,128)(2,1)S(1)} %fusion.18), channel_id=1, source_target_pairs={{0,2},{2,0},{1,3},{3,1},{4,6},{6,4},{5,7},{7,5},{8,10},{10,8},{9,1... | collective-permute-start | bytes 786440 | tf_op jit(solution)/shard_map/ppermute | solution.py:24
  33.4 0.7 collective-permute-start.4
  34.2 3.4 %collective-permute-start.5 = (f32[24,64]{1,0:T(8,128)S(1)}, f32[24,64]{1,0:T(8,128)S(1)}, u32[]{:S(2)}, u32[]{:S(2)}) collective-permute-start(f32[24,64]{1,0:T(8,128)S(1)} %maximum_bitcast_fusion), channel_id=1, source_target_pairs={{0,8},{4,12},{8,0},{12,4},{1,9},{5,13},{9,1},{13,5},{2,10},{6,14},... | collective-permute-start | bytes 18440 | tf_op jit(solution)/shard_map/ppermute | solution.py:24
  37.5 2.8 %collective-permute-done.3 = bf16[64,2048]{1,0:T(8,128)(2,1)S(1)} collective-permute-done((bf16[64,2048]{1,0:T(8,128)(2,1)S(1)}, bf16[64,2048]{1,0:T(8,128)(2,1)S(1)}, u32[]{:S(2)}, u32[]{:S(2)}) %collective-permute-start.3) | collective-permute-done | bytes 262176 | tf_op jit(solution)/shard_map/ppermute | solution.py:24
  40.6 0.8 copy-done.3
  41.6 0.6 collective-permute-start.8
  42.2 3.4 %collective-permute-start.10 = (bf16[64,1024]{1,0:T(8,128)(2,1)S(1)}, bf16[64,1024]{1,0:T(8,128)(2,1)S(1)}, u32[]{:S(2)}, u32[]{:S(2)}) collective-permute-start(bf16[64,1024]{1,0:T(8,128)(2,1)S(1)} %constant_dynamic-slice_fusion.8), channel_id=1, source_target_pairs={{0,8},{4,12},{8,0},{12,4},{1,9},{5,13},{9,1},{13,5},{2,10},{6,14},... | collective-permute-start | bytes 393224 | tf_op jit(solution)/shard_map/ppermute | solution.py:24
  45.7 0.5 add_convert_fusion.1
  46.2 0.7 eq.155
  47.0 3.0 %collective-permute-done.8 = bf16[64,1024]{1,0:T(8,128)(2,1)S(1)} collective-permute-done((bf16[64,1024]{1,0:T(8,128)(2,1)S(1)}, bf16[64,1024]{1,0:T(8,128)(2,1)S(1)}, u32[]{:S(2)}, u32[]{:S(2)}) %collective-permute-start.8) | collective-permute-done | bytes 131104 | tf_op jit(solution)/shard_map/ppermute | solution.py:24
  49.9 1.4 %collective-permute-start.9 = (bf16[64,1024]{1,0:T(8,128)(2,1)S(1)}, bf16[64,1024]{1,0:T(8,128)(2,1)S(1)}, u32[]{:S(2)}, u32[]{:S(2)}) collective-permute-start(bf16[64,1024]{1,0:T(8,128)(2,1)S(1)} %collective-permute-done.8), channel_id=1, source_target_pairs={{0,2},{2,0},{1,3},{3,1},{4,6},{6,4},{5,7},{7,5},{8,10},{10,8},{9,1... | collective-permute-start | bytes 393224 | tf_op jit(solution)/shard_map/ppermute | solution.py:24
  51.3 2.5 %collective-permute-done.10 = bf16[64,1024]{1,0:T(8,128)(2,1)S(1)} collective-permute-done((bf16[64,1024]{1,0:T(8,128)(2,1)S(1)}, bf16[64,1024]{1,0:T(8,128)(2,1)S(1)}, u32[]{:S(2)}, u32[]{:S(2)}) %collective-permute-start.10) | collective-permute-done | bytes 131104 | tf_op jit(solution)/shard_map/ppermute | solution.py:24
  53.8 1.4 %collective-permute-start.11 = (bf16[64,1024]{1,0:T(8,128)(2,1)S(1)}, bf16[64,1024]{1,0:T(8,128)(2,1)S(1)}, u32[]{:S(2)}, u32[]{:S(2)}) collective-permute-start(bf16[64,1024]{1,0:T(8,128)(2,1)S(1)} %collective-permute-done.10), channel_id=1, source_target_pairs={{0,2},{2,0},{1,3},{3,1},{4,6},{6,4},{5,7},{7,5},{8,10},{10,8},{9,1... | collective-permute-start | bytes 393224 | tf_op jit(solution)/shard_map/ppermute | solution.py:24
  55.2 0.7 collective-permute-start.13
  55.9 0.6 add_add_fusion.1
  57.3 1.8 %dynamic_update_slice.19 = bf16[2,64,1024]{2,0,1:T(2,128)(2,1)S(1)} dynamic-update-slice(bf16[2,64,1024]{2,0,1:T(2,128)(2,1)S(1)} %broadcast.412.clone.2, bf16[1,64,1024]{2,0,1:T(2,128)(2,1)S(1)} %copy.75, s32[]{:T(128)S(6)} %select_n.128, s32[]{:T(128)} %constant.138.clone.1, s32[]{:T(128)} %constant.138.clone.1) | dynamic-update-slice | bytes 262148 | tf_op jit(solution)/shard_map/jit(dynamic_update_index_in_dim)/dynamic_update_slice | solution.py:177
  59.2 1.8 %dynamic_update_slice.21 = bf16[2,64,1024]{2,0,1:T(2,128)(2,1)S(1)} dynamic-update-slice(bf16[2,64,1024]{2,0,1:T(2,128)(2,1)S(1)} %broadcast.412.clone.1, bf16[1,64,1024]{2,0,1:T(2,128)(2,1)S(1)} %copy.77, s32[]{:T(128)S(6)} %select_n.128, s32[]{:T(128)} %constant.138.clone.1, s32[]{:T(128)} %constant.138.clone.1) | dynamic-update-slice | bytes 262148 | tf_op jit(solution)/shard_map/jit(dynamic_update_index_in_dim)/dynamic_update_slice | solution.py:177
  61.1 1.8 %dynamic_update_slice.23 = bf16[2,64,1024]{2,0,1:T(2,128)(2,1)S(1)} dynamic-update-slice(bf16[2,64,1024]{2,0,1:T(2,128)(2,1)S(1)} %broadcast.412.clone, bf16[1,64,1024]{2,0,1:T(2,128)(2,1)S(1)} %copy.79, s32[]{:T(128)S(6)} %select_n.128, s32[]{:T(128)} %constant.138.clone.1, s32[]{:T(128)} %constant.138.clone.1) | dynamic-update-slice | bytes 262148 | tf_op jit(solution)/shard_map/jit(dynamic_update_index_in_dim)/dynamic_update_slice | solution.py:177
  63.2 1.8 %dynamic_update_slice.20 = bf16[2,64,1024]{2,0,1:T(2,128)(2,1)S(1)} dynamic-update-slice(bf16[2,64,1024]{2,0,1:T(2,128)(2,1)S(1)} %dynamic_update_slice.19, bf16[1,64,1024]{2,0,1:T(2,128)(2,1)S(1)} %copy.76, s32[]{:T(128)S(6)} %select_n.130, s32[]{:T(128)} %constant.138.clone.1, s32[]{:T(128)} %constant.138.clone.1) | dynamic-update-slice | bytes 262148 | tf_op jit(solution)/shard_map/jit(dynamic_update_index_in_dim)/dynamic_update_slice | solution.py:177
  65.2 1.8 %dynamic_update_slice.22 = bf16[2,64,1024]{2,0,1:T(2,128)(2,1)S(1)} dynamic-update-slice(bf16[2,64,1024]{2,0,1:T(2,128)(2,1)S(1)} %dynamic_update_slice.21, bf16[1,64,1024]{2,0,1:T(2,128)(2,1)S(1)} %copy.78, s32[]{:T(128)S(6)} %select_n.130, s32[]{:T(128)} %constant.138.clone.1, s32[]{:T(128)} %constant.138.clone.1) | dynamic-update-slice | bytes 262148 | tf_op jit(solution)/shard_map/jit(dynamic_update_index_in_dim)/dynamic_update_slice | solution.py:177
  67.4 1.8 %dynamic_update_slice.24 = bf16[2,64,1024]{2,0,1:T(2,128)(2,1)S(1)} dynamic-update-slice(bf16[2,64,1024]{2,0,1:T(2,128)(2,1)S(1)} %dynamic_update_slice.23, bf16[1,64,1024]{2,0,1:T(2,128)(2,1)S(1)} %copy.80, s32[]{:T(128)S(6)} %select_n.130, s32[]{:T(128)} %constant.138.clone.1, s32[]{:T(128)} %constant.138.clone.1) | dynamic-update-slice | bytes 262148 | tf_op jit(solution)/shard_map/jit(dynamic_update_index_in_dim)/dynamic_update_slice | solution.py:177
  69.4 0.7 slice_compare_fusion
  70.3 1.0 bitcast_compare_fusion
  71.3 0.9 select_reduce_fusion
  72.2 0.9 copy.81.scale_ref
  73.1 1.0 fusion.12
  74.1 2.7 %add_convert_fusion = bf16[768,2048]{1,0:T(8,128)(2,1)} fusion(f32[768,2048]{1,0:T(8,128)S(1)} %fusion.12, bf16[256,2048]{1,0:T(8,128)(2,1)S(1)} %collective-permute-done.14, pred[768,512]{1,0:T(32,128)(4,1)S(1)} %bitcast_compare_fusion), kind=kOutput, calls=%fused_computation | convolution fusion | flops 808452096 | bytes 10682368 | tf_op jit(solution)/shard_map/dot_general | solution.py:183
  76.8 21.0 %shard_map.127 = bf16[8,96,2048]{2,1,0:T(8,128)(2,1)} custom-call(bf16[8,96,2048]{2,1,0:T(8,128)(2,1)} %bitcast.180, bf16[8,2048,2,384]{3,2,1,0:T(2,128)(2,1)} %gate_up_ref.1, bf16[8,384,2048]{2,1,0:T(8,128)(2,1)} %down_ref.1, f32[8,96,1]{2,1,0:T(8,128)} %copy.81.scale_ref), custom_call_target="tpu_custom_call" | custom-call | tf_op jit(solution)/shard_map/pallas_call | solution.py:40
  97.8 4.2 %convolution_convert_fusion = bf16[256,2048]{1,0:T(8,128)(2,1)} fusion(bf16[768,2048]{1,0:T(8,128)(2,1)} %bitcast.178, pred[768,512]{1,0:T(32,128)(4,1)} %copy-done.5), kind=kOutput, calls=%fused_computation.3 | convolution fusion | flops 805830656 | bytes 4390912 | tf_op jit(solution)/shard_map/dot_general | solution.py:188
  102.0 0.5 collective-permute-start.15
  102.5 2.6 %collective-permute-done.15 = bf16[256,2048]{1,0:T(8,128)(2,1)} collective-permute-done((bf16[256,2048]{1,0:T(8,128)(2,1)}, bf16[256,2048]{1,0:T(8,128)(2,1)}, u32[]{:S(2)}, u32[]{:S(2)}) %collective-permute-start.15) | collective-permute-done | bytes 1048608 | tf_op jit(solution)/shard_map/ppermute | solution.py:24
  105.1 2.4 %convert_add_fusion = f32[256,2048]{1,0:T(8,128)S(1)} fusion(bf16[256,2048]{1,0:T(8,128)(2,1)} %collective-permute-done.15, bf16[768,2048]{1,0:T(8,128)(2,1)S(1)} %bitcast.179, pred[768,512]{1,0:T(32,128)(4,1)} %copy-done.5), kind=kOutput, calls=%fused_computation.4 | convolution fusion | flops 806354944 | bytes 6488064 | tf_op jit(solution)/shard_map/dot_general | solution.py:188
  107.7 0.4 slice.63
  108.2 0.2 constant_dynamic-slice_fusion.4
  108.4 0.2 constant_dynamic-slice_fusion.5
  108.7 0.4 slice.65
  109.1 0.2 constant_dynamic-slice_fusion.2
  109.4 0.2 constant_dynamic-slice_fusion.3
  109.7 1.4 %collective-permute-start.17 = (bf16[1,64,1024]{2,1,0:T(8,128)(2,1)S(1)}, bf16[1,64,1024]{2,1,0:T(8,128)(2,1)}, u32[]{:S(2)}, u32[]{:S(2)}) collective-permute-start(bf16[1,64,1024]{2,1,0:T(8,128)(2,1)S(1)} %bitcast.203), channel_id=1, source_target_pairs={{0,2},{2,0},{1,3},{3,1},{4,6},{6,4},{5,7},{7,5},{8,10},{10,8},{9,1... | collective-permute-start | bytes 393224 | tf_op jit(solution)/shard_map/ppermute | solution.py:24
  111.2 0.7 collective-permute-start.19
  111.9 0.4 slice.67
  112.3 0.2 constant_dynamic-slice_fusion
  112.6 1.4 %collective-permute-start.21 = (bf16[1,64,1024]{2,1,0:T(8,128)(2,1)S(1)}, bf16[1,64,1024]{2,1,0:T(8,128)(2,1)S(1)}, u32[]{:S(2)}, u32[]{:S(2)}) collective-permute-start(bf16[1,64,1024]{2,1,0:T(8,128)(2,1)S(1)} %bitcast.201), channel_id=1, source_target_pairs={{0,2},{2,0},{1,3},{3,1},{4,6},{6,4},{5,7},{7,5},{8,10},{10,8},{9,1... | collective-permute-start | bytes 393224 | tf_op jit(solution)/shard_map/ppermute | solution.py:24
  114.1 0.4 slice.61
  114.5 0.2 constant_dynamic-slice_fusion.6
  114.8 0.7 collective-permute-start.16
  115.8 0.4 collective-permute-done.17
  116.2 1.0 fusion.67
  117.2 2.7 %collective-permute-start.18 = (bf16[64,1024]{1,0:T(8,128)(2,1)S(1)}, bf16[64,1024]{1,0:T(8,128)(2,1)S(1)}, u32[]{:S(2)}, u32[]{:S(2)}) collective-permute-start(bf16[64,1024]{1,0:T(8,128)(2,1)S(1)} %fusion.67), channel_id=1, source_target_pairs={{0,12},{4,0},{8,4},{12,8},{1,13},{5,1},{9,5},{13,9},{2,14},{6,2},{... | collective-permute-start | bytes 393224 | tf_op jit(solution)/shard_map/ppermute | solution.py:24
  119.8 1.0 fusion.68
  120.8 1.6 %collective-permute-start.20 = (bf16[64,1024]{1,0:T(8,128)(2,1)S(1)}, bf16[64,1024]{1,0:T(8,128)(2,1)S(1)}, u32[]{:S(2)}, u32[]{:S(2)}) collective-permute-start(bf16[64,1024]{1,0:T(8,128)(2,1)S(1)} %fusion.68), channel_id=1, source_target_pairs={{0,8},{4,12},{8,0},{12,4},{1,9},{5,13},{9,1},{13,5},{2,10},{6,14},... | collective-permute-start | bytes 393224 | tf_op jit(solution)/shard_map/ppermute | solution.py:24
  122.4 2.1 %collective-permute-start.22 = (bf16[64,1024]{1,0:T(8,128)(2,1)S(1)}, bf16[64,1024]{1,0:T(8,128)(2,1)S(1)}, u32[]{:S(2)}, u32[]{:S(2)}) collective-permute-start(bf16[64,1024]{1,0:T(8,128)(2,1)S(1)} %fusion.69), channel_id=1, source_target_pairs={{0,4},{4,8},{8,12},{12,0},{1,5},{5,9},{9,13},{13,1},{2,6},{6,10},{... | collective-permute-start | bytes 393224 | tf_op jit(solution)/shard_map/ppermute | solution.py:24
  124.7 8.0 %collective-permute-done.20 = bf16[64,1024]{1,0:T(8,128)(2,1)S(1)} collective-permute-done((bf16[64,1024]{1,0:T(8,128)(2,1)S(1)}, bf16[64,1024]{1,0:T(8,128)(2,1)S(1)}, u32[]{:S(2)}, u32[]{:S(2)}) %collective-permute-start.20) | collective-permute-done | bytes 131104 | tf_op jit(solution)/shard_map/ppermute | solution.py:24
  132.7 0.8 fusion.45
  (103 shorter events, 5.1 us)
Async XLA Ops:
  0.0 1.2 copy-start
  0.0 13.9 %copy-start.8 = (bf16[128,1024]{1,0:T(8,128)(2,1)S(1)}, bf16[128,1024]{1,0:T(8,128)(2,1)}, u32[]{:S(2)}) copy-start(bf16[128,1024]{1,0:T(8,128)(2,1)} %param.13) | copy-start | bytes 786436
  1.4 9.4 %collective-permute-start = (bf16[8,128,128]{2,1,0:T(8,128)(2,1)S(1)}, bf16[8,128,128]{2,1,0:T(8,128)(2,1)S(1)}, u32[]{:S(2)}, u32[]{:S(2)}) collective-permute-start(bf16[8,128,128]{2,1,0:T(8,128)(2,1)S(1)} %convolution_convert_fusion.1), channel_id=1, source_target_pairs={{0,4},{4,0},{8,12},{12,8},{1,5},{5,1},{9,13},{13,9},{2,6},{6,2},{1... | collective-permute-start | bytes 786440 | tf_op jit(solution)/shard_map/ppermute | solution.py:18
  11.0 14.1 %collective-permute-start.1 = (bf16[8,128,128]{2,1,0:T(8,128)(2,1)S(1)}, bf16[8,128,128]{2,1,0:T(8,128)(2,1)S(1)}, u32[]{:S(2)}, u32[]{:S(2)}) collective-permute-start(bf16[8,128,128]{2,1,0:T(8,128)(2,1)S(1)} %get-tuple-element.14), channel_id=1, source_target_pairs={{0,8},{4,12},{8,0},{12,4},{1,9},{5,13},{9,1},{13,5},{2,10},{6,14},... | collective-permute-start | bytes 786440 | tf_op jit(solution)/shard_map/ppermute | solution.py:18
  27.3 3.1 %copy-start.12 = (s32[64,8]{0,1:T(8,128)S(1)}, s32[64,8]{0,1:T(8,128)}, u32[]{:S(2)}) copy-start(s32[64,8]{0,1:T(8,128)} %param.21) | copy-start | bytes 6148
  27.3 3.1 %copy-start.13 = (s32[64,8]{0,1:T(8,128)S(1)}, s32[64,8]{0,1:T(8,128)}, u32[]{:S(2)}) copy-start(s32[64,8]{0,1:T(8,128)} %param.22) | copy-start | bytes 6148
  27.3 6.1 %copy-start.14 = (f32[64,8]{0,1:T(8,128)S(1)}, f32[64,8]{0,1:T(8,128)}, u32[]{:S(2)}) copy-start(f32[64,8]{0,1:T(8,128)} %param.23) | copy-start | bytes 6148
  27.3 13.1 %copy-start.7 = (bf16[64,2048]{1,0:T(8,128)(2,1)S(1)}, bf16[64,2048]{1,0:T(8,128)(2,1)}, u32[]{:S(2)}) copy-start(bf16[64,2048]{1,0:T(8,128)(2,1)} %param.19) | copy-start | bytes 786436
  30.3 11.2 %copy-start.11 = (f32[2048]{0:T(1024)S(1)}, f32[2048]{0:T(1024)}, u32[]{:S(2)}) copy-start(f32[2048]{0:T(1024)} %param.20) | copy-start | bytes 24580
  30.3 1.6 %collective-permute-start.2 = (bf16[64,2048]{1,0:T(8,128)(2,1)S(1)}, bf16[64,2048]{1,0:T(8,128)(2,1)S(1)}, u32[]{:S(2)}, u32[]{:S(2)}) collective-permute-start(bf16[64,2048]{1,0:T(8,128)(2,1)S(1)} %fusion.29), channel_id=1, source_target_pairs={{0,1},{1,0},{2,3},{3,2},{4,5},{5,4},{6,7},{7,6},{8,9},{9,8},{10,11... | collective-permute-start | bytes 786440 | tf_op jit(solution)/shard_map/ppermute | solution.py:24
  32.0 8.4 %collective-permute-start.3 = (bf16[64,2048]{1,0:T(8,128)(2,1)S(1)}, bf16[64,2048]{1,0:T(8,128)(2,1)S(1)}, u32[]{:S(2)}, u32[]{:S(2)}) collective-permute-start(bf16[64,2048]{1,0:T(8,128)(2,1)S(1)} %fusion.18), channel_id=1, source_target_pairs={{0,2},{2,0},{1,3},{3,1},{4,6},{6,4},{5,7},{7,5},{8,10},{10,8},{9,1... | collective-permute-start | bytes 786440 | tf_op jit(solution)/shard_map/ppermute | solution.py:24
  33.4 12.2 %collective-permute-start.4 = (f32[24,64]{1,0:T(8,128)S(1)}, f32[24,64]{1,0:T(8,128)S(1)}, u32[]{:S(2)}, u32[]{:S(2)}) collective-permute-start(f32[24,64]{1,0:T(8,128)S(1)} %maximum_bitcast_fusion), channel_id=1, source_target_pairs={{0,4},{4,8},{8,12},{12,0},{1,5},{5,9},{9,13},{13,1},{2,6},{6,10},{... | collective-permute-start | bytes 18440 | tf_op jit(solution)/shard_map/ppermute | solution.py:24
  34.2 11.4 %collective-permute-start.5 = (f32[24,64]{1,0:T(8,128)S(1)}, f32[24,64]{1,0:T(8,128)S(1)}, u32[]{:S(2)}, u32[]{:S(2)}) collective-permute-start(f32[24,64]{1,0:T(8,128)S(1)} %maximum_bitcast_fusion), channel_id=1, source_target_pairs={{0,8},{4,12},{8,0},{12,4},{1,9},{5,13},{9,1},{13,5},{2,10},{6,14},... | collective-permute-start | bytes 18440 | tf_op jit(solution)/shard_map/ppermute | solution.py:24
  37.5 8.1 %collective-permute-start.6 = (f32[24,64]{1,0:T(8,128)S(1)}, f32[24,64]{1,0:T(8,128)S(1)}, u32[]{:S(2)}, u32[]{:S(2)}) collective-permute-start(f32[24,64]{1,0:T(8,128)S(1)} %maximum_bitcast_fusion), channel_id=1, source_target_pairs={{0,12},{4,0},{8,4},{12,8},{1,13},{5,1},{9,5},{13,9},{2,14},{6,2},{... | collective-permute-start | bytes 18440 | tf_op jit(solution)/shard_map/ppermute | solution.py:24
  37.5 19.7 %copy-start.15 = (f32[96]{0:T(128)}, f32[96]{0:T(128)S(1)}, u32[]{:S(2)}) copy-start(f32[96]{0:T(128)S(1)} %iota_convert_fusion) | copy-start | bytes 1156
  40.6 0.8 copy-start.3
  41.6 8.4 %collective-permute-start.8 = (bf16[64,1024]{1,0:T(8,128)(2,1)S(1)}, bf16[64,1024]{1,0:T(8,128)(2,1)S(1)}, u32[]{:S(2)}, u32[]{:S(2)}) collective-permute-start(bf16[64,1024]{1,0:T(8,128)(2,1)S(1)} %constant_dynamic-slice_fusion.8), channel_id=1, source_target_pairs={{0,4},{4,8},{8,12},{12,0},{1,5},{5,9},{9,13},{13,1},{2,6},{6,10},{... | collective-permute-start | bytes 393224 | tf_op jit(solution)/shard_map/ppermute | solution.py:24
  42.2 11.6 %collective-permute-start.10 = (bf16[64,1024]{1,0:T(8,128)(2,1)S(1)}, bf16[64,1024]{1,0:T(8,128)(2,1)S(1)}, u32[]{:S(2)}, u32[]{:S(2)}) collective-permute-start(bf16[64,1024]{1,0:T(8,128)(2,1)S(1)} %constant_dynamic-slice_fusion.8), channel_id=1, source_target_pairs={{0,8},{4,12},{8,0},{12,4},{1,9},{5,13},{9,1},{13,5},{2,10},{6,14},... | collective-permute-start | bytes 393224 | tf_op jit(solution)/shard_map/ppermute | solution.py:24
  45.6 9.6 %collective-permute-start.12 = (bf16[64,1024]{1,0:T(8,128)(2,1)S(1)}, bf16[64,1024]{1,0:T(8,128)(2,1)S(1)}, u32[]{:S(2)}, u32[]{:S(2)}) collective-permute-start(bf16[64,1024]{1,0:T(8,128)(2,1)S(1)} %constant_dynamic-slice_fusion.8), channel_id=1, source_target_pairs={{0,12},{4,0},{8,4},{12,8},{1,13},{5,1},{9,5},{13,9},{2,14},{6,2},{... | collective-permute-start | bytes 393224 | tf_op jit(solution)/shard_map/ppermute | solution.py:24
  45.7 1.2 collective-permute-start.7
  47.0 9.9 %copy-start.6 = (f32[24,512]{1,0:T(8,128)}, f32[24,512]{1,0:T(8,128)S(1)}, u32[]{:S(2)}) copy-start(f32[24,512]{1,0:T(8,128)S(1)} %concatenate.15) | copy-start | bytes 147460
  49.9 13.0 %collective-permute-start.9 = (bf16[64,1024]{1,0:T(8,128)(2,1)S(1)}, bf16[64,1024]{1,0:T(8,128)(2,1)S(1)}, u32[]{:S(2)}, u32[]{:S(2)}) collective-permute-start(bf16[64,1024]{1,0:T(8,128)(2,1)S(1)} %collective-permute-done.8), channel_id=1, source_target_pairs={{0,2},{2,0},{1,3},{3,1},{4,6},{6,4},{5,7},{7,5},{8,10},{10,8},{9,1... | collective-permute-start | bytes 393224 | tf_op jit(solution)/shard_map/ppermute | solution.py:24
  53.8 11.2 %collective-permute-start.11 = (bf16[64,1024]{1,0:T(8,128)(2,1)S(1)}, bf16[64,1024]{1,0:T(8,128)(2,1)S(1)}, u32[]{:S(2)}, u32[]{:S(2)}) collective-permute-start(bf16[64,1024]{1,0:T(8,128)(2,1)S(1)} %collective-permute-done.10), channel_id=1, source_target_pairs={{0,2},{2,0},{1,3},{3,1},{4,6},{6,4},{5,7},{7,5},{8,10},{10,8},{9,1... | collective-permute-start | bytes 393224 | tf_op jit(solution)/shard_map/ppermute | solution.py:24
  55.2 11.9 %collective-permute-start.13 = (bf16[64,1024]{1,0:T(8,128)(2,1)S(1)}, bf16[64,1024]{1,0:T(8,128)(2,1)S(1)}, u32[]{:S(2)}, u32[]{:S(2)}) collective-permute-start(bf16[64,1024]{1,0:T(8,128)(2,1)S(1)} %collective-permute-done.12), channel_id=1, source_target_pairs={{0,2},{2,0},{1,3},{3,1},{4,6},{6,4},{5,7},{7,5},{8,10},{10,8},{9,1... | collective-permute-start | bytes 393224 | tf_op jit(solution)/shard_map/ppermute | solution.py:24
  67.0 3.1 %copy-start.9 = (f32[8,512]{1,0:T(8,128)S(1)}, f32[8,512]{1,0:T(8,128)}, u32[]{:S(2)}) copy-start(f32[8,512]{1,0:T(8,128)} %get-tuple-element.24) | copy-start | bytes 49156
  67.1 3.1 %copy-start.10 = (f32[8,512]{1,0:T(8,128)S(1)}, f32[8,512]{1,0:T(8,128)}, u32[]{:S(2)}) copy-start(f32[8,512]{1,0:T(8,128)} %get-tuple-element.25) | copy-start | bytes 49156
  67.1 3.1 %copy-start.16 = (f32[8]{0:T(128)S(1)}, f32[8]{0:T(128)}, u32[]{:S(2)}) copy-start(f32[8]{0:T(128)} %add_convert_fusion.1) | copy-start | bytes 100
  69.3 4.8 %collective-permute-start.14 = (bf16[256,2048]{1,0:T(8,128)(2,1)S(1)}, bf16[256,2048]{1,0:T(8,128)(2,1)S(1)}, u32[]{:S(2)}, u32[]{:S(2)}) collective-permute-start(bf16[256,2048]{1,0:T(8,128)(2,1)S(1)} %pad_maximum_fusion), channel_id=1, source_target_pairs={{0,1},{1,0},{2,3},{3,2},{4,5},{5,4},{6,7},{7,6},{8,9},{9,8},{10,11... | collective-permute-start | bytes 3145736 | tf_op jit(solution)/shard_map/ppermute | solution.py:24
  71.3 2.9 %copy-start.5 = (pred[768,512]{1,0:T(32,128)(4,1)}, pred[768,512]{1,0:T(32,128)(4,1)S(1)}, u32[]{:S(2)}) copy-start(pred[768,512]{1,0:T(32,128)(4,1)S(1)} %bitcast_compare_fusion) | copy-start | bytes 1179652
  97.8 7.3 %copy-start.2 = (bf16[8,96,2048]{2,1,0:T(8,128)(2,1)S(1)}, bf16[8,96,2048]{2,1,0:T(8,128)(2,1)}, u32[]{:S(2)}) copy-start(bf16[8,96,2048]{2,1,0:T(8,128)(2,1)} %shard_map.127) | copy-start | bytes 9437188
  102.0 3.1 %collective-permute-start.15 = (bf16[256,2048]{1,0:T(8,128)(2,1)}, bf16[256,2048]{1,0:T(8,128)(2,1)}, u32[]{:S(2)}, u32[]{:S(2)}) collective-permute-start(bf16[256,2048]{1,0:T(8,128)(2,1)} %convolution_convert_fusion), channel_id=1, source_target_pairs={{0,1},{1,0},{2,3},{3,2},{4,5},{5,4},{6,7},{7,6},{8,9},{9,8},{10,11... | collective-permute-start | bytes 3145736 | tf_op jit(solution)/shard_map/ppermute | solution.py:24
  109.7 6.5 %collective-permute-start.17 = (bf16[1,64,1024]{2,1,0:T(8,128)(2,1)S(1)}, bf16[1,64,1024]{2,1,0:T(8,128)(2,1)}, u32[]{:S(2)}, u32[]{:S(2)}) collective-permute-start(bf16[1,64,1024]{2,1,0:T(8,128)(2,1)S(1)} %bitcast.203), channel_id=1, source_target_pairs={{0,2},{2,0},{1,3},{3,1},{4,6},{6,4},{5,7},{7,5},{8,10},{10,8},{9,1... | collective-permute-start | bytes 393224 | tf_op jit(solution)/shard_map/ppermute | solution.py:24
  111.2 8.7 %collective-permute-start.19 = (bf16[1,64,1024]{2,1,0:T(8,128)(2,1)S(1)}, bf16[1,64,1024]{2,1,0:T(8,128)(2,1)}, u32[]{:S(2)}, u32[]{:S(2)}) collective-permute-start(bf16[1,64,1024]{2,1,0:T(8,128)(2,1)S(1)} %bitcast.202), channel_id=1, source_target_pairs={{0,2},{2,0},{1,3},{3,1},{4,6},{6,4},{5,7},{7,5},{8,10},{10,8},{9,1... | collective-permute-start | bytes 393224 | tf_op jit(solution)/shard_map/ppermute | solution.py:24
  112.6 9.7 %collective-permute-start.21 = (bf16[1,64,1024]{2,1,0:T(8,128)(2,1)S(1)}, bf16[1,64,1024]{2,1,0:T(8,128)(2,1)S(1)}, u32[]{:S(2)}, u32[]{:S(2)}) collective-permute-start(bf16[1,64,1024]{2,1,0:T(8,128)(2,1)S(1)} %bitcast.201), channel_id=1, source_target_pairs={{0,2},{2,0},{1,3},{3,1},{4,6},{6,4},{5,7},{7,5},{8,10},{10,8},{9,1... | collective-permute-start | bytes 393224 | tf_op jit(solution)/shard_map/ppermute | solution.py:24
  114.1 18.6 %copy-start.4 = (f32[64,2048]{1,0:T(8,128)S(1)}, f32[64,2048]{1,0:T(8,128)}, u32[]{:S(2)}) copy-start(f32[64,2048]{1,0:T(8,128)} %copy-done.3) | copy-start | bytes 1572868
  114.5 19.0 %copy-start.1 = (bf16[128,1024]{1,0:T(8,128)(2,1)S(1)}, bf16[128,1024]{1,0:T(8,128)(2,1)}, u32[]{:S(2)}) copy-start(bf16[128,1024]{1,0:T(8,128)(2,1)} %param.15) | copy-start | bytes 786436
  114.8 9.9 %collective-permute-start.16 = (bf16[1,64,1024]{2,1,0:T(8,128)(2,1)S(1)}, bf16[1,64,1024]{2,1,0:T(8,128)(2,1)S(1)}, u32[]{:S(2)}, u32[]{:S(2)}) collective-permute-start(bf16[1,64,1024]{2,1,0:T(8,128)(2,1)S(1)} %bitcast.199), channel_id=1, source_target_pairs={{0,2},{2,0},{1,3},{3,1},{4,6},{6,4},{5,7},{7,5},{8,10},{10,8},{9,1... | collective-permute-start | bytes 393224 | tf_op jit(solution)/shard_map/ppermute | solution.py:24
  117.2 7.5 %collective-permute-start.18 = (bf16[64,1024]{1,0:T(8,128)(2,1)S(1)}, bf16[64,1024]{1,0:T(8,128)(2,1)S(1)}, u32[]{:S(2)}, u32[]{:S(2)}) collective-permute-start(bf16[64,1024]{1,0:T(8,128)(2,1)S(1)} %fusion.67), channel_id=1, source_target_pairs={{0,12},{4,0},{8,4},{12,8},{1,13},{5,1},{9,5},{13,9},{2,14},{6,2},{... | collective-permute-start | bytes 393224 | tf_op jit(solution)/shard_map/ppermute | solution.py:24
  120.8 11.9 %collective-permute-start.20 = (bf16[64,1024]{1,0:T(8,128)(2,1)S(1)}, bf16[64,1024]{1,0:T(8,128)(2,1)S(1)}, u32[]{:S(2)}, u32[]{:S(2)}) collective-permute-start(bf16[64,1024]{1,0:T(8,128)(2,1)S(1)} %fusion.68), channel_id=1, source_target_pairs={{0,8},{4,12},{8,0},{12,4},{1,9},{5,13},{9,1},{13,5},{2,10},{6,14},... | collective-permute-start | bytes 393224 | tf_op jit(solution)/shard_map/ppermute | solution.py:24
  122.4 10.3 %collective-permute-start.22 = (bf16[64,1024]{1,0:T(8,128)(2,1)S(1)}, bf16[64,1024]{1,0:T(8,128)(2,1)S(1)}, u32[]{:S(2)}, u32[]{:S(2)}) collective-permute-start(bf16[64,1024]{1,0:T(8,128)(2,1)S(1)} %fusion.69), channel_id=1, source_target_pairs={{0,4},{4,8},{8,12},{12,0},{1,5},{5,9},{9,13},{13,1},{2,6},{6,10},{... | collective-permute-start | bytes 393224 | tf_op jit(solution)/shard_map/ppermute | solution.py:24

commit v2 on v1

v2 whole, which is shorter than its diff:
```python
import functools

import jax
import jax.numpy as jnp
from jax import lax
from jax.experimental import pallas as pl
from jax.experimental.pallas import tpu as pltpu
from jax.sharding import PartitionSpec as P

D = 2048
HEAD_DIM = 128
EXPERTS = 64
TOPK = 8
LOCAL_LEVELS = 8
FUSED_BYTES = 4 << 20

bf16, f32 = jnp.bfloat16, jnp.float32
SMEM = pltpu.MemorySpace.SMEM
VMEM = pltpu.MemorySpace.VMEM


def moved(value, axis, distance):
    size = lax.axis_size(axis)
    pairs = [(source, (source + distance) % size) for source in range(size)]
    return lax.ppermute(value, axis, pairs)


def swapped(value, axis, distance, upward):
    mask = 2**distance
    pairs = [(s, s ^ mask) for s in range(lax.axis_size(axis)) if not (upward and s & mask)]
    return lax.ppermute(value, axis, pairs)


def dot(a, b, contract=((1,), (0,))):
    return lax.dot_general(a, b, (contract, ((), ())), preferred_element_type=f32)


def bit_length(numbers, digits):
    counted = jnp.zeros_like(numbers)
    for place_bit in range(digits):
        counted = counted + (numbers >= 1 << place_bit).astype(jnp.int32)
    return counted


def columns(head):
    return slice(head * HEAD_DIM, (head + 1) * HEAD_DIM)


def looked_up(index, table_ref, head):
    weight = jnp.zeros(index.shape, f32)
    for entry in range(table_ref.shape[0]):
        weight = jnp.where(index == entry, table_ref[entry, head], weight)
    return weight


def state_kernel(keys_ref, values_ref, out_ref):
    for head in range(out_ref.shape[0]):
        span = columns(head)
        out_ref[head] = dot(keys_ref[:, span], values_ref[:, span], ((0,), (0,))).astype(bf16)


def within_kernel(table_ref, queries_ref, keys_ref, values_ref, index_ref, out_ref):
    block = queries_ref.shape[0]
    rows = lax.broadcasted_iota(jnp.int32, (block, block), 0)
    cols = lax.broadcasted_iota(jnp.int32, (block, block), 1)
    depth = jnp.where(cols <= rows, bit_length(rows ^ cols, LOCAL_LEVELS), -1)
    index = index_ref[...]
    for head in range(out_ref.shape[1] // HEAD_DIM):
        span = columns(head)
        weight = looked_up(index, table_ref, head)
        mix = jnp.zeros((block, block), f32)
        for level in range(LOCAL_LEVELS):
            mix = jnp.where(depth == level, weight[:, level : level + 1], mix)
        scores = dot(queries_ref[:, span], keys_ref[:, span], ((1,), (1,)))
        mixed = (scores * mix).astype(bf16)
        out_ref[:, span] = dot(mixed, values_ref[:, span])


def project_kernel(n_levels, table_ref, place_ref, within_ref, queries_ref, index_ref, *rest):
    state_refs = rest[:n_levels]
    weight_ref, own_ref, away_ref, attended_ref = rest[n_levels:]

    @pl.when(pl.program_id(0) == 0)
    def _():
        index = index_ref[...]
        for head in range(queries_ref.shape[1] // HEAD_DIM):
            span = columns(head)
            weight = looked_up(index, table_ref, head)
            total = within_ref[:, span]
            for level in range(n_levels):
                read = dot(queries_ref[:, span], state_refs[level][head])
                column = LOCAL_LEVELS + level
                owned = (place_ref[1] >> level & 1).astype(f32)
                total = total + (weight[:, column : column + 1] * owned) * read
            attended_ref[:, span] = (total * HEAD_DIM ** (-0.5)).astype(bf16)

    tokens = own_ref.shape[0]
    n_sub = away_ref.shape[0] + 1
    my_sub = place_ref[0]
    weight = weight_ref[...]
    for hop in range(n_sub):
        start = pl.multiple_of((my_sub + hop) % n_sub * tokens, tokens)
        value = dot(attended_ref[pl.ds(start, tokens), :], weight)
        if hop:
            away_ref[hop - 1] = value.astype(bf16)
        else:
            own_ref[...] = value


def whole(shape):
    return pl.BlockSpec(shape, lambda *_: (0,) * len(shape))


def scalars():
    return pl.BlockSpec(memory_space=SMEM)


def attention(queries, keys, values, level_index, level_table, out_weight, my_tokens):
    block, width = queries.shape
    heads = width // HEAD_DIM
    n_seq, n_sub = lax.axis_size("seq"), lax.axis_size("sub")
    my_block = lax.axis_index("seq")
    state = pl.pallas_call(
        state_kernel, out_shape=jax.ShapeDtypeStruct((heads, HEAD_DIM, HEAD_DIM), bf16)
    )(keys, values)
    levels = n_seq.bit_length() - 1
    running = state.astype(f32)
    found = []
    for level in range(levels):
        partner = swapped(running.astype(bf16), "seq", level, level == levels - 1)
        found.append(partner)
        running = running + partner.astype(f32)
    within = pl.pallas_call(
        within_kernel,
        in_specs=[scalars()] + [pl.BlockSpec(memory_space=VMEM)] * 4,
        out_shape=jax.ShapeDtypeStruct((block, width), f32),
    )(level_table, queries, keys, values, level_index)
    place = jnp.stack([lax.axis_index("sub"), my_block]).astype(jnp.int32)
    out_width = out_weight.shape[1]
    step = out_width // 4
    return pl.pallas_call(
        functools.partial(project_kernel, levels),
        grid=(out_width // step,),
        in_specs=[
            scalars(),
            scalars(),
            whole((block, width)),
            whole((block, width)),
            whole(level_index.shape),
        ]
        + [whole((heads, HEAD_DIM, HEAD_DIM))] * levels
        + [pl.BlockSpec((width, step), lambda i: (0, i))],
        out_specs=[
            pl.BlockSpec((my_tokens, step), lambda i: (0, i)),
            pl.BlockSpec((n_sub - 1, my_tokens, step), lambda i: (0, 0, i)),
        ],
        out_shape=[
            jax.ShapeDtypeStruct((my_tokens, out_width), f32),
            jax.ShapeDtypeStruct((n_sub - 1, my_tokens, out_width), bf16),
        ],
        scratch_shapes=[pltpu.VMEM((block, width), bf16)],
    )(level_table, place, within, queries, level_index, *found, out_weight)


def swiglu(gate, up):
    return (gate / (1.0 + jnp.exp(-gate)) * up).astype(bf16)


def expert_kernel(rows_ref, gate_up_ref, down_ref, scale_ref, out_ref):
    pair = jnp.swapaxes(gate_up_ref[0], 0, 1)
    rows = rows_ref[0]
    active = swiglu(dot(rows, pair[0]), dot(rows, pair[1]))
    out_ref[0] = (dot(active, down_ref[0]) * scale_ref[0]).astype(bf16)


def run_experts(rows, w_gate_up, w_down, scale):
    experts, count, width = rows.shape
    hidden = w_down.shape[1]
    return pl.pallas_call(
        expert_kernel,
        grid=(experts,),
        in_specs=[
            pl.BlockSpec((1, count, width), lambda e: (e, 0, 0)),
            pl.BlockSpec((1, width, 2, hidden), lambda e: (e, 0, 0, 0)),
            pl.BlockSpec((1, hidden, width), lambda e: (e, 0, 0)),
            pl.BlockSpec((1, count, 1), lambda e: (e, 0, 0)),
        ],
        out_specs=pl.BlockSpec((1, count, width), lambda e: (e, 0, 0)),
        out_shape=jax.ShapeDtypeStruct(rows.shape, bf16),
    )(rows, w_gate_up, w_down, scale)


def routed(named, slots, weights, expert, slot_base):
    match = (named == expert) & (slots >= 0)
    place = jnp.sum(jnp.where(match, slots + slot_base + 1.0, 0.0), axis=-2, keepdims=True) - 1.0
    share = jnp.sum(jnp.where(match, weights, 0.0), axis=-2, keepdims=True)
    return place, share


def fused_kernel(n_pieces, n_head, capacity, where_ref, routes_ref, *rest):
    piece_refs = rest[:n_pieces]
    gate_up_ref, down_ref, out_ref, pick_ref, tokens_ref, rows_ref, scale_ref = rest[n_pieces:]
    step = pl.program_id(0)
    experts = pl.num_programs(0)
    count = scale_ref.shape[1]
    width = tokens_ref.shape[2]

    @pl.when(step == 0)
    def _():
        my_head = where_ref[1]
        size = piece_refs[0].shape[0]
        for number, ref in enumerate(piece_refs):
            block, side = divmod(number, n_head)
            part = (my_head + n_head - side) % n_head
            tokens_ref[part, block * size : (block + 1) * size, :] = ref[...]
        all_tokens = routes_ref.shape[1]
        named = routes_ref[0:TOPK, :]
        slots = routes_ref[TOPK : 2 * TOPK, :]
        weights = routes_ref[2 * TOPK : 3 * TOPK, :]
        lane = lax.broadcasted_iota(jnp.int32, (1, all_tokens), 1)
        slot_base = (lane // size * capacity).astype(f32)
        row = lax.broadcasted_iota(jnp.int32, (count, all_tokens), 0).astype(f32)
        for expert in range(scale_ref.shape[0]):
            name = (where_ref[0] + expert).astype(f32)
            place, share = routed(named, slots, weights, name, slot_base)
            chosen = place == row
            scale_ref[expert] = jnp.sum(jnp.where(chosen, share, 0.0), axis=1, keepdims=True)
            pick_ref[expert * count : (expert + 1) * count, :] = jnp.where(
                chosen, 1.0, 0.0
            ).astype(bf16)
        for part in range(n_head):
            rows_ref[part] = dot(pick_ref[...], tokens_ref[part]).astype(bf16)

    start = pl.multiple_of(step * count, count)
    pair = jnp.swapaxes(gate_up_ref[0], 0, 1)
    gate = up = 0.0
    for part in range(n_head):
        rows = rows_ref[part, pl.ds(start, count), :]
        span = slice(part * width, (part + 1) * width)
        gate = gate + dot(rows, pair[0, span, :])
        up = up + dot(rows, pair[1, span, :])
    piece = (dot(swiglu(gate, up), down_ref[0]) * scale_ref[step]).astype(bf16)
    for part in range(n_head):
        out_ref[part] = piece[:, part * width : (part + 1) * width]


def run_fused(where, routes, pieces, w_gate_up, w_down, n_head, capacity):
    experts, full, _, hidden = w_gate_up.shape
    size, width = pieces[0].shape
    all_tokens = routes.shape[1]
    count = all_tokens // size * capacity
    return pl.pallas_call(
        functools.partial(fused_kernel, len(pieces), n_head, capacity),
        grid=(experts,),
        in_specs=[scalars(), whole(routes.shape)]
        + [whole((size, width))] * len(pieces)
        + [
            pl.BlockSpec((1, full, 2, hidden), lambda e: (e, 0, 0, 0)),
            pl.BlockSpec((1, hidden, full), lambda e: (e, 0, 0)),
        ],
        out_specs=[
            pl.BlockSpec((n_head, count, width), lambda e: (0, e, 0)),
            whole((experts * count, all_tokens)),
        ],
        out_shape=[
            jax.ShapeDtypeStruct((n_head, experts * count, width), bf16),
            jax.ShapeDtypeStruct((experts * count, all_tokens), bf16),
        ],
        scratch_shapes=[
            pltpu.VMEM((n_head, all_tokens, width), bf16),
            pltpu.VMEM((n_head, experts * count, width), bf16),
            pltpu.VMEM((experts, count, 1), f32),
        ],
    )(where, routes, *pieces, w_gate_up, w_down)


def combine_kernel(part_ref, pick_ref, rows_ref, *rest):
    out_ref = rest[-1]
    value = dot(pick_ref[...], rows_ref[0], ((0,), (0,)))
    for ref in rest[:-1]:
        value = value + ref[...].astype(f32)
    out_ref[...] = value.astype(out_ref.dtype)


def run_combine(part, pick, rows, sub, n_sub, extra, dtype):
    total, all_tokens = pick.shape
    tokens = all_tokens // n_sub
    width = rows.shape[2]
    return pl.pallas_call(
        combine_kernel,
        grid_spec=pltpu.PrefetchScalarGridSpec(
            num_scalar_prefetch=1,
            grid=(1,),
            in_specs=[
                pl.BlockSpec((total, tokens), lambda i, part_ref: (0, sub)),
                pl.BlockSpec((1, total, width), lambda i, part_ref: (part_ref[0], 0, 0)),
            ]
            + [whole((tokens, width))] * len(extra),
            out_specs=whole((tokens, width)),
        ),
        out_shape=jax.ShapeDtypeStruct((tokens, width), dtype),
    )(part, pick, rows, *extra)


def on_device(
    queries,
    keys,
    values,
    level_index,
    level_table,
    out_weight,
    residual,
    norm_gain,
    expert_ids,
    expert_slots,
    route_weight,
    w_gate_up,
    w_down,
):
    n_seq, n_head, n_sub = (lax.axis_size(name) for name in ("seq", "head", "sub"))
    my_seq, my_head, my_sub = (lax.axis_index(name) for name in ("seq", "head", "sub"))
    my_tokens = residual.shape[0]
    route = jnp.concatenate(
        [expert_ids.astype(f32), expert_slots.astype(f32), route_weight], axis=1
    ).T
    routes = [route] + [moved(route, "seq", hop) for hop in range(1, n_seq)]
    routes = jnp.concatenate(routes, axis=1)
    routes = jnp.concatenate([routes] + [moved(routes, "sub", hop) for hop in range(1, n_sub)], axis=1)

    my_rows, away = attention(
        queries, keys, values, level_index, level_table, out_weight, my_tokens
    )
    for hop in range(1, n_sub):
        my_rows = my_rows + moved(away[hop - 1], "sub", hop).astype(f32)
    shared = my_rows.astype(bf16)
    total = shared.astype(f32)
    for hop in range(1, n_head):
        total = total + moved(shared, "head", hop).astype(f32)
    stream = residual.astype(f32) + total
    mean_square = jnp.mean(stream * stream, axis=-1, keepdims=True)
    normed = (stream * lax.rsqrt(mean_square + 1e-06) * norm_gain).astype(bf16)

    width = D // n_head
    capacity = 3 * (my_tokens * TOPK // EXPERTS) // 2
    exp_here = w_gate_up.shape[0]
    all_tokens = routes.shape[1]
    first = (my_seq * n_sub + my_sub) * exp_here
    stream_part = lax.dynamic_slice_in_dim(stream, my_head * width, width, 1)

    def part_of(value, side):
        return lax.dynamic_slice_in_dim(value, (my_head - side) % n_head * width, width, 1)

    mine = part_of(normed, 0)
    if all_tokens * D * 2 <= FUSED_BYTES:
        blocks = [[part_of(normed, side) for side in range(n_head)]]
        for hop in range(1, n_seq):
            part = moved(mine, "seq", hop)
            blocks.append([part] + [moved(part, "head", side) for side in range(1, n_head)])
        pieces = [piece for block in blocks for piece in block]
        pieces = pieces + [
            moved(piece, "sub", hop) for hop in range(1, n_sub) for piece in pieces
        ]
        where = jnp.stack([first, my_head]).astype(jnp.int32)
        rows, pick = run_fused(where, routes, pieces, w_gate_up, w_down, n_head, capacity)

        reduced = []
        for side in [*range(1, n_head), 0]:
            part = ((my_head + side) % n_head).astype(jnp.int32).reshape(1)
            extra = [
                moved(run_combine(part, pick, rows, hop, n_sub, [], bf16), "sub", -hop)
                for hop in range(1, n_sub)
            ]
            value = run_combine(part, pick, rows, 0, n_sub, extra, bf16 if side else f32)
            reduced.append(value.reshape(n_seq, my_tokens, width))
        expert_sum = 0.0
        for hop in [*range(1, n_seq), 0]:
            own = reduced[-1][hop]
            for side in range(1, n_head):
                own = own + moved(reduced[side - 1][hop], "head", side).astype(f32)
            if hop:
                own = moved(own.astype(bf16), "seq", -hop).astype(f32)
            expert_sum = expert_sum + own
        return (stream_part + expert_sum).astype(bf16)

    step = max(1, n_seq // 4)
    gathered = [normed]
    for begin in range(1, n_seq, step):
        hops = range(begin, min(begin + step, n_seq))
        part = jnp.concatenate([moved(mine, "seq", hop) for hop in hops], axis=0)
        joined = jnp.zeros((n_head, part.shape[0], width), bf16)
        parts = [part] + [moved(part, "head", side) for side in range(1, n_head)]
        for side, piece in enumerate(parts):
            joined = lax.dynamic_update_index_in_dim(joined, piece, (my_head - side) % n_head, 0)
        gathered.append(jnp.transpose(joined, (1, 0, 2)).reshape(-1, D))
    here = jnp.concatenate(gathered, axis=0)

    named, slots, weights = jnp.split(routes, 3, axis=0)
    count = all_tokens // my_tokens * capacity
    local = (first + jnp.arange(exp_here, dtype=jnp.int32)).astype(f32)
    block_of = (jnp.arange(all_tokens, dtype=jnp.int32) // my_tokens * capacity).astype(f32)
    place, share = routed(named[None], slots[None], weights[None], local[:, None, None], block_of)
    row = jnp.arange(count, dtype=jnp.int32).astype(f32)
    chosen = place == row[None, :, None]
    scale = jnp.sum(jnp.where(chosen, share, 0.0), axis=2, keepdims=True)
    pick = chosen.astype(bf16).reshape(exp_here * count, all_tokens)
    picks = jnp.split(pick, n_sub, axis=1)
    rows = dot(picks[0], here)
    for hop in range(1, n_sub):
        rows = rows + dot(picks[hop], moved(here, "sub", hop))
    rows = rows.astype(bf16).reshape(exp_here, count, D)
    pieces = run_experts(rows, w_gate_up, w_down, scale).reshape(-1, D)

    def combined(part):
        return dot(part, pieces, ((0,), (0,)))

    sent = [moved(combined(picks[hop]).astype(bf16), "sub", -hop) for hop in range(1, n_sub)]
    merged = combined(picks[0])
    for value in sent:
        merged = merged + value.astype(f32)
    by_head = merged.reshape(n_seq, my_tokens, n_head, width)
    expert_sum = 0.0
    for begin in range(0, n_seq, step):
        hops = range(begin, min(begin + step, n_seq))
        group = by_head[begin : hops[-1] + 1]
        own = lax.dynamic_index_in_dim(group, my_head, 2, keepdims=False)
        for side in range(1, n_head):
            away = lax.dynamic_index_in_dim(group, (my_head + side) % n_head, 2, keepdims=False)
            own = own + moved(away.astype(bf16), "head", side).astype(f32)
        for place_in, hop in enumerate(hops):
            value = own[place_in]
            if hop:
                value = moved(value.astype(bf16), "seq", -hop).astype(f32)
            expert_sum = expert_sum + value
    return (stream_part + expert_sum).astype(bf16)


def solution(mesh):
    return jax.shard_map(
        on_device,
        mesh=mesh,
        in_specs=(
            P(("groups", "seq"), ("head", "sub")),
            P(("groups", "seq"), ("head", "sub")),
            P(("groups", "seq"), ("head", "sub")),
            P(("groups", "seq"), None),
            P(None, ("head", "sub")),
            P(("head", "sub"), None),
            P(("groups", "seq", "sub"), None),
            P(),
            P(("groups", "seq", "sub"), None),
            P(("groups", "seq", "sub"), None),
            P(("groups", "seq", "sub"), None),
            P(("seq", "sub"), None, None, "head"),
            P(("seq", "sub"), "head", None),
        ),
        out_specs=P(("groups", "seq", "sub"), "head"),
        check_vma=False,
    )
```

time: 134 us -> 136 us (1.015)
  Pallas kernels: 21 us -> 47.5 us
  matrix products: 16 us -> 0 us
  local copies, waits for them, and re-layouts: 20.9 us -> 8.26 us
  starting transfers between devices: 30.1 us -> 34.9 us
  waiting for transfers between devices: 37.1 us -> 33.6 us
  other arithmetic: 7.72 us -> 10.5 us
    pallas_call x1 -> x8, Pallas kernels: 21 us -> 47.5 us  [the longest x1 23.8 us: run_fused(): pl.pallas_call(functools.partial(fused_kernel, len(pieces), n_head, capac...]
    dot_general x9 -> x0, matrix products: 16 us -> none  [the longest x2 6.58 us: combined(): lax.dot_general(part, pieces, (((0,), (0,)), ((), ())), preferred_element...]
    dynamic_update_slice x6 -> x0, local copies, waits for them, and re-layouts: 10.7 us -> none  [on_device(): lax.dynamic_update_index_in_dim(whole, piece, (my_head - side) % n_head, 0)]
    ppermute x2, waiting for transfers between devices: 16.2 us -> 6.52 us  [swapped(): return lax.ppermute(value, axis, pairs)]
    ppermute x21 -> x29, waiting for transfers between devices: 20.9 us -> 27.1 us  [moved(): return lax.ppermute(value, axis, pairs)]
    unnamed x42, local copies, waits for them, and re-layouts: 1.26 us -> 6.42 us
    ppermute x21 -> x29, starting transfers between devices: 24.2 us -> 27.2 us  [moved(): return lax.ppermute(value, axis, pairs)]
    broadcast_in_dim x7 -> x0, local copies, waits for them, and re-layouts: 2.17 us -> none  [the longest x6 1.22 us: on_device(): lax.dynamic_update_index_in_dim(whole, piece, (my_head - side) % n_head, 0)]
  transfers between devices with their start and end apart: 23 -> 31, of which waited for: 9 -> 11; matrix products, arithmetic and copies ran while one was open for 17% -> 8% of each run, Pallas kernels for 0% -> 9%
where the time goes in v2:
time: 136 us; the launch traced here: 135 us
  Pallas kernels  47.5 us (35%)
  starting transfers between devices  34.9 us (26%)
  waiting for transfers between devices  33.6 us (25%)
  other arithmetic  10.5 us (8%)
  local copies, waits for them, and re-layouts  8.26 us (6%)
    ppermute x29, starting transfers between devices, moved(): return lax.ppermute(value, axis, pairs)  27.2 us
    ppermute x29, waiting for transfers between devices, moved(): return lax.ppermute(value, axis, pairs)  27.1 us
    pallas_call x1, Pallas kernels, run_fused(): pl.pallas_call(functools.partial(fused_kernel, len(pieces), n_head, capac...  23.8 us
    pallas_call x4, Pallas kernels, run_combine(): pl.pallas_call(combine_kernel, grid_spec=pltpu.PrefetchScalarGridSpec(num...  12.2 us
    ppermute x2, starting transfers between devices, swapped(): return lax.ppermute(value, axis, pairs)  7.73 us
    ppermute x2, waiting for transfers between devices, swapped(): return lax.ppermute(value, axis, pairs)  6.52 us
    unnamed x42, local copies, waits for them, and re-layouts  6.42 us
    pallas_call x1, Pallas kernels, attention(): pl.pallas_call(functools.partial(project_kernel, levels), grid=(out_width...  5.92 us
  transfers between devices with their start and end apart: 31, of which 11 were waited for; matrix products, arithmetic and copies ran while one was open for 8% of the time, Pallas kernels for 9%

profile of v2, /device:TPU:0, one launch (start us, length us, event | category | flops | bytes accessed | tf_op | source)
XLA Modules:
  0.0 135.1 jit_solution(16993487526021737156)
XLA Ops:
  0.0 2.0 %shard_map.128 = bf16[8,128,128]{2,1,0:T(8,128)(2,1)} custom-call(bf16[128,1024]{1,0:T(8,128)(2,1)} %keys_ref.3, bf16[128,1024]{1,0:T(8,128)(2,1)} %values_ref.3), custom_call_target="tpu_custom_call" | custom-call | tf_op jit(solution)/shard_map/pallas_call | solution.py:123
  2.0 3.1 %collective-permute-start = (bf16[8,128,128]{2,1,0:T(8,128)(2,1)}, bf16[8,128,128]{2,1,0:T(8,128)(2,1)S(1)}, u32[]{:S(2)}, u32[]{:S(2)}) collective-permute-start(bf16[8,128,128]{2,1,0:T(8,128)(2,1)} %shard_map.128), channel_id=1, source_target_pairs={{0,4},{4,0},{8,12},{12,8},{1,5},{5,1},{9,13},{13,9},{2,6},{6,2},{1... | collective-permute-start | bytes 786440 | tf_op jit(solution)/shard_map/ppermute | solution.py:31
  5.0 6.5 %collective-permute-done.rest_0_ = bf16[8,128,128]{2,1,0:T(8,128)(2,1)S(1)} collective-permute-done((bf16[8,128,128]{2,1,0:T(8,128)(2,1)}, bf16[8,128,128]{2,1,0:T(8,128)(2,1)S(1)}, u32[]{:S(2)}, u32[]{:S(2)}) %collective-permute-start) | collective-permute-done | bytes 262176 | tf_op jit(solution)/shard_map/ppermute | solution.py:31
  11.6 1.1 add_convert_fusion.1
  12.7 4.7 %collective-permute-start.1 = (bf16[8,128,128]{2,1,0:T(8,128)(2,1)S(1)}, bf16[8,128,128]{2,1,0:T(8,128)(2,1)S(1)}, u32[]{:S(2)}, u32[]{:S(2)}) collective-permute-start(bf16[8,128,128]{2,1,0:T(8,128)(2,1)S(1)} %add_convert_fusion.1), channel_id=1, source_target_pairs={{0,8},{4,12},{1,9},{5,13},{2,10},{6,14},{3,11},{7,15},{16,24},{20,... | collective-permute-start | bytes 786440 | tf_op jit(solution)/shard_map/ppermute | solution.py:31
  17.4 1.4 %copy.15.index_ref = s32[128,21]{1,0:T(8,128)} copy(s32[128,21]{0,1:T(8,128)} %param.16) | data formatting | bytes 21504 | tf_op args[3]
  18.8 1.4 copy.16.table_ref
  20.2 3.6 %shard_map.127.within_ref = f32[128,1024]{1,0:T(8,128)} custom-call(f32[16,8]{1,0:T(8,128)} %copy.16.table_ref, bf16[128,1024]{1,0:T(8,128)(2,1)} %queries_ref.3, bf16[128,1024]{1,0:T(8,128)(2,1)} %keys_ref.3, bf16[128,1024]{1,0:T(8,128)(2,1)} %values_ref.3, s32[128,21]{1,0:T(8,128)} %copy.15.index_ref), custom_call_target="tpu_custom_call" | custom-call | tf_op jit(solution)/shard_map/pallas_call | solution.py:133
  23.8 0.7 pad_add_fusion.place_ref
  24.4 0.7 copy-done.5
  25.1 5.9 %shard_map.129 = (f32[64,2048]{1,0:T(8,128)}, bf16[1,64,2048]{2,1,0:T(8,128)(2,1)}) custom-call(f32[16,8]{1,0:T(8,128)} %copy.16.table_ref, s32[2]{0:T(128)} %pad_add_fusion.place_ref, f32[128,1024]{1,0:T(8,128)} %shard_map.127.within_ref, bf16[128,1024]{1,0:T(8,128)(2,1)} %queries_ref.3, s32[128,21]{1,0:T(8,128)} %copy.15.index_ref, ...), custom_call_target="tpu_custom_call" | custom-call | tf_op jit(solution)/shard_map/pallas_call | solution.py:141
  31.1 1.7 %collective-permute-done.2 = bf16[64,2048]{1,0:T(8,128)(2,1)S(1)} collective-permute-done((bf16[64,2048]{1,0:T(8,128)(2,1)}, bf16[64,2048]{1,0:T(8,128)(2,1)S(1)}, u32[]{:S(2)}, u32[]{:S(2)}) %collective-permute-start.2) | collective-permute-done | bytes 262176 | tf_op jit(solution)/shard_map/ppermute | solution.py:25
  32.8 1.1 add_convert_fusion
  33.9 1.6 %collective-permute-start.3 = (bf16[64,2048]{1,0:T(8,128)(2,1)S(1)}, bf16[64,2048]{1,0:T(8,128)(2,1)S(1)}, u32[]{:S(2)}, u32[]{:S(2)}) collective-permute-start(bf16[64,2048]{1,0:T(8,128)(2,1)S(1)} %add_convert_fusion), channel_id=1, source_target_pairs={{0,2},{2,0},{1,3},{3,1},{4,6},{6,4},{5,7},{7,5},{8,10},{10,8},{9,1... | collective-permute-start | bytes 786440 | tf_op jit(solution)/shard_map/ppermute | solution.py:25
  35.5 0.7 convert_element_type.75
  36.1 0.7 convert_element_type.76
  36.8 0.7 maximum_bitcast_fusion
  37.5 4.7 %collective-permute-start.4 = (f32[24,64]{1,0:T(8,128)S(1)}, f32[24,64]{1,0:T(8,128)S(1)}, u32[]{:S(2)}, u32[]{:S(2)}) collective-permute-start(f32[24,64]{1,0:T(8,128)S(1)} %maximum_bitcast_fusion), channel_id=1, source_target_pairs={{0,4},{4,8},{8,12},{12,0},{1,5},{5,9},{9,13},{13,1},{2,6},{6,10},{... | collective-permute-start | bytes 18440 | tf_op jit(solution)/shard_map/ppermute | solution.py:25
  42.2 3.4 %collective-permute-start.5 = (f32[24,64]{1,0:T(8,128)S(1)}, f32[24,64]{1,0:T(8,128)S(1)}, u32[]{:S(2)}, u32[]{:S(2)}) collective-permute-start(f32[24,64]{1,0:T(8,128)S(1)} %maximum_bitcast_fusion), channel_id=1, source_target_pairs={{0,8},{4,12},{8,0},{12,4},{1,9},{5,13},{9,1},{13,5},{2,10},{6,14},... | collective-permute-start | bytes 18440 | tf_op jit(solution)/shard_map/ppermute | solution.py:25
  45.6 1.2 multiply_reduce_fusion
  46.8 0.8 multiply_convert_fusion
  47.7 2.1 %collective-permute-start.8 = (bf16[64,1024]{1,0:T(8,128)(2,1)S(1)}, bf16[64,1024]{1,0:T(8,128)(2,1)S(1)}, u32[]{:S(2)}, u32[]{:S(2)}) collective-permute-start(bf16[64,1024]{1,0:T(8,128)(2,1)S(1)} %get-tuple-element.23.rest_0_), channel_id=1, source_target_pairs={{0,4},{4,8},{8,12},{12,0},{1,5},{5,9},{9,13},{13,1},{2,6},{6,10},{... | collective-permute-start | bytes 393224 | tf_op jit(solution)/shard_map/ppermute | solution.py:25
  49.7 2.8 %collective-permute-start.10 = (bf16[64,1024]{1,0:T(8,128)(2,1)S(1)}, bf16[64,1024]{1,0:T(8,128)(2,1)S(1)}, u32[]{:S(2)}, u32[]{:S(2)}) collective-permute-start(bf16[64,1024]{1,0:T(8,128)(2,1)S(1)} %get-tuple-element.23.rest_0_), channel_id=1, source_target_pairs={{0,8},{4,12},{8,0},{12,4},{1,9},{5,13},{9,1},{13,5},{2,10},{6,14},... | collective-permute-start | bytes 393224 | tf_op jit(solution)/shard_map/ppermute | solution.py:25
  52.6 0.1 pad_maximum_fusion
  52.7 0.5 collective-permute-start.7
  53.2 0.8 collective-permute-done.7
  54.0 0.3 collective-permute-start.15
  54.4 2.0 %collective-permute-done.8.rest_2_ = bf16[64,1024]{1,0:T(8,128)(2,1)S(1)} collective-permute-done((bf16[64,1024]{1,0:T(8,128)(2,1)S(1)}, bf16[64,1024]{1,0:T(8,128)(2,1)S(1)}, u32[]{:S(2)}, u32[]{:S(2)}) %collective-permute-start.8) | collective-permute-done | bytes 131104 | tf_op jit(solution)/shard_map/ppermute | solution.py:25
  56.4 1.5 %collective-permute-start.9 = (bf16[64,1024]{1,0:T(8,128)(2,1)S(1)}, bf16[64,1024]{1,0:T(8,128)(2,1)S(1)}, u32[]{:S(2)}, u32[]{:S(2)}) collective-permute-start(bf16[64,1024]{1,0:T(8,128)(2,1)S(1)} %collective-permute-done.8.rest_2_), channel_id=1, source_target_pairs={{0,2},{2,0},{1,3},{3,1},{4,6},{6,4},{5,7},{7,5},{8,10},{10,8},{9,1... | collective-permute-start | bytes 393224 | tf_op jit(solution)/shard_map/ppermute | solution.py:25
  57.9 2.8 %collective-permute-done.10.rest_4_ = bf16[64,1024]{1,0:T(8,128)(2,1)S(1)} collective-permute-done((bf16[64,1024]{1,0:T(8,128)(2,1)S(1)}, bf16[64,1024]{1,0:T(8,128)(2,1)S(1)}, u32[]{:S(2)}, u32[]{:S(2)}) %collective-permute-start.10) | collective-permute-done | bytes 131104 | tf_op jit(solution)/shard_map/ppermute | solution.py:25
  60.6 1.5 %collective-permute-start.11 = (bf16[64,1024]{1,0:T(8,128)(2,1)S(1)}, bf16[64,1024]{1,0:T(8,128)(2,1)S(1)}, u32[]{:S(2)}, u32[]{:S(2)}) collective-permute-start(bf16[64,1024]{1,0:T(8,128)(2,1)S(1)} %collective-permute-done.10.rest_4_), channel_id=1, source_target_pairs={{0,2},{2,0},{1,3},{3,1},{4,6},{6,4},{5,7},{7,5},{8,10},{10,8},{9,1... | collective-permute-start | bytes 393224 | tf_op jit(solution)/shard_map/ppermute | solution.py:25
  62.1 0.5 collective-permute-start.13
  62.7 0.5 collective-permute-start.18
  63.2 0.1 collective-permute-start.20
  63.3 3.7 %collective-permute-done.11.rest_5_ = bf16[64,1024]{1,0:T(8,128)(2,1)S(1)} collective-permute-done((bf16[64,1024]{1,0:T(8,128)(2,1)S(1)}, bf16[64,1024]{1,0:T(8,128)(2,1)S(1)}, u32[]{:S(2)}, u32[]{:S(2)}) %collective-permute-start.11) | collective-permute-done | bytes 131104 | tf_op jit(solution)/shard_map/ppermute | solution.py:25
  67.0 1.8 %collective-permute-done.13.rest_7_ = bf16[64,1024]{1,0:T(8,128)(2,1)S(1)} collective-permute-done((bf16[64,1024]{1,0:T(8,128)(2,1)S(1)}, bf16[64,1024]{1,0:T(8,128)(2,1)S(1)}, u32[]{:S(2)}, u32[]{:S(2)}) %collective-permute-start.13) | collective-permute-done | bytes 131104 | tf_op jit(solution)/shard_map/ppermute | solution.py:25
  68.8 0.5 collective-permute-start.21
  69.3 0.6 pad_add_fusion.1.where_ref
  69.9 0.7 concatenate.12.routes_ref
  70.8 0.5 copy-done.15
  71.4 0.7 copy-done.19
  72.0 23.8 %shard_map.130 = (bf16[2,768,1024]{2,1,0:T(8,128)(2,1)}, bf16[768,512]{1,0:T(8,128)(2,1)}) custom-call(s32[2]{0:T(128)} %pad_add_fusion.1.where_ref, f32[24,512]{1,0:T(8,128)} %concatenate.12.routes_ref, bf16[64,1024]{1,0:T(8,128)(2,1)} %copy-done.2, bf16[64,1024]{1,0:T(8,128)(2,1)} %copy-done.1, bf16[64,1024]{1,0:T(8,128)(2,1)} %copy-done.6, ...), custom_call_target="tpu_custom_call" | custom-call | tf_op jit(solution)/shard_map/pallas_call | solution.py:252
  95.9 3.0 %shard_map.133 = bf16[256,1024]{1,0:T(8,128)(2,1)} custom-call(s32[1]{0:T(128)} %bitcast.7.part_ref, bf16[768,512]{1,0:T(8,128)(2,1)} %get-tuple-element.11.pick_ref, bf16[2,768,1024]{2,1,0:T(8,128)(2,1)} %get-tuple-element.12.rows_ref), custom_call_target="tpu_custom_call" | custom-call | tf_op jit(solution)/shard_map/pallas_call | solution.py:289
  98.8 0.1 collective-permute-start.23
  98.9 2.9 %shard_map.131 = bf16[256,1024]{1,0:T(8,128)(2,1)} custom-call(s32[1]{0:T(128)} %bitcast.3.part_ref, bf16[768,512]{1,0:T(8,128)(2,1)} %get-tuple-element.11.pick_ref, bf16[2,768,1024]{2,1,0:T(8,128)(2,1)} %get-tuple-element.12.rows_ref), custom_call_target="tpu_custom_call" | custom-call | tf_op jit(solution)/shard_map/pallas_call | solution.py:289
  101.8 0.4 collective-permute-start.22
  102.3 0.8 copy-done.3
  103.1 3.0 %shard_map.134 = bf16[256,1024]{1,0:T(8,128)(2,1)} custom-call(s32[1]{0:T(128)} %bitcast.7.part_ref, bf16[768,512]{1,0:T(8,128)(2,1)} %get-tuple-element.11.pick_ref, bf16[2,768,1024]{2,1,0:T(8,128)(2,1)} %get-tuple-element.12.rows_ref, bf16[256,1024]{1,0:T(8,128)(2,1)} %copy-done.3), custom_call_target="tpu_custom_call" | custom-call | tf_op jit(solution)/shard_map/pallas_call | solution.py:289
  106.1 1.1 fusion.6
  107.2 1.6 %collective-permute-start.24 = (bf16[64,1024]{1,0:T(8,128)(2,1)S(1)}, bf16[64,1024]{1,0:T(8,128)(2,1)S(1)}, u32[]{:S(2)}, u32[]{:S(2)}) collective-permute-start(bf16[64,1024]{1,0:T(8,128)(2,1)S(1)} %get-tuple-element.18), channel_id=1, source_target_pairs={{0,2},{2,0},{1,3},{3,1},{4,6},{6,4},{5,7},{7,5},{8,10},{10,8},{9,1... | collective-permute-start | bytes 393224 | tf_op jit(solution)/shard_map/ppermute | solution.py:25
  108.8 0.5 collective-permute-start.26
  109.3 1.5 %collective-permute-start.28 = (bf16[64,1024]{1,0:T(8,128)(2,1)S(1)}, bf16[64,1024]{1,0:T(8,128)(2,1)S(1)}, u32[]{:S(2)}, u32[]{:S(2)}) collective-permute-start(bf16[64,1024]{1,0:T(8,128)(2,1)S(1)} %get-tuple-element.20), channel_id=1, source_target_pairs={{0,2},{2,0},{1,3},{3,1},{4,6},{6,4},{5,7},{7,5},{8,10},{10,8},{9,1... | collective-permute-start | bytes 393224 | tf_op jit(solution)/shard_map/ppermute | solution.py:25
  110.9 0.5 collective-permute-start.30
  111.4 0.8 copy-done.4
  112.2 3.2 %shard_map.132 = f32[256,1024]{1,0:T(8,128)} custom-call(s32[1]{0:T(128)} %bitcast.3.part_ref, bf16[768,512]{1,0:T(8,128)(2,1)} %get-tuple-element.11.pick_ref, bf16[2,768,1024]{2,1,0:T(8,128)(2,1)} %get-tuple-element.12.rows_ref, bf16[256,1024]{1,0:T(8,128)(2,1)} %copy-done.4), custom_call_target="tpu_custom_call" | custom-call | tf_op jit(solution)/shard_map/pallas_call | solution.py:289
  115.4 1.1 collective-permute-done.26
  116.5 2.8 %collective-permute-done.28 = bf16[64,1024]{1,0:T(8,128)(2,1)S(1)} collective-permute-done((bf16[64,1024]{1,0:T(8,128)(2,1)S(1)}, bf16[64,1024]{1,0:T(8,128)(2,1)S(1)}, u32[]{:S(2)}, u32[]{:S(2)}) %collective-permute-start.28) | collective-permute-done | bytes 131104 | tf_op jit(solution)/shard_map/ppermute | solution.py:25
  119.3 1.2 fusion.5
  120.5 2.0 %collective-permute-start.25 = (bf16[64,1024]{1,0:T(8,128)(2,1)S(1)}, bf16[64,1024]{1,0:T(8,128)(2,1)S(1)}, u32[]{:S(2)}, u32[]{:S(2)}) collective-permute-start(bf16[64,1024]{1,0:T(8,128)(2,1)S(1)} %get-tuple-element.15), channel_id=1, source_target_pairs={{0,12},{4,0},{8,4},{12,8},{1,13},{5,1},{9,5},{13,9},{2,14},{6,2},{... | collective-permute-start | bytes 393224 | tf_op jit(solution)/shard_map/ppermute | solution.py:25
  122.5 0.1 collective-permute-start.27
  122.6 0.5 collective-permute-start.29
  123.1 3.2 %collective-permute-done.25 = bf16[64,1024]{1,0:T(8,128)(2,1)S(1)} collective-permute-done((bf16[64,1024]{1,0:T(8,128)(2,1)S(1)}, bf16[64,1024]{1,0:T(8,128)(2,1)S(1)}, u32[]{:S(2)}, u32[]{:S(2)}) %collective-permute-start.25) | collective-permute-done | bytes 131104 | tf_op jit(solution)/shard_map/ppermute | solution.py:25
  126.3 7.0 %collective-permute-done.27 = bf16[64,1024]{1,0:T(8,128)(2,1)S(1)} collective-permute-done((bf16[64,1024]{1,0:T(8,128)(2,1)S(1)}, bf16[64,1024]{1,0:T(8,128)(2,1)S(1)}, u32[]{:S(2)}, u32[]{:S(2)}) %collective-permute-start.27) | collective-permute-done | bytes 131104 | tf_op jit(solution)/shard_map/ppermute | solution.py:25
  133.4 1.7 %fusion.2 = bf16[64,1024]{1,0:T(8,128)(2,1)} fusion(f32[256,1024]{1,0:T(8,128)} %shard_map.132, bf16[64,1024]{1,0:T(8,128)(2,1)S(1)} %collective-permute-done.30, bf16[64,1024]{1,0:T(8,128)(2,1)S(1)} %collective-permute-done.29, bf16[64,1024]{1,0:T(8,128)(2,1)S(1)} %collective-permute-done.27, bf16[64,1024]{1,0:T(8,128)(2,1)S(1)} %collective-permute-done.25, ...), kind=kLoop, calls=%fused_computation.8 | loop fusion | flops 655360 | bytes 1179652 | tf_op jit(solution)/shard_map/convert_element_type | solution.py:383
  (64 shorter events, 0.4 us)
Async XLA Ops:
  2.0 9.6 %collective-permute-start = (bf16[8,128,128]{2,1,0:T(8,128)(2,1)}, bf16[8,128,128]{2,1,0:T(8,128)(2,1)S(1)}, u32[]{:S(2)}, u32[]{:S(2)}) collective-permute-start(bf16[8,128,128]{2,1,0:T(8,128)(2,1)} %shard_map.128), channel_id=1, source_target_pairs={{0,4},{4,0},{8,12},{12,8},{1,5},{5,1},{9,13},{13,9},{2,6},{6,2},{1... | collective-permute-start | bytes 786440 | tf_op jit(solution)/shard_map/ppermute | solution.py:31
  11.6 12.9 %copy-start = (bf16[8,128,128]{2,1,0:T(8,128)(2,1)}, bf16[8,128,128]{2,1,0:T(8,128)(2,1)S(1)}, u32[]{:S(2)}) copy-start(bf16[8,128,128]{2,1,0:T(8,128)(2,1)S(1)} %collective-permute-done.rest_0_) | copy-start | bytes 786436
  12.7 11.7 %collective-permute-start.1 = (bf16[8,128,128]{2,1,0:T(8,128)(2,1)S(1)}, bf16[8,128,128]{2,1,0:T(8,128)(2,1)S(1)}, u32[]{:S(2)}, u32[]{:S(2)}) collective-permute-start(bf16[8,128,128]{2,1,0:T(8,128)(2,1)S(1)} %add_convert_fusion.1), channel_id=1, source_target_pairs={{0,8},{4,12},{1,9},{5,13},{2,10},{6,14},{3,11},{7,15},{16,24},{20,... | collective-permute-start | bytes 786440 | tf_op jit(solution)/shard_map/ppermute | solution.py:31
  24.4 0.7 copy-start.5
  31.0 1.7 %collective-permute-start.2 = (bf16[64,2048]{1,0:T(8,128)(2,1)}, bf16[64,2048]{1,0:T(8,128)(2,1)S(1)}, u32[]{:S(2)}, u32[]{:S(2)}) collective-permute-start(bf16[64,2048]{1,0:T(8,128)(2,1)} %bitcast.9), channel_id=1, source_target_pairs={{0,1},{1,0},{2,3},{3,2},{4,5},{5,4},{6,7},{7,6},{8,9},{9,8},{10,11... | collective-permute-start | bytes 786440 | tf_op jit(solution)/shard_map/ppermute | solution.py:25
  33.9 11.7 %collective-permute-start.3 = (bf16[64,2048]{1,0:T(8,128)(2,1)S(1)}, bf16[64,2048]{1,0:T(8,128)(2,1)S(1)}, u32[]{:S(2)}, u32[]{:S(2)}) collective-permute-start(bf16[64,2048]{1,0:T(8,128)(2,1)S(1)} %add_convert_fusion), channel_id=1, source_target_pairs={{0,2},{2,0},{1,3},{3,1},{4,6},{6,4},{5,7},{7,5},{8,10},{10,8},{9,1... | collective-permute-start | bytes 786440 | tf_op jit(solution)/shard_map/ppermute | solution.py:25
  37.5 15.0 %collective-permute-start.4 = (f32[24,64]{1,0:T(8,128)S(1)}, f32[24,64]{1,0:T(8,128)S(1)}, u32[]{:S(2)}, u32[]{:S(2)}) collective-permute-start(f32[24,64]{1,0:T(8,128)S(1)} %maximum_bitcast_fusion), channel_id=1, source_target_pairs={{0,4},{4,8},{8,12},{12,0},{1,5},{5,9},{9,13},{13,1},{2,6},{6,10},{... | collective-permute-start | bytes 18440 | tf_op jit(solution)/shard_map/ppermute | solution.py:25
  42.2 10.3 %collective-permute-start.5 = (f32[24,64]{1,0:T(8,128)S(1)}, f32[24,64]{1,0:T(8,128)S(1)}, u32[]{:S(2)}, u32[]{:S(2)}) collective-permute-start(f32[24,64]{1,0:T(8,128)S(1)} %maximum_bitcast_fusion), channel_id=1, source_target_pairs={{0,8},{4,12},{8,0},{12,4},{1,9},{5,13},{9,1},{13,5},{2,10},{6,14},... | collective-permute-start | bytes 18440 | tf_op jit(solution)/shard_map/ppermute | solution.py:25
  45.6 7.0 %collective-permute-start.6 = (f32[24,64]{1,0:T(8,128)S(1)}, f32[24,64]{1,0:T(8,128)S(1)}, u32[]{:S(2)}, u32[]{:S(2)}) collective-permute-start(f32[24,64]{1,0:T(8,128)S(1)} %maximum_bitcast_fusion), channel_id=1, source_target_pairs={{0,12},{4,0},{8,4},{12,8},{1,13},{5,1},{9,5},{13,9},{2,14},{6,2},{... | collective-permute-start | bytes 18440 | tf_op jit(solution)/shard_map/ppermute | solution.py:25
  47.6 23.0 %copy-start.1 = (bf16[64,1024]{1,0:T(8,128)(2,1)}, bf16[64,1024]{1,0:T(8,128)(2,1)S(1)}, u32[]{:S(2)}) copy-start(bf16[64,1024]{1,0:T(8,128)(2,1)S(1)} %get-tuple-element.22.rest_1_) | copy-start | bytes 393220
  47.7 23.0 %copy-start.2 = (bf16[64,1024]{1,0:T(8,128)(2,1)}, bf16[64,1024]{1,0:T(8,128)(2,1)S(1)}, u32[]{:S(2)}) copy-start(bf16[64,1024]{1,0:T(8,128)(2,1)S(1)} %get-tuple-element.23.rest_0_) | copy-start | bytes 393220
  47.7 8.7 %collective-permute-start.8 = (bf16[64,1024]{1,0:T(8,128)(2,1)S(1)}, bf16[64,1024]{1,0:T(8,128)(2,1)S(1)}, u32[]{:S(2)}, u32[]{:S(2)}) collective-permute-start(bf16[64,1024]{1,0:T(8,128)(2,1)S(1)} %get-tuple-element.23.rest_0_), channel_id=1, source_target_pairs={{0,4},{4,8},{8,12},{12,0},{1,5},{5,9},{9,13},{13,1},{2,6},{6,10},{... | collective-permute-start | bytes 393224 | tf_op jit(solution)/shard_map/ppermute | solution.py:25
  49.7 10.9 %collective-permute-start.10 = (bf16[64,1024]{1,0:T(8,128)(2,1)S(1)}, bf16[64,1024]{1,0:T(8,128)(2,1)S(1)}, u32[]{:S(2)}, u32[]{:S(2)}) collective-permute-start(bf16[64,1024]{1,0:T(8,128)(2,1)S(1)} %get-tuple-element.23.rest_0_), channel_id=1, source_target_pairs={{0,8},{4,12},{8,0},{12,4},{1,9},{5,13},{9,1},{13,5},{2,10},{6,14},... | collective-permute-start | bytes 393224 | tf_op jit(solution)/shard_map/ppermute | solution.py:25
  52.5 9.6 %collective-permute-start.12 = (bf16[64,1024]{1,0:T(8,128)(2,1)S(1)}, bf16[64,1024]{1,0:T(8,128)(2,1)S(1)}, u32[]{:S(2)}, u32[]{:S(2)}) collective-permute-start(bf16[64,1024]{1,0:T(8,128)(2,1)S(1)} %get-tuple-element.23.rest_0_), channel_id=1, source_target_pairs={{0,12},{4,0},{8,4},{12,8},{1,13},{5,1},{9,5},{13,9},{2,14},{6,2},{... | collective-permute-start | bytes 393224 | tf_op jit(solution)/shard_map/ppermute | solution.py:25
  52.5 10.2 %collective-permute-start.14 = (bf16[64,1024]{1,0:T(8,128)(2,1)S(1)}, bf16[64,1024]{1,0:T(8,128)(2,1)S(1)}, u32[]{:S(2)}, u32[]{:S(2)}) collective-permute-start(bf16[64,1024]{1,0:T(8,128)(2,1)S(1)} %get-tuple-element.23.rest_0_), channel_id=1, source_target_pairs={{0,1},{1,0},{2,3},{3,2},{4,5},{5,4},{6,7},{7,6},{8,9},{9,8},{10,11... | collective-permute-start | bytes 393224 | tf_op jit(solution)/shard_map/ppermute | solution.py:25
  52.7 1.3 collective-permute-start.7
  54.0 8.7 %collective-permute-start.15 = (bf16[64,1024]{1,0:T(8,128)(2,1)S(1)}, bf16[64,1024]{1,0:T(8,128)(2,1)S(1)}, u32[]{:S(2)}, u32[]{:S(2)}) collective-permute-start(bf16[64,1024]{1,0:T(8,128)(2,1)S(1)} %get-tuple-element.22.rest_1_), channel_id=1, source_target_pairs={{0,1},{1,0},{2,3},{3,2},{4,5},{5,4},{6,7},{7,6},{8,9},{9,8},{10,11... | collective-permute-start | bytes 393224 | tf_op jit(solution)/shard_map/ppermute | solution.py:25
  56.4 14.3 %copy-start.6 = (bf16[64,1024]{1,0:T(8,128)(2,1)}, bf16[64,1024]{1,0:T(8,128)(2,1)S(1)}, u32[]{:S(2)}) copy-start(bf16[64,1024]{1,0:T(8,128)(2,1)S(1)} %collective-permute-done.8.rest_2_) | copy-start | bytes 393220
  56.4 6.8 %collective-permute-start.9 = (bf16[64,1024]{1,0:T(8,128)(2,1)S(1)}, bf16[64,1024]{1,0:T(8,128)(2,1)S(1)}, u32[]{:S(2)}, u32[]{:S(2)}) collective-permute-start(bf16[64,1024]{1,0:T(8,128)(2,1)S(1)} %collective-permute-done.8.rest_2_), channel_id=1, source_target_pairs={{0,2},{2,0},{1,3},{3,1},{4,6},{6,4},{5,7},{7,5},{8,10},{10,8},{9,1... | collective-permute-start | bytes 393224 | tf_op jit(solution)/shard_map/ppermute | solution.py:25
  60.6 10.0 %copy-start.7 = (bf16[64,1024]{1,0:T(8,128)(2,1)}, bf16[64,1024]{1,0:T(8,128)(2,1)S(1)}, u32[]{:S(2)}) copy-start(bf16[64,1024]{1,0:T(8,128)(2,1)S(1)} %collective-permute-done.10.rest_4_) | copy-start | bytes 393220
  60.6 6.4 %collective-permute-start.11 = (bf16[64,1024]{1,0:T(8,128)(2,1)S(1)}, bf16[64,1024]{1,0:T(8,128)(2,1)S(1)}, u32[]{:S(2)}, u32[]{:S(2)}) collective-permute-start(bf16[64,1024]{1,0:T(8,128)(2,1)S(1)} %collective-permute-done.10.rest_4_), channel_id=1, source_target_pairs={{0,2},{2,0},{1,3},{3,1},{4,6},{6,4},{5,7},{7,5},{8,10},{10,8},{9,1... | collective-permute-start | bytes 393224 | tf_op jit(solution)/shard_map/ppermute | solution.py:25
  62.1 8.5 %copy-start.8 = (bf16[64,1024]{1,0:T(8,128)(2,1)}, bf16[64,1024]{1,0:T(8,128)(2,1)S(1)}, u32[]{:S(2)}) copy-start(bf16[64,1024]{1,0:T(8,128)(2,1)S(1)} %collective-permute-done.12.rest_6_) | copy-start | bytes 393220
  62.1 6.6 %collective-permute-start.13 = (bf16[64,1024]{1,0:T(8,128)(2,1)S(1)}, bf16[64,1024]{1,0:T(8,128)(2,1)S(1)}, u32[]{:S(2)}, u32[]{:S(2)}) collective-permute-start(bf16[64,1024]{1,0:T(8,128)(2,1)S(1)} %collective-permute-done.12.rest_6_), channel_id=1, source_target_pairs={{0,2},{2,0},{1,3},{3,1},{4,6},{6,4},{5,7},{7,5},{8,10},{10,8},{9,1... | collective-permute-start | bytes 393224 | tf_op jit(solution)/shard_map/ppermute | solution.py:25
  62.7 8.0 %copy-start.9 = (bf16[64,1024]{1,0:T(8,128)(2,1)}, bf16[64,1024]{1,0:T(8,128)(2,1)S(1)}, u32[]{:S(2)}) copy-start(bf16[64,1024]{1,0:T(8,128)(2,1)S(1)} %collective-permute-done.14.rest_8_) | copy-start | bytes 393220
  62.7 6.1 %collective-permute-start.16 = (bf16[64,1024]{1,0:T(8,128)(2,1)S(1)}, bf16[64,1024]{1,0:T(8,128)(2,1)S(1)}, u32[]{:S(2)}, u32[]{:S(2)}) collective-permute-start(bf16[64,1024]{1,0:T(8,128)(2,1)S(1)} %collective-permute-done.8.rest_2_), channel_id=1, source_target_pairs={{0,1},{1,0},{2,3},{3,2},{4,5},{5,4},{6,7},{7,6},{8,9},{9,8},{10,11... | collective-permute-start | bytes 393224 | tf_op jit(solution)/shard_map/ppermute | solution.py:25
  62.7 8.0 %copy-start.10 = (bf16[64,1024]{1,0:T(8,128)(2,1)}, bf16[64,1024]{1,0:T(8,128)(2,1)S(1)}, u32[]{:S(2)}) copy-start(bf16[64,1024]{1,0:T(8,128)(2,1)S(1)} %collective-permute-done.15.rest_9_) | copy-start | bytes 393220
  62.7 7.9 %collective-permute-start.18 = (bf16[64,1024]{1,0:T(8,128)(2,1)S(1)}, bf16[64,1024]{1,0:T(8,128)(2,1)S(1)}, u32[]{:S(2)}, u32[]{:S(2)}) collective-permute-start(bf16[64,1024]{1,0:T(8,128)(2,1)S(1)} %collective-permute-done.10.rest_4_), channel_id=1, source_target_pairs={{0,1},{1,0},{2,3},{3,2},{4,5},{5,4},{6,7},{7,6},{8,9},{9,8},{10,11... | collective-permute-start | bytes 393224 | tf_op jit(solution)/shard_map/ppermute | solution.py:25
  63.2 7.5 %copy-start.11 = (bf16[64,1024]{1,0:T(8,128)(2,1)}, bf16[64,1024]{1,0:T(8,128)(2,1)S(1)}, u32[]{:S(2)}) copy-start(bf16[64,1024]{1,0:T(8,128)(2,1)S(1)} %collective-permute-done.9.rest_3_) | copy-start | bytes 393220
  63.2 7.4 %collective-permute-start.20 = (bf16[64,1024]{1,0:T(8,128)(2,1)S(1)}, bf16[64,1024]{1,0:T(8,128)(2,1)S(1)}, u32[]{:S(2)}, u32[]{:S(2)}) collective-permute-start(bf16[64,1024]{1,0:T(8,128)(2,1)S(1)} %collective-permute-done.12.rest_6_), channel_id=1, source_target_pairs={{0,1},{1,0},{2,3},{3,2},{4,5},{5,4},{6,7},{7,6},{8,9},{9,8},{10,11... | collective-permute-start | bytes 393224 | tf_op jit(solution)/shard_map/ppermute | solution.py:25
  67.0 3.7 %copy-start.12 = (bf16[64,1024]{1,0:T(8,128)(2,1)}, bf16[64,1024]{1,0:T(8,128)(2,1)S(1)}, u32[]{:S(2)}) copy-start(bf16[64,1024]{1,0:T(8,128)(2,1)S(1)} %collective-permute-done.11.rest_5_) | copy-start | bytes 393220
  67.0 3.6 %collective-permute-start.17 = (bf16[64,1024]{1,0:T(8,128)(2,1)S(1)}, bf16[64,1024]{1,0:T(8,128)(2,1)S(1)}, u32[]{:S(2)}, u32[]{:S(2)}) collective-permute-start(bf16[64,1024]{1,0:T(8,128)(2,1)S(1)} %collective-permute-done.9.rest_3_), channel_id=1, source_target_pairs={{0,1},{1,0},{2,3},{3,2},{4,5},{5,4},{6,7},{7,6},{8,9},{9,8},{10,11... | collective-permute-start | bytes 393224 | tf_op jit(solution)/shard_map/ppermute | solution.py:25
  68.8 2.0 %copy-start.13 = (bf16[64,1024]{1,0:T(8,128)(2,1)}, bf16[64,1024]{1,0:T(8,128)(2,1)S(1)}, u32[]{:S(2)}) copy-start(bf16[64,1024]{1,0:T(8,128)(2,1)S(1)} %collective-permute-done.13.rest_7_) | copy-start | bytes 393220
  68.8 1.8 %collective-permute-start.19 = (bf16[64,1024]{1,0:T(8,128)(2,1)S(1)}, bf16[64,1024]{1,0:T(8,128)(2,1)S(1)}, u32[]{:S(2)}, u32[]{:S(2)}) collective-permute-start(bf16[64,1024]{1,0:T(8,128)(2,1)S(1)} %collective-permute-done.11.rest_5_), channel_id=1, source_target_pairs={{0,1},{1,0},{2,3},{3,2},{4,5},{5,4},{6,7},{7,6},{8,9},{9,8},{10,11... | collective-permute-start | bytes 393224 | tf_op jit(solution)/shard_map/ppermute | solution.py:25
  68.8 2.0 %copy-start.14 = (bf16[64,1024]{1,0:T(8,128)(2,1)}, bf16[64,1024]{1,0:T(8,128)(2,1)S(1)}, u32[]{:S(2)}) copy-start(bf16[64,1024]{1,0:T(8,128)(2,1)S(1)} %collective-permute-done.16.rest_10_) | copy-start | bytes 393220
  68.8 1.8 %collective-permute-start.21 = (bf16[64,1024]{1,0:T(8,128)(2,1)S(1)}, bf16[64,1024]{1,0:T(8,128)(2,1)S(1)}, u32[]{:S(2)}, u32[]{:S(2)}) collective-permute-start(bf16[64,1024]{1,0:T(8,128)(2,1)S(1)} %collective-permute-done.13.rest_7_), channel_id=1, source_target_pairs={{0,1},{1,0},{2,3},{3,2},{4,5},{5,4},{6,7},{7,6},{8,9},{9,8},{10,11... | collective-permute-start | bytes 393224 | tf_op jit(solution)/shard_map/ppermute | solution.py:25
  70.6 0.6 copy-start.15
  70.6 0.7 copy-start.16
  70.6 0.7 copy-start.17
  70.6 0.7 copy-start.18
  71.4 0.7 copy-start.19
  98.8 3.5 %collective-permute-start.23 = (bf16[256,1024]{1,0:T(8,128)(2,1)}, bf16[256,1024]{1,0:T(8,128)(2,1)S(1)}, u32[]{:S(2)}, u32[]{:S(2)}) collective-permute-start(bf16[256,1024]{1,0:T(8,128)(2,1)} %shard_map.133), channel_id=1, source_target_pairs={{0,1},{1,0},{2,3},{3,2},{4,5},{5,4},{6,7},{7,6},{8,9},{9,8},{10,11... | collective-permute-start | bytes 1572872 | tf_op jit(solution)/shard_map/ppermute | solution.py:25
  101.8 9.5 %collective-permute-start.22 = (bf16[256,1024]{1,0:T(8,128)(2,1)}, bf16[256,1024]{1,0:T(8,128)(2,1)S(1)}, u32[]{:S(2)}, u32[]{:S(2)}) collective-permute-start(bf16[256,1024]{1,0:T(8,128)(2,1)} %shard_map.131), channel_id=1, source_target_pairs={{0,1},{1,0},{2,3},{3,2},{4,5},{5,4},{6,7},{7,6},{8,9},{9,8},{10,11... | collective-permute-start | bytes 1572872 | tf_op jit(solution)/shard_map/ppermute | solution.py:25
  102.3 0.8 copy-start.3
  107.2 8.1 %collective-permute-start.24 = (bf16[64,1024]{1,0:T(8,128)(2,1)S(1)}, bf16[64,1024]{1,0:T(8,128)(2,1)S(1)}, u32[]{:S(2)}, u32[]{:S(2)}) collective-permute-start(bf16[64,1024]{1,0:T(8,128)(2,1)S(1)} %get-tuple-element.18), channel_id=1, source_target_pairs={{0,2},{2,0},{1,3},{3,1},{4,6},{6,4},{5,7},{7,5},{8,10},{10,8},{9,1... | collective-permute-start | bytes 393224 | tf_op jit(solution)/shard_map/ppermute | solution.py:25
  108.8 7.7 %collective-permute-start.26 = (bf16[64,1024]{1,0:T(8,128)(2,1)S(1)}, bf16[64,1024]{1,0:T(8,128)(2,1)S(1)}, u32[]{:S(2)}, u32[]{:S(2)}) collective-permute-start(bf16[64,1024]{1,0:T(8,128)(2,1)S(1)} %get-tuple-element.21), channel_id=1, source_target_pairs={{0,2},{2,0},{1,3},{3,1},{4,6},{6,4},{5,7},{7,5},{8,10},{10,8},{9,1... | collective-permute-start | bytes 393224 | tf_op jit(solution)/shard_map/ppermute | solution.py:25
  109.3 10.0 %collective-permute-start.28 = (bf16[64,1024]{1,0:T(8,128)(2,1)S(1)}, bf16[64,1024]{1,0:T(8,128)(2,1)S(1)}, u32[]{:S(2)}, u32[]{:S(2)}) collective-permute-start(bf16[64,1024]{1,0:T(8,128)(2,1)S(1)} %get-tuple-element.20), channel_id=1, source_target_pairs={{0,2},{2,0},{1,3},{3,1},{4,6},{6,4},{5,7},{7,5},{8,10},{10,8},{9,1... | collective-permute-start | bytes 393224 | tf_op jit(solution)/shard_map/ppermute | solution.py:25
  110.9 12.2 %collective-permute-start.30 = (bf16[64,1024]{1,0:T(8,128)(2,1)S(1)}, bf16[64,1024]{1,0:T(8,128)(2,1)S(1)}, u32[]{:S(2)}, u32[]{:S(2)}) collective-permute-start(bf16[64,1024]{1,0:T(8,128)(2,1)S(1)} %get-tuple-element.19), channel_id=1, source_target_pairs={{0,2},{2,0},{1,3},{3,1},{4,6},{6,4},{5,7},{7,5},{8,10},{10,8},{9,1... | collective-permute-start | bytes 393224 | tf_op jit(solution)/shard_map/ppermute | solution.py:25
  111.4 0.8 copy-start.4
  120.5 5.8 %collective-permute-start.25 = (bf16[64,1024]{1,0:T(8,128)(2,1)S(1)}, bf16[64,1024]{1,0:T(8,128)(2,1)S(1)}, u32[]{:S(2)}, u32[]{:S(2)}) collective-permute-start(bf16[64,1024]{1,0:T(8,128)(2,1)S(1)} %get-tuple-element.15), channel_id=1, source_target_pairs={{0,12},{4,0},{8,4},{12,8},{1,13},{5,1},{9,5},{13,9},{2,14},{6,2},{... | collective-permute-start | bytes 393224 | tf_op jit(solution)/shard_map/ppermute | solution.py:25
  122.5 10.9 %collective-permute-start.27 = (bf16[64,1024]{1,0:T(8,128)(2,1)S(1)}, bf16[64,1024]{1,0:T(8,128)(2,1)S(1)}, u32[]{:S(2)}, u32[]{:S(2)}) collective-permute-start(bf16[64,1024]{1,0:T(8,128)(2,1)S(1)} %get-tuple-element.17), channel_id=1, source_target_pairs={{0,8},{4,12},{8,0},{12,4},{1,9},{5,13},{9,1},{13,5},{2,10},{6,14},... | collective-permute-start | bytes 393224 | tf_op jit(solution)/shard_map/ppermute | solution.py:25
  122.6 10.8 %collective-permute-start.29 = (bf16[64,1024]{1,0:T(8,128)(2,1)S(1)}, bf16[64,1024]{1,0:T(8,128)(2,1)S(1)}, u32[]{:S(2)}, u32[]{:S(2)}) collective-permute-start(bf16[64,1024]{1,0:T(8,128)(2,1)S(1)} %get-tuple-element.16), channel_id=1, source_target_pairs={{0,4},{4,8},{8,12},{12,0},{1,5},{5,9},{9,13},{13,1},{2,6},{6,10},{... | collective-permute-start | bytes 393224 | tf_op jit(solution)/shard_map/ppermute | solution.py:25

commit v3 on v2

--- a/solution.py
+++ b/solution.py
@@ -48,8 +48,8 @@
 
 def looked_up(index, table_ref, head):
     weight = jnp.zeros(index.shape, f32)
-    for entry in range(table_ref.shape[0]):
-        weight = jnp.where(index == entry, table_ref[entry, head], weight)
+    for entry in range(table_ref.shape[1]):
+        weight = jnp.where(index == float(entry), table_ref[head, entry], weight)
     return weight
 
 
@@ -59,13 +59,16 @@
         out_ref[head] = dot(keys_ref[:, span], values_ref[:, span], ((0,), (0,))).astype(bf16)
 
 
-def within_kernel(table_ref, queries_ref, keys_ref, values_ref, index_ref, out_ref):
+def within_kernel(table_ref, queries_ref, keys_ref, values_ref, index_ref, out_ref, weight_ref):
     block = queries_ref.shape[0]
+    heads = queries_ref.shape[1] // HEAD_DIM
+    levels = weight_ref.shape[1] // heads
+    my_block = lax.axis_index("seq")
     rows = lax.broadcasted_iota(jnp.int32, (block, block), 0)
     cols = lax.broadcasted_iota(jnp.int32, (block, block), 1)
     depth = jnp.where(cols <= rows, bit_length(rows ^ cols, LOCAL_LEVELS), -1)
-    index = index_ref[...]
-    for head in range(out_ref.shape[1] // HEAD_DIM):
+    index = index_ref[...].astype(f32).T
+    for head in range(heads):
         span = columns(head)
         weight = looked_up(index, table_ref, head)
         mix = jnp.zeros((block, block), f32)
@@ -74,29 +77,31 @@
         scores = dot(queries_ref[:, span], keys_ref[:, span], ((1,), (1,)))
         mixed = (scores * mix).astype(bf16)
         out_ref[:, span] = dot(mixed, values_ref[:, span])
-
-
-def project_kernel(n_levels, table_ref, place_ref, within_ref, queries_ref, index_ref, *rest):
+        for level in range(levels):
+            owned = (my_block >> level & 1).astype(f32)
+            column, slot = LOCAL_LEVELS + level, head * levels + level
+            weight_ref[:, slot : slot + 1] = weight[:, column : column + 1] * owned
+
+
+def project_kernel(n_levels, within_ref, queries_ref, level_ref, *rest):
     state_refs = rest[:n_levels]
     weight_ref, own_ref, away_ref, attended_ref = rest[n_levels:]
 
     @pl.when(pl.program_id(0) == 0)
     def _():
-        index = index_ref[...]
         for head in range(queries_ref.shape[1] // HEAD_DIM):
             span = columns(head)
-            weight = looked_up(index, table_ref, head)
             total = within_ref[:, span]
+            joined = jnp.concatenate([ref[head] for ref in state_refs], axis=1)
+            reads = dot(queries_ref[:, span], joined)
             for level in range(n_levels):
-                read = dot(queries_ref[:, span], state_refs[level][head])
-                column = LOCAL_LEVELS + level
-                owned = (place_ref[1] >> level & 1).astype(f32)
-                total = total + (weight[:, column : column + 1] * owned) * read
+                slot = head * n_levels + level
+                total = total + level_ref[:, slot : slot + 1] * reads[:, columns(level)]
             attended_ref[:, span] = (total * HEAD_DIM ** (-0.5)).astype(bf16)
 
     tokens = own_ref.shape[0]
     n_sub = away_ref.shape[0] + 1
-    my_sub = place_ref[0]
+    my_sub = lax.axis_index("sub")
     weight = weight_ref[...]
     for hop in range(n_sub):
         start = pl.multiple_of((my_sub + hop) % n_sub * tokens, tokens)
@@ -107,6 +112,10 @@
             own_ref[...] = value
 
 
+def grant(mebibytes):
+    return pltpu.CompilerParams(vmem_limit_bytes=mebibytes << 20)
+
+
 def whole(shape):
     return pl.BlockSpec(shape, lambda *_: (0,) * len(shape))
 
@@ -115,39 +124,48 @@
     return pl.BlockSpec(memory_space=SMEM)
 
 
-def attention(queries, keys, values, level_index, level_table, out_weight, my_tokens):
+def attention(queries, keys, values, level_index, level_table, out_weight, my_tokens, route):
     block, width = queries.shape
     heads = width // HEAD_DIM
     n_seq, n_sub = lax.axis_size("seq"), lax.axis_size("sub")
-    my_block = lax.axis_index("seq")
     state = pl.pallas_call(
-        state_kernel, out_shape=jax.ShapeDtypeStruct((heads, HEAD_DIM, HEAD_DIM), bf16)
+        state_kernel,
+        out_shape=jax.ShapeDtypeStruct((heads, HEAD_DIM, HEAD_DIM), bf16),
+        compiler_params=grant(8),
     )(keys, values)
     levels = n_seq.bit_length() - 1
+    in_vmem = pl.BlockSpec(memory_space=VMEM)
+    within, level_weight = pl.pallas_call(
+        within_kernel,
+        in_specs=[scalars()] + [in_vmem] * 4,
+        out_shape=[
+            jax.ShapeDtypeStruct((block, width), f32),
+            jax.ShapeDtypeStruct((block, heads * levels), f32),
+        ],
+        compiler_params=grant(8),
+    )(level_table.T, queries, keys, values, level_index.T)
     running = state.astype(f32)
     found = []
     for level in range(levels):
-        partner = swapped(running.astype(bf16), "seq", level, level == levels - 1)
+        sent = running.astype(bf16)
+        last = level == levels - 1
+        if last:
+            sent, within, level_weight, route = lax.optimization_barrier(
+                (sent, within, level_weight, route)
+            )
+        partner = swapped(sent, "seq", level, last)
         found.append(partner)
         running = running + partner.astype(f32)
-    within = pl.pallas_call(
-        within_kernel,
-        in_specs=[scalars()] + [pl.BlockSpec(memory_space=VMEM)] * 4,
-        out_shape=jax.ShapeDtypeStruct((block, width), f32),
-    )(level_table, queries, keys, values, level_index)
-    place = jnp.stack([lax.axis_index("sub"), my_block]).astype(jnp.int32)
+    routes = [route] + [moved(route, "seq", hop) for hop in range(1, n_seq)]
+    routes = jnp.concatenate(routes, axis=1)
+    routes = jnp.concatenate([routes] + [moved(routes, "sub", hop) for hop in range(1, n_sub)], axis=1)
+    found[-1], routes = lax.optimization_barrier((found[-1], routes))
     out_width = out_weight.shape[1]
     step = out_width // 4
-    return pl.pallas_call(
+    own, away = pl.pallas_call(
         functools.partial(project_kernel, levels),
         grid=(out_width // step,),
-        in_specs=[
-            scalars(),
-            scalars(),
-            whole((block, width)),
-            whole((block, width)),
-            whole(level_index.shape),
-        ]
+        in_specs=[whole((block, width)), whole((block, width)), whole(level_weight.shape)]
         + [whole((heads, HEAD_DIM, HEAD_DIM))] * levels
         + [pl.BlockSpec((width, step), lambda i: (0, i))],
         out_specs=[
@@ -159,7 +177,9 @@
             jax.ShapeDtypeStruct((n_sub - 1, my_tokens, out_width), bf16),
         ],
         scratch_shapes=[pltpu.VMEM((block, width), bf16)],
-    )(level_table, place, within, queries, level_index, *found, out_weight)
+        compiler_params=grant(12),
+    )(within, queries, level_weight, *found, out_weight)
+    return own, away, routes
 
 
 def swiglu(gate, up):
@@ -197,31 +217,33 @@
     return place, share
 
 
-def fused_kernel(n_pieces, n_head, capacity, where_ref, routes_ref, *rest):
+def fused_kernel(n_pieces, n_head, n_sub, capacity, routes_ref, *rest):
     piece_refs = rest[:n_pieces]
-    gate_up_ref, down_ref, out_ref, pick_ref, tokens_ref, rows_ref, scale_ref = rest[n_pieces:]
+    gate_up_ref, down_ref = rest[n_pieces : n_pieces + 2]
+    out_refs = rest[n_pieces + 2 : -5]
+    pick_ref, tokens_ref, rows_ref, scale_ref, result_ref = rest[-5:]
     step = pl.program_id(0)
-    experts = pl.num_programs(0)
-    count = scale_ref.shape[1]
+    experts, count = scale_ref.shape[0], scale_ref.shape[1]
     width = tokens_ref.shape[2]
+    all_tokens = routes_ref.shape[1]
+    my_head = lax.axis_index("head")
 
     @pl.when(step == 0)
     def _():
-        my_head = where_ref[1]
+        first = (lax.axis_index("seq") * n_sub + lax.axis_index("sub")) * experts
         size = piece_refs[0].shape[0]
         for number, ref in enumerate(piece_refs):
             block, side = divmod(number, n_head)
             part = (my_head + n_head - side) % n_head
             tokens_ref[part, block * size : (block + 1) * size, :] = ref[...]
-        all_tokens = routes_ref.shape[1]
         named = routes_ref[0:TOPK, :]
         slots = routes_ref[TOPK : 2 * TOPK, :]
         weights = routes_ref[2 * TOPK : 3 * TOPK, :]
         lane = lax.broadcasted_iota(jnp.int32, (1, all_tokens), 1)
         slot_base = (lane // size * capacity).astype(f32)
         row = lax.broadcasted_iota(jnp.int32, (count, all_tokens), 0).astype(f32)
-        for expert in range(scale_ref.shape[0]):
-            name = (where_ref[0] + expert).astype(f32)
+        for expert in range(experts):
+            name = (first + expert).astype(f32)
             place, share = routed(named, slots, weights, name, slot_base)
             chosen = place == row
             scale_ref[expert] = jnp.sum(jnp.where(chosen, share, 0.0), axis=1, keepdims=True)
@@ -241,65 +263,45 @@
         up = up + dot(rows, pair[1, span, :])
     piece = (dot(swiglu(gate, up), down_ref[0]) * scale_ref[step]).astype(bf16)
     for part in range(n_head):
-        out_ref[part] = piece[:, part * width : (part + 1) * width]
-
-
-def run_fused(where, routes, pieces, w_gate_up, w_down, n_head, capacity):
+        result_ref[part, pl.ds(start, count), :] = piece[:, part * width : (part + 1) * width]
+
+    @pl.when(step == experts - 1)
+    def _():
+        tokens = all_tokens // n_sub
+        for number, ref in enumerate(out_refs):
+            hop, side = divmod(number, n_head)
+            part = (my_head + side) % n_head
+            pick = pick_ref[:, hop * tokens : (hop + 1) * tokens]
+            ref[...] = dot(pick, result_ref[part], ((0,), (0,))).astype(ref.dtype)
+
+
+def run_fused(routes, pieces, w_gate_up, w_down, n_head, n_sub, capacity):
     experts, full, _, hidden = w_gate_up.shape
     size, width = pieces[0].shape
     all_tokens = routes.shape[1]
+    tokens = all_tokens // n_sub
     count = all_tokens // size * capacity
+    dtypes = [f32] * n_head + [bf16] * (n_head * (n_sub - 1))
     return pl.pallas_call(
-        functools.partial(fused_kernel, len(pieces), n_head, capacity),
+        functools.partial(fused_kernel, len(pieces), n_head, n_sub, capacity),
         grid=(experts,),
-        in_specs=[scalars(), whole(routes.shape)]
+        in_specs=[whole(routes.shape)]
         + [whole((size, width))] * len(pieces)
         + [
             pl.BlockSpec((1, full, 2, hidden), lambda e: (e, 0, 0, 0)),
             pl.BlockSpec((1, hidden, full), lambda e: (e, 0, 0)),
         ],
-        out_specs=[
-            pl.BlockSpec((n_head, count, width), lambda e: (0, e, 0)),
-            whole((experts * count, all_tokens)),
-        ],
-        out_shape=[
-            jax.ShapeDtypeStruct((n_head, experts * count, width), bf16),
-            jax.ShapeDtypeStruct((experts * count, all_tokens), bf16),
-        ],
+        out_specs=[whole((tokens, width))] * len(dtypes),
+        out_shape=[jax.ShapeDtypeStruct((tokens, width), dtype) for dtype in dtypes],
         scratch_shapes=[
+            pltpu.VMEM((experts * count, all_tokens), bf16),
             pltpu.VMEM((n_head, all_tokens, width), bf16),
             pltpu.VMEM((n_head, experts * count, width), bf16),
             pltpu.VMEM((experts, count, 1), f32),
-        ],
-    )(where, routes, *pieces, w_gate_up, w_down)
-
-
-def combine_kernel(part_ref, pick_ref, rows_ref, *rest):
-    out_ref = rest[-1]
-    value = dot(pick_ref[...], rows_ref[0], ((0,), (0,)))
-    for ref in rest[:-1]:
-        value = value + ref[...].astype(f32)
-    out_ref[...] = value.astype(out_ref.dtype)
-
-
-def run_combine(part, pick, rows, sub, n_sub, extra, dtype):
-    total, all_tokens = pick.shape
-    tokens = all_tokens // n_sub
-    width = rows.shape[2]
-    return pl.pallas_call(
-        combine_kernel,
-        grid_spec=pltpu.PrefetchScalarGridSpec(
-            num_scalar_prefetch=1,
-            grid=(1,),
-            in_specs=[
-                pl.BlockSpec((total, tokens), lambda i, part_ref: (0, sub)),
-                pl.BlockSpec((1, total, width), lambda i, part_ref: (part_ref[0], 0, 0)),
-            ]
-            + [whole((tokens, width))] * len(extra),
-            out_specs=whole((tokens, width)),
-        ),
-        out_shape=jax.ShapeDtypeStruct((tokens, width), dtype),
-    )(part, pick, rows, *extra)
+            pltpu.VMEM((n_head, experts * count, width), bf16),
+        ],
+        compiler_params=grant(44),
+    )(routes, *pieces, w_gate_up, w_down)
 
 
 def on_device(
@@ -323,12 +325,9 @@
     route = jnp.concatenate(
         [expert_ids.astype(f32), expert_slots.astype(f32), route_weight], axis=1
     ).T
-    routes = [route] + [moved(route, "seq", hop) for hop in range(1, n_seq)]
-    routes = jnp.concatenate(routes, axis=1)
-    routes = jnp.concatenate([routes] + [moved(routes, "sub", hop) for hop in range(1, n_sub)], axis=1)
-
-    my_rows, away = attention(
-        queries, keys, values, level_index, level_table, out_weight, my_tokens
+
+    my_rows, away, routes = attention(
+        queries, keys, values, level_index, level_table, out_weight, my_tokens, route
     )
     for hop in range(1, n_sub):
         my_rows = my_rows + moved(away[hop - 1], "sub", hop).astype(f32)
@@ -360,23 +359,25 @@
         pieces = pieces + [
             moved(piece, "sub", hop) for hop in range(1, n_sub) for piece in pieces
         ]
-        where = jnp.stack([first, my_head]).astype(jnp.int32)
-        rows, pick = run_fused(where, routes, pieces, w_gate_up, w_down, n_head, capacity)
-
-        reduced = []
-        for side in [*range(1, n_head), 0]:
-            part = ((my_head + side) % n_head).astype(jnp.int32).reshape(1)
-            extra = [
-                moved(run_combine(part, pick, rows, hop, n_sub, [], bf16), "sub", -hop)
-                for hop in range(1, n_sub)
+        results = run_fused(routes, pieces, w_gate_up, w_down, n_head, n_sub, capacity)
+
+        def reduced(side):
+            value = results[side]
+            for hop in range(1, n_sub):
+                value = value + moved(results[hop * n_head + side], "sub", -hop).astype(f32)
+            return [
+                value[hop * my_tokens : (hop + 1) * my_tokens].astype(bf16 if side else f32)
+                for hop in range(n_seq)
             ]
-            value = run_combine(part, pick, rows, 0, n_sub, extra, bf16 if side else f32)
-            reduced.append(value.reshape(n_seq, my_tokens, width))
+
+        order = [*range(1, n_seq), 0]
+        others = [lax.optimization_barrier(reduced(side)) for side in range(1, n_head)]
+        owns = lax.optimization_barrier(reduced(0))
         expert_sum = 0.0
-        for hop in [*range(1, n_seq), 0]:
-            own = reduced[-1][hop]
+        for hop in order:
+            own = owns[hop]
             for side in range(1, n_head):
-                own = own + moved(reduced[side - 1][hop], "head", side).astype(f32)
+                own = own + moved(others[side - 1][hop], "head", side).astype(f32)
             if hop:
                 own = moved(own.astype(bf16), "seq", -hop).astype(f32)
             expert_sum = expert_sum + own

time: 136 us -> 120 us (0.88)
  Pallas kernels: 47.5 us -> 29 us
  waiting for transfers between devices: 33.6 us -> 44.9 us
  other arithmetic: 10.5 us -> 5.42 us
  starting transfers between devices: 34.9 us -> 30.4 us
    ppermute x29, waiting for transfers between devices: 27.1 us -> 44.9 us  [moved(): return lax.ppermute(value, axis, pairs)]
    pallas_call x6 -> x2, Pallas kernels: 39.6 us -> 26 us  [the longest x1 23.5 us: run_fused(): pl.pallas_call(functools.partial(fused_kernel, len(pieces), n_head, n_sub...]
    ppermute x2, waiting for transfers between devices: 6.52 us -> 0.01 us  [swapped(): return lax.ppermute(value, axis, pairs)]
    ppermute x29, starting transfers between devices: 27.2 us -> 22.8 us  [moved(): return lax.ppermute(value, axis, pairs)]
    pallas_call x1, Pallas kernels: 5.92 us -> 2.71 us  [attention(): pl.pallas_call(functools.partial(project_kernel, levels), grid=(out_width...]
    unnamed x42 -> x18, local copies, waits for them, and re-layouts: 6.42 us -> 9.28 us
    pallas_call x1, Pallas kernels: 1.99 us -> 0.26 us  [attention(): pl.pallas_call(state_kernel, out_shape=jax.ShapeDtypeStruct((heads, HEAD_...]
  transfers between devices with their start and end apart: 31 -> 31, of which waited for: 11 -> 18; matrix products, arithmetic and copies ran while one was open for 8% -> 2% of each run, Pallas kernels for 9% -> 2%
where the time goes in v3:
time: 120 us; the launch traced here: 119 us
  waiting for transfers between devices  44.9 us (37%)
  starting transfers between devices  30.4 us (25%)
  Pallas kernels  29 us (24%)
  local copies, waits for them, and re-layouts  9.5 us (8%)
  other arithmetic  5.42 us (5%)
    ppermute x29, waiting for transfers between devices, moved(): return lax.ppermute(value, axis, pairs)  44.9 us
    pallas_call x1, Pallas kernels, run_fused(): pl.pallas_call(functools.partial(fused_kernel, len(pieces), n_head, n_sub...  23.5 us
    ppermute x29, starting transfers between devices, moved(): return lax.ppermute(value, axis, pairs)  22.8 us
    unnamed x18, local copies, waits for them, and re-layouts  9.28 us
    ppermute x2, starting transfers between devices, swapped(): return lax.ppermute(value, axis, pairs)  7.63 us
    pallas_call x1, Pallas kernels, attention(): pl.pallas_call(functools.partial(project_kernel, levels), grid=(out_width...  2.71 us
    pallas_call x1, Pallas kernels, attention(): pl.pallas_call(within_kernel, in_specs=[scalars()] + [in_vmem] * 4, out_s...  2.53 us
  transfers between devices with their start and end apart: 31, of which 18 were waited for; matrix products, arithmetic and copies ran while one was open for 2% of the time, Pallas kernels for 2%

profile of v3, /device:TPU:0, one launch (start us, length us, event | category | flops | bytes accessed | tf_op | source)
XLA Modules:
  0.0 119.4 jit_solution(16873823556293829631)
XLA Ops:
  0.0 0.9 copy-done.1
  1.0 0.9 copy-done.3
  1.9 0.3 shard_map.127
  2.2 3.1 %collective-permute-start = (bf16[8,128,128]{2,1,0:T(8,128)(2,1)S(1)}, bf16[8,128,128]{2,1,0:T(8,128)(2,1)S(1)}, u32[]{:S(2)}, u32[]{:S(2)}) collective-permute-start(bf16[8,128,128]{2,1,0:T(8,128)(2,1)S(1)} %shard_map.127), channel_id=1, source_target_pairs={{0,4},{4,0},{8,12},{12,8},{1,5},{5,1},{9,13},{13,9},{2,6},{6,2},{1... | collective-permute-start | bytes 786440 | tf_op jit(solution)/shard_map/ppermute | solution.py:31
  5.3 0.7 convert_element_type.81
  6.0 0.7 convert_element_type.82
  6.7 0.9 copy-done.2
  7.6 0.9 copy-done.4
  8.6 0.9 copy-done.5
  9.5 0.7 copy-done.7
  10.2 0.7 copy-done.8
  10.9 2.5 %shard_map.128 = (f32[128,1024]{1,0:T(8,128)S(1)}, f32[128,16]{1,0:T(8,128)S(1)}) custom-call(f32[8,16]{1,0:T(8,128)S(1)} %bitcast.6, bf16[128,1024]{1,0:T(8,128)(2,1)S(1)} %copy-done.5, bf16[128,1024]{1,0:T(8,128)(2,1)S(1)} %copy-done.2, bf16[128,1024]{1,0:T(8,128)(2,1)S(1)} %copy-done.4, s32[21,128]{1,0:T(8,128)S(1)} %bitcast.5), custom_call_target="tpu_custom_call" | custom-call | tf_op jit(solution)/shard_map/pallas_call | solution.py:138
  13.4 0.7 maximum_bitcast_fusion
  14.1 0.1 add_convert_fusion.2
  14.2 4.5 %collective-permute-start.1 = (bf16[8,128,128]{2,1,0:T(8,128)(2,1)S(1)}, bf16[8,128,128]{2,1,0:T(8,128)(2,1)S(1)}, u32[]{:S(2)}, u32[]{:S(2)}) collective-permute-start(bf16[8,128,128]{2,1,0:T(8,128)(2,1)S(1)} %add_convert_fusion.2), channel_id=1, source_target_pairs={{0,8},{4,12},{1,9},{5,13},{2,10},{6,14},{3,11},{7,15},{16,24},{20,... | collective-permute-start | bytes 786440 | tf_op jit(solution)/shard_map/ppermute | solution.py:31
  18.8 1.9 %collective-permute-start.3 = (f32[24,64]{1,0:T(8,128)S(1)}, f32[24,64]{1,0:T(8,128)S(1)}, u32[]{:S(2)}, u32[]{:S(2)}) collective-permute-start(f32[24,64]{1,0:T(8,128)S(1)} %maximum_bitcast_fusion), channel_id=1, source_target_pairs={{0,8},{4,12},{8,0},{12,4},{1,9},{5,13},{9,1},{13,5},{2,10},{6,14},... | collective-permute-start | bytes 18440 | tf_op jit(solution)/shard_map/ppermute | solution.py:25
  20.7 0.1 collective-permute-start.2
  20.8 3.7 %collective-permute-done.4 = f32[24,64]{1,0:T(8,128)S(1)} collective-permute-done((f32[24,64]{1,0:T(8,128)S(1)}, f32[24,64]{1,0:T(8,128)S(1)}, u32[]{:S(2)}, u32[]{:S(2)}) %collective-permute-start.4) | collective-permute-done | bytes 6176 | tf_op jit(solution)/shard_map/ppermute | solution.py:25
  24.6 0.1 collective-permute-done.3
  24.7 1.5 %collective-permute-done.2 = f32[24,64]{1,0:T(8,128)S(1)} collective-permute-done((f32[24,64]{1,0:T(8,128)S(1)}, f32[24,64]{1,0:T(8,128)S(1)}, u32[]{:S(2)}, u32[]{:S(2)}) %collective-permute-start.2) | collective-permute-done | bytes 6176 | tf_op jit(solution)/shard_map/ppermute | solution.py:25
  26.2 0.1 pad_maximum_fusion
  26.3 1.2 collective-permute-done.5
  27.5 0.1 concatenate.12.routes_ref
  27.6 2.2 %copy-done = bf16[1024,2048]{1,0:T(8,128)(2,1)S(1)} copy-done((bf16[1024,2048]{1,0:T(8,128)(2,1)S(1)}, bf16[1024,2048]{1,0:T(8,128)(2,1)}, u32[]{:S(2)}) %copy-start) | copy-done | bytes 4194328
  29.7 0.9 copy-done.6
  30.7 2.7 %shard_map.129 = (f32[64,2048]{1,0:T(8,128)S(1)}, bf16[1,64,2048]{2,1,0:T(8,128)(2,1)S(1)}) custom-call(f32[128,1024]{1,0:T(8,128)S(1)} %get-tuple-element.29.within_ref, bf16[128,1024]{1,0:T(8,128)(2,1)S(1)} %copy-done.6, f32[128,16]{1,0:T(8,128)S(1)} %get-tuple-element.30.level_ref, bf16[8,128,128]{2,1,0:T(8,128)(2,1)S(1)} %collective-permute-done.rest_0_, ...), custom_call_target="tpu_custom_call" | custom-call | tf_op jit(solution)/shard_map/pallas_call | solution.py:165
  33.4 0.2 collective-permute-start.6
  33.7 1.4 %collective-permute-done.6 = bf16[64,2048]{1,0:T(8,128)(2,1)S(1)} collective-permute-done((bf16[64,2048]{1,0:T(8,128)(2,1)S(1)}, bf16[64,2048]{1,0:T(8,128)(2,1)S(1)}, u32[]{:S(2)}, u32[]{:S(2)}) %collective-permute-start.6) | collective-permute-done | bytes 262176 | tf_op jit(solution)/shard_map/ppermute | solution.py:25
  35.1 1.6 %collective-permute-start.7 = (bf16[64,2048]{1,0:T(8,128)(2,1)S(1)}, bf16[64,2048]{1,0:T(8,128)(2,1)S(1)}, u32[]{:S(2)}, u32[]{:S(2)}) collective-permute-start(bf16[64,2048]{1,0:T(8,128)(2,1)S(1)} %add_convert_fusion.1), channel_id=1, source_target_pairs={{0,2},{2,0},{1,3},{3,1},{4,6},{6,4},{5,7},{7,5},{8,10},{10,8},{9,1... | collective-permute-start | bytes 786440 | tf_op jit(solution)/shard_map/ppermute | solution.py:25
  36.6 6.9 %collective-permute-done.7 = bf16[64,2048]{1,0:T(8,128)(2,1)S(1)} collective-permute-done((bf16[64,2048]{1,0:T(8,128)(2,1)S(1)}, bf16[64,2048]{1,0:T(8,128)(2,1)S(1)}, u32[]{:S(2)}, u32[]{:S(2)}) %collective-permute-start.7) | collective-permute-done | bytes 262176 | tf_op jit(solution)/shard_map/ppermute | solution.py:25
  43.5 1.2 multiply_reduce_fusion
  44.7 0.8 multiply_convert_fusion
  45.6 7.6 %collective-permute-start.12 = (bf16[64,1024]{1,0:T(8,128)(2,1)S(1)}, bf16[64,1024]{1,0:T(8,128)(2,1)S(1)}, u32[]{:S(2)}, u32[]{:S(2)}) collective-permute-start(bf16[64,1024]{1,0:T(8,128)(2,1)S(1)} %get-tuple-element.60.rest_0_), channel_id=1, source_target_pairs={{0,12},{4,0},{8,4},{12,8},{1,13},{5,1},{9,5},{13,9},{2,14},{6,2},{... | collective-permute-start | bytes 393224 | tf_op jit(solution)/shard_map/ppermute | solution.py:25
  53.2 1.3 %collective-permute-start.8 = (bf16[64,1024]{1,0:T(8,128)(2,1)S(1)}, bf16[64,1024]{1,0:T(8,128)(2,1)S(1)}, u32[]{:S(2)}, u32[]{:S(2)}) collective-permute-start(bf16[64,1024]{1,0:T(8,128)(2,1)S(1)} %get-tuple-element.60.rest_0_), channel_id=1, source_target_pairs={{0,4},{4,8},{8,12},{12,0},{1,5},{5,9},{9,13},{13,1},{2,6},{6,10},{... | collective-permute-start | bytes 393224 | tf_op jit(solution)/shard_map/ppermute | solution.py:25
  54.5 2.6 %collective-permute-done.12.rest_6_ = bf16[64,1024]{1,0:T(8,128)(2,1)S(1)} collective-permute-done((bf16[64,1024]{1,0:T(8,128)(2,1)S(1)}, bf16[64,1024]{1,0:T(8,128)(2,1)S(1)}, u32[]{:S(2)}, u32[]{:S(2)}) %collective-permute-start.12) | collective-permute-done | bytes 131104 | tf_op jit(solution)/shard_map/ppermute | solution.py:25
  57.1 1.5 %collective-permute-start.13 = (bf16[64,1024]{1,0:T(8,128)(2,1)S(1)}, bf16[64,1024]{1,0:T(8,128)(2,1)S(1)}, u32[]{:S(2)}, u32[]{:S(2)}) collective-permute-start(bf16[64,1024]{1,0:T(8,128)(2,1)S(1)} %collective-permute-done.12.rest_6_), channel_id=1, source_target_pairs={{0,2},{2,0},{1,3},{3,1},{4,6},{6,4},{5,7},{7,5},{8,10},{10,8},{9,1... | collective-permute-start | bytes 393224 | tf_op jit(solution)/shard_map/ppermute | solution.py:25
  58.6 6.0 %collective-permute-done.10.rest_4_ = bf16[64,1024]{1,0:T(8,128)(2,1)S(1)} collective-permute-done((bf16[64,1024]{1,0:T(8,128)(2,1)S(1)}, bf16[64,1024]{1,0:T(8,128)(2,1)S(1)}, u32[]{:S(2)}, u32[]{:S(2)}) %collective-permute-start.10) | collective-permute-done | bytes 131104 | tf_op jit(solution)/shard_map/ppermute | solution.py:25
  64.6 1.5 %collective-permute-start.11 = (bf16[64,1024]{1,0:T(8,128)(2,1)S(1)}, bf16[64,1024]{1,0:T(8,128)(2,1)S(1)}, u32[]{:S(2)}, u32[]{:S(2)}) collective-permute-start(bf16[64,1024]{1,0:T(8,128)(2,1)S(1)} %collective-permute-done.10.rest_4_), channel_id=1, source_target_pairs={{0,2},{2,0},{1,3},{3,1},{4,6},{6,4},{5,7},{7,5},{8,10},{10,8},{9,1... | collective-permute-start | bytes 393224 | tf_op jit(solution)/shard_map/ppermute | solution.py:25
  66.1 0.5 collective-permute-start.9
  66.6 0.5 collective-permute-start.16
  67.1 0.1 collective-permute-start.21
  67.2 3.7 %collective-permute-done.11.rest_5_ = bf16[64,1024]{1,0:T(8,128)(2,1)S(1)} collective-permute-done((bf16[64,1024]{1,0:T(8,128)(2,1)S(1)}, bf16[64,1024]{1,0:T(8,128)(2,1)S(1)}, u32[]{:S(2)}, u32[]{:S(2)}) %collective-permute-start.11) | collective-permute-done | bytes 131104 | tf_op jit(solution)/shard_map/ppermute | solution.py:25
  70.9 1.7 %collective-permute-done.9.rest_3_ = bf16[64,1024]{1,0:T(8,128)(2,1)S(1)} collective-permute-done((bf16[64,1024]{1,0:T(8,128)(2,1)S(1)}, bf16[64,1024]{1,0:T(8,128)(2,1)S(1)}, u32[]{:S(2)}, u32[]{:S(2)}) %collective-permute-start.9) | collective-permute-done | bytes 131104 | tf_op jit(solution)/shard_map/ppermute | solution.py:25
  72.7 1.3 %collective-permute-done.17.rest_11_ = bf16[64,1024]{1,0:T(8,128)(2,1)S(1)} collective-permute-done((bf16[64,1024]{1,0:T(8,128)(2,1)S(1)}, bf16[64,1024]{1,0:T(8,128)(2,1)S(1)}, u32[]{:S(2)}, u32[]{:S(2)}) %collective-permute-start.17) | collective-permute-done | bytes 131104 | tf_op jit(solution)/shard_map/ppermute | solution.py:25
  74.0 23.5 %shard_map.130 = (f32[256,1024]{1,0:T(8,128)S(1)}, f32[256,1024]{1,0:T(8,128)S(1)}, bf16[256,1024]{1,0:T(8,128)(2,1)S(1)}, bf16[256,1024]{1,0:T(8,128)(2,1)S(1)}) custom-call(f32[24,512]{1,0:T(8,128)S(1)} %concatenate.12.routes_ref, bf16[64,1024]{1,0:T(8,128)(2,1)S(1)} %get-tuple-element.60.rest_0_, bf16[64,1024]{1,0:T(8,128)(2,1)S(1)} %get-tuple-element.59.rest_1_, ...), custom_call_target="tpu_custom_call" | custom-call | tf_op jit(solution)/shard_map/pallas_call | solution.py:285
  97.5 0.2 collective-permute-start.23
  97.7 0.4 collective-permute-start.22
  98.1 1.4 %collective-permute-done.23 = bf16[256,1024]{1,0:T(8,128)(2,1)S(1)} collective-permute-done((bf16[256,1024]{1,0:T(8,128)(2,1)S(1)}, bf16[256,1024]{1,0:T(8,128)(2,1)S(1)}, u32[]{:S(2)}, u32[]{:S(2)}) %collective-permute-start.23) | collective-permute-done | bytes 524320 | tf_op jit(solution)/shard_map/ppermute | solution.py:25
  99.5 0.1 add_convert_fusion
  99.7 1.6 %collective-permute-start.24 = (bf16[64,1024]{1,0:T(8,128)(2,1)S(1)}, bf16[64,1024]{1,0:T(8,128)(2,1)S(1)}, u32[]{:S(2)}, u32[]{:S(2)}) collective-permute-start(bf16[64,1024]{1,0:T(8,128)(2,1)S(1)} %get-tuple-element.42), channel_id=1, source_target_pairs={{0,2},{2,0},{1,3},{3,1},{4,6},{6,4},{5,7},{7,5},{8,10},{10,8},{9,1... | collective-permute-start | bytes 393224 | tf_op jit(solution)/shard_map/ppermute | solution.py:25
  101.3 0.2 convert_add_fusion
  101.4 0.1 fusion
  101.5 0.6 collective-permute-start.26
  102.1 1.5 %collective-permute-start.28 = (bf16[64,1024]{1,0:T(8,128)(2,1)S(1)}, bf16[64,1024]{1,0:T(8,128)(2,1)S(1)}, u32[]{:S(2)}, u32[]{:S(2)}) collective-permute-start(bf16[64,1024]{1,0:T(8,128)(2,1)S(1)} %get-tuple-element.46), channel_id=1, source_target_pairs={{0,2},{2,0},{1,3},{3,1},{4,6},{6,4},{5,7},{7,5},{8,10},{10,8},{9,1... | collective-permute-start | bytes 393224 | tf_op jit(solution)/shard_map/ppermute | solution.py:25
  103.6 0.5 collective-permute-start.30
  104.2 2.0 %collective-permute-done.24 = bf16[64,1024]{1,0:T(8,128)(2,1)S(1)} collective-permute-done((bf16[64,1024]{1,0:T(8,128)(2,1)S(1)}, bf16[64,1024]{1,0:T(8,128)(2,1)S(1)}, u32[]{:S(2)}, u32[]{:S(2)}) %collective-permute-start.24) | collective-permute-done | bytes 131104 | tf_op jit(solution)/shard_map/ppermute | solution.py:25
  106.2 1.0 collective-permute-start.25
  107.1 1.8 %collective-permute-done.26 = bf16[64,1024]{1,0:T(8,128)(2,1)S(1)} collective-permute-done((bf16[64,1024]{1,0:T(8,128)(2,1)S(1)}, bf16[64,1024]{1,0:T(8,128)(2,1)S(1)}, u32[]{:S(2)}, u32[]{:S(2)}) %collective-permute-start.26) | collective-permute-done | bytes 131104 | tf_op jit(solution)/shard_map/ppermute | solution.py:25
  109.0 0.1 collective-permute-start.27
  109.1 2.7 %collective-permute-done.28 = bf16[64,1024]{1,0:T(8,128)(2,1)S(1)} collective-permute-done((bf16[64,1024]{1,0:T(8,128)(2,1)S(1)}, bf16[64,1024]{1,0:T(8,128)(2,1)S(1)}, u32[]{:S(2)}, u32[]{:S(2)}) %collective-permute-start.28) | collective-permute-done | bytes 131104 | tf_op jit(solution)/shard_map/ppermute | solution.py:25
  111.8 1.9 %collective-permute-done.30 = bf16[64,1024]{1,0:T(8,128)(2,1)S(1)} collective-permute-done((bf16[64,1024]{1,0:T(8,128)(2,1)S(1)}, bf16[64,1024]{1,0:T(8,128)(2,1)S(1)}, u32[]{:S(2)}, u32[]{:S(2)}) %collective-permute-start.30) | collective-permute-done | bytes 131104 | tf_op jit(solution)/shard_map/ppermute | solution.py:25
  113.7 3.5 %collective-permute-done.27 = bf16[64,1024]{1,0:T(8,128)(2,1)S(1)} collective-permute-done((bf16[64,1024]{1,0:T(8,128)(2,1)S(1)}, bf16[64,1024]{1,0:T(8,128)(2,1)S(1)}, u32[]{:S(2)}, u32[]{:S(2)}) %collective-permute-start.27) | collective-permute-done | bytes 131104 | tf_op jit(solution)/shard_map/ppermute | solution.py:25
  117.3 1.4 %collective-permute-done.29 = bf16[64,1024]{1,0:T(8,128)(2,1)S(1)} collective-permute-done((bf16[64,1024]{1,0:T(8,128)(2,1)S(1)}, bf16[64,1024]{1,0:T(8,128)(2,1)S(1)}, u32[]{:S(2)}, u32[]{:S(2)}) %collective-permute-start.29) | collective-permute-done | bytes 131104 | tf_op jit(solution)/shard_map/ppermute | solution.py:25
  118.7 0.7 add_convert_fusion.3
  (39 shorter events, 0.4 us)
Async XLA Ops:
  0.0 0.9 copy-start.1
  1.0 0.9 copy-start.3
  2.2 12.0 %collective-permute-start = (bf16[8,128,128]{2,1,0:T(8,128)(2,1)S(1)}, bf16[8,128,128]{2,1,0:T(8,128)(2,1)S(1)}, u32[]{:S(2)}, u32[]{:S(2)}) collective-permute-start(bf16[8,128,128]{2,1,0:T(8,128)(2,1)S(1)} %shard_map.127), channel_id=1, source_target_pairs={{0,4},{4,0},{8,12},{12,8},{1,5},{5,1},{9,13},{13,9},{2,6},{6,2},{1... | collective-permute-start | bytes 786440 | tf_op jit(solution)/shard_map/ppermute | solution.py:31
  6.7 0.9 copy-start.2
  7.6 0.9 copy-start.4
  8.6 0.9 copy-start.5
  9.5 0.7 copy-start.7
  10.2 0.7 copy-start.8
  14.2 13.3 %collective-permute-start.1 = (bf16[8,128,128]{2,1,0:T(8,128)(2,1)S(1)}, bf16[8,128,128]{2,1,0:T(8,128)(2,1)S(1)}, u32[]{:S(2)}, u32[]{:S(2)}) collective-permute-start(bf16[8,128,128]{2,1,0:T(8,128)(2,1)S(1)} %add_convert_fusion.2), channel_id=1, source_target_pairs={{0,8},{4,12},{1,9},{5,13},{2,10},{6,14},{3,11},{7,15},{16,24},{20,... | collective-permute-start | bytes 786440 | tf_op jit(solution)/shard_map/ppermute | solution.py:31
  18.7 5.8 %collective-permute-start.4 = (f32[24,64]{1,0:T(8,128)S(1)}, f32[24,64]{1,0:T(8,128)S(1)}, u32[]{:S(2)}, u32[]{:S(2)}) collective-permute-start(f32[24,64]{1,0:T(8,128)S(1)} %maximum_bitcast_fusion), channel_id=1, source_target_pairs={{0,12},{4,0},{8,4},{12,8},{1,13},{5,1},{9,5},{13,9},{2,14},{6,2},{... | collective-permute-start | bytes 18440 | tf_op jit(solution)/shard_map/ppermute | solution.py:25
  18.8 5.9 %collective-permute-start.3 = (f32[24,64]{1,0:T(8,128)S(1)}, f32[24,64]{1,0:T(8,128)S(1)}, u32[]{:S(2)}, u32[]{:S(2)}) collective-permute-start(f32[24,64]{1,0:T(8,128)S(1)} %maximum_bitcast_fusion), channel_id=1, source_target_pairs={{0,8},{4,12},{8,0},{12,4},{1,9},{5,13},{9,1},{13,5},{2,10},{6,14},... | collective-permute-start | bytes 18440 | tf_op jit(solution)/shard_map/ppermute | solution.py:25
  20.7 5.5 %collective-permute-start.2 = (f32[24,64]{1,0:T(8,128)S(1)}, f32[24,64]{1,0:T(8,128)S(1)}, u32[]{:S(2)}, u32[]{:S(2)}) collective-permute-start(f32[24,64]{1,0:T(8,128)S(1)} %maximum_bitcast_fusion), channel_id=1, source_target_pairs={{0,4},{4,8},{8,12},{12,0},{1,5},{5,9},{9,13},{13,1},{2,6},{6,10},{... | collective-permute-start | bytes 18440 | tf_op jit(solution)/shard_map/ppermute | solution.py:25
  26.3 1.2 %collective-permute-start.5 = (f32[24,256]{1,0:T(8,128)S(1)}, f32[24,256]{1,0:T(8,128)S(1)}, u32[]{:S(2)}, u32[]{:S(2)}) collective-permute-start(f32[24,256]{1,0:T(8,128)S(1)} %pad_maximum_fusion), channel_id=1, source_target_pairs={{0,1},{1,0},{2,3},{3,2},{4,5},{5,4},{6,7},{7,6},{8,9},{9,8},{10,11... | collective-permute-start | bytes 73736 | tf_op jit(solution)/shard_map/ppermute | solution.py:25
  27.6 2.2 %copy-start = (bf16[1024,2048]{1,0:T(8,128)(2,1)S(1)}, bf16[1024,2048]{1,0:T(8,128)(2,1)}, u32[]{:S(2)}) copy-start(bf16[1024,2048]{1,0:T(8,128)(2,1)} %rest_2_.1) | copy-start | bytes 12582916
  29.7 0.9 copy-start.6
  33.4 1.6 %collective-permute-start.6 = (bf16[64,2048]{1,0:T(8,128)(2,1)S(1)}, bf16[64,2048]{1,0:T(8,128)(2,1)S(1)}, u32[]{:S(2)}, u32[]{:S(2)}) collective-permute-start(bf16[64,2048]{1,0:T(8,128)(2,1)S(1)} %bitcast.7), channel_id=1, source_target_pairs={{0,1},{1,0},{2,3},{3,2},{4,5},{5,4},{6,7},{7,6},{8,9},{9,8},{10,11... | collective-permute-start | bytes 786440 | tf_op jit(solution)/shard_map/ppermute | solution.py:25
  35.1 8.4 %collective-permute-start.7 = (bf16[64,2048]{1,0:T(8,128)(2,1)S(1)}, bf16[64,2048]{1,0:T(8,128)(2,1)S(1)}, u32[]{:S(2)}, u32[]{:S(2)}) collective-permute-start(bf16[64,2048]{1,0:T(8,128)(2,1)S(1)} %add_convert_fusion.1), channel_id=1, source_target_pairs={{0,2},{2,0},{1,3},{3,1},{4,6},{6,4},{5,7},{7,5},{8,10},{10,8},{9,1... | collective-permute-start | bytes 786440 | tf_op jit(solution)/shard_map/ppermute | solution.py:25
  45.6 11.5 %collective-permute-start.12 = (bf16[64,1024]{1,0:T(8,128)(2,1)S(1)}, bf16[64,1024]{1,0:T(8,128)(2,1)S(1)}, u32[]{:S(2)}, u32[]{:S(2)}) collective-permute-start(bf16[64,1024]{1,0:T(8,128)(2,1)S(1)} %get-tuple-element.60.rest_0_), channel_id=1, source_target_pairs={{0,12},{4,0},{8,4},{12,8},{1,13},{5,1},{9,5},{13,9},{2,14},{6,2},{... | collective-permute-start | bytes 393224 | tf_op jit(solution)/shard_map/ppermute | solution.py:25
  53.2 3.9 %collective-permute-start.15 = (bf16[64,1024]{1,0:T(8,128)(2,1)S(1)}, bf16[64,1024]{1,0:T(8,128)(2,1)S(1)}, u32[]{:S(2)}, u32[]{:S(2)}) collective-permute-start(bf16[64,1024]{1,0:T(8,128)(2,1)S(1)} %get-tuple-element.59.rest_1_), channel_id=1, source_target_pairs={{0,1},{1,0},{2,3},{3,2},{4,5},{5,4},{6,7},{7,6},{8,9},{9,8},{10,11... | collective-permute-start | bytes 393224 | tf_op jit(solution)/shard_map/ppermute | solution.py:25
  53.2 11.4 %collective-permute-start.10 = (bf16[64,1024]{1,0:T(8,128)(2,1)S(1)}, bf16[64,1024]{1,0:T(8,128)(2,1)S(1)}, u32[]{:S(2)}, u32[]{:S(2)}) collective-permute-start(bf16[64,1024]{1,0:T(8,128)(2,1)S(1)} %get-tuple-element.60.rest_0_), channel_id=1, source_target_pairs={{0,8},{4,12},{8,0},{12,4},{1,9},{5,13},{9,1},{13,5},{2,10},{6,14},... | collective-permute-start | bytes 393224 | tf_op jit(solution)/shard_map/ppermute | solution.py:25
  53.2 12.9 %collective-permute-start.8 = (bf16[64,1024]{1,0:T(8,128)(2,1)S(1)}, bf16[64,1024]{1,0:T(8,128)(2,1)S(1)}, u32[]{:S(2)}, u32[]{:S(2)}) collective-permute-start(bf16[64,1024]{1,0:T(8,128)(2,1)S(1)} %get-tuple-element.60.rest_0_), channel_id=1, source_target_pairs={{0,4},{4,8},{8,12},{12,0},{1,5},{5,9},{9,13},{13,1},{2,6},{6,10},{... | collective-permute-start | bytes 393224 | tf_op jit(solution)/shard_map/ppermute | solution.py:25
  54.5 12.1 %collective-permute-start.14 = (bf16[64,1024]{1,0:T(8,128)(2,1)S(1)}, bf16[64,1024]{1,0:T(8,128)(2,1)S(1)}, u32[]{:S(2)}, u32[]{:S(2)}) collective-permute-start(bf16[64,1024]{1,0:T(8,128)(2,1)S(1)} %get-tuple-element.60.rest_0_), channel_id=1, source_target_pairs={{0,1},{1,0},{2,3},{3,2},{4,5},{5,4},{6,7},{7,6},{8,9},{9,8},{10,11... | collective-permute-start | bytes 393224 | tf_op jit(solution)/shard_map/ppermute | solution.py:25
  57.1 9.5 %collective-permute-start.20 = (bf16[64,1024]{1,0:T(8,128)(2,1)S(1)}, bf16[64,1024]{1,0:T(8,128)(2,1)S(1)}, u32[]{:S(2)}, u32[]{:S(2)}) collective-permute-start(bf16[64,1024]{1,0:T(8,128)(2,1)S(1)} %collective-permute-done.12.rest_6_), channel_id=1, source_target_pairs={{0,1},{1,0},{2,3},{3,2},{4,5},{5,4},{6,7},{7,6},{8,9},{9,8},{10,11... | collective-permute-start | bytes 393224 | tf_op jit(solution)/shard_map/ppermute | solution.py:25
  57.1 10.0 %collective-permute-start.13 = (bf16[64,1024]{1,0:T(8,128)(2,1)S(1)}, bf16[64,1024]{1,0:T(8,128)(2,1)S(1)}, u32[]{:S(2)}, u32[]{:S(2)}) collective-permute-start(bf16[64,1024]{1,0:T(8,128)(2,1)S(1)} %collective-permute-done.12.rest_6_), channel_id=1, source_target_pairs={{0,2},{2,0},{1,3},{3,1},{4,6},{6,4},{5,7},{7,5},{8,10},{10,8},{9,1... | collective-permute-start | bytes 393224 | tf_op jit(solution)/shard_map/ppermute | solution.py:25
  64.6 6.4 %collective-permute-start.11 = (bf16[64,1024]{1,0:T(8,128)(2,1)S(1)}, bf16[64,1024]{1,0:T(8,128)(2,1)S(1)}, u32[]{:S(2)}, u32[]{:S(2)}) collective-permute-start(bf16[64,1024]{1,0:T(8,128)(2,1)S(1)} %collective-permute-done.10.rest_4_), channel_id=1, source_target_pairs={{0,2},{2,0},{1,3},{3,1},{4,6},{6,4},{5,7},{7,5},{8,10},{10,8},{9,1... | collective-permute-start | bytes 393224 | tf_op jit(solution)/shard_map/ppermute | solution.py:25
  66.1 6.6 %collective-permute-start.9 = (bf16[64,1024]{1,0:T(8,128)(2,1)S(1)}, bf16[64,1024]{1,0:T(8,128)(2,1)S(1)}, u32[]{:S(2)}, u32[]{:S(2)}) collective-permute-start(bf16[64,1024]{1,0:T(8,128)(2,1)S(1)} %collective-permute-done.8.rest_2_), channel_id=1, source_target_pairs={{0,2},{2,0},{1,3},{3,1},{4,6},{6,4},{5,7},{7,5},{8,10},{10,8},{9,1... | collective-permute-start | bytes 393224 | tf_op jit(solution)/shard_map/ppermute | solution.py:25
  66.6 6.1 %collective-permute-start.18 = (bf16[64,1024]{1,0:T(8,128)(2,1)S(1)}, bf16[64,1024]{1,0:T(8,128)(2,1)S(1)}, u32[]{:S(2)}, u32[]{:S(2)}) collective-permute-start(bf16[64,1024]{1,0:T(8,128)(2,1)S(1)} %collective-permute-done.10.rest_4_), channel_id=1, source_target_pairs={{0,1},{1,0},{2,3},{3,2},{4,5},{5,4},{6,7},{7,6},{8,9},{9,8},{10,11... | collective-permute-start | bytes 393224 | tf_op jit(solution)/shard_map/ppermute | solution.py:25
  66.6 6.1 %collective-permute-start.16 = (bf16[64,1024]{1,0:T(8,128)(2,1)S(1)}, bf16[64,1024]{1,0:T(8,128)(2,1)S(1)}, u32[]{:S(2)}, u32[]{:S(2)}) collective-permute-start(bf16[64,1024]{1,0:T(8,128)(2,1)S(1)} %collective-permute-done.8.rest_2_), channel_id=1, source_target_pairs={{0,1},{1,0},{2,3},{3,2},{4,5},{5,4},{6,7},{7,6},{8,9},{9,8},{10,11... | collective-permute-start | bytes 393224 | tf_op jit(solution)/shard_map/ppermute | solution.py:25
  67.1 5.6 %collective-permute-start.21 = (bf16[64,1024]{1,0:T(8,128)(2,1)S(1)}, bf16[64,1024]{1,0:T(8,128)(2,1)S(1)}, u32[]{:S(2)}, u32[]{:S(2)}) collective-permute-start(bf16[64,1024]{1,0:T(8,128)(2,1)S(1)} %collective-permute-done.13.rest_7_), channel_id=1, source_target_pairs={{0,1},{1,0},{2,3},{3,2},{4,5},{5,4},{6,7},{7,6},{8,9},{9,8},{10,11... | collective-permute-start | bytes 393224 | tf_op jit(solution)/shard_map/ppermute | solution.py:25
  70.9 1.7 %collective-permute-start.19 = (bf16[64,1024]{1,0:T(8,128)(2,1)S(1)}, bf16[64,1024]{1,0:T(8,128)(2,1)S(1)}, u32[]{:S(2)}, u32[]{:S(2)}) collective-permute-start(bf16[64,1024]{1,0:T(8,128)(2,1)S(1)} %collective-permute-done.11.rest_5_), channel_id=1, source_target_pairs={{0,1},{1,0},{2,3},{3,2},{4,5},{5,4},{6,7},{7,6},{8,9},{9,8},{10,11... | collective-permute-start | bytes 393224 | tf_op jit(solution)/shard_map/ppermute | solution.py:25
  72.7 1.3 %collective-permute-start.17 = (bf16[64,1024]{1,0:T(8,128)(2,1)S(1)}, bf16[64,1024]{1,0:T(8,128)(2,1)S(1)}, u32[]{:S(2)}, u32[]{:S(2)}) collective-permute-start(bf16[64,1024]{1,0:T(8,128)(2,1)S(1)} %collective-permute-done.9.rest_3_), channel_id=1, source_target_pairs={{0,1},{1,0},{2,3},{3,2},{4,5},{5,4},{6,7},{7,6},{8,9},{9,8},{10,11... | collective-permute-start | bytes 393224 | tf_op jit(solution)/shard_map/ppermute | solution.py:25
  97.5 2.0 %collective-permute-start.23 = (bf16[256,1024]{1,0:T(8,128)(2,1)S(1)}, bf16[256,1024]{1,0:T(8,128)(2,1)S(1)}, u32[]{:S(2)}, u32[]{:S(2)}) collective-permute-start(bf16[256,1024]{1,0:T(8,128)(2,1)S(1)} %get-tuple-element.41), channel_id=1, source_target_pairs={{0,1},{1,0},{2,3},{3,2},{4,5},{5,4},{6,7},{7,6},{8,9},{9,8},{10,11... | collective-permute-start | bytes 1572872 | tf_op jit(solution)/shard_map/ppermute | solution.py:25
  97.7 3.5 %collective-permute-start.22 = (bf16[256,1024]{1,0:T(8,128)(2,1)S(1)}, bf16[256,1024]{1,0:T(8,128)(2,1)S(1)}, u32[]{:S(2)}, u32[]{:S(2)}) collective-permute-start(bf16[256,1024]{1,0:T(8,128)(2,1)S(1)} %get-tuple-element.38), channel_id=1, source_target_pairs={{0,1},{1,0},{2,3},{3,2},{4,5},{5,4},{6,7},{7,6},{8,9},{9,8},{10,11... | collective-permute-start | bytes 1572872 | tf_op jit(solution)/shard_map/ppermute | solution.py:25
  99.7 6.4 %collective-permute-start.24 = (bf16[64,1024]{1,0:T(8,128)(2,1)S(1)}, bf16[64,1024]{1,0:T(8,128)(2,1)S(1)}, u32[]{:S(2)}, u32[]{:S(2)}) collective-permute-start(bf16[64,1024]{1,0:T(8,128)(2,1)S(1)} %get-tuple-element.42), channel_id=1, source_target_pairs={{0,2},{2,0},{1,3},{3,1},{4,6},{6,4},{5,7},{7,5},{8,10},{10,8},{9,1... | collective-permute-start | bytes 393224 | tf_op jit(solution)/shard_map/ppermute | solution.py:25
  101.5 7.4 %collective-permute-start.26 = (bf16[64,1024]{1,0:T(8,128)(2,1)S(1)}, bf16[64,1024]{1,0:T(8,128)(2,1)S(1)}, u32[]{:S(2)}, u32[]{:S(2)}) collective-permute-start(bf16[64,1024]{1,0:T(8,128)(2,1)S(1)} %get-tuple-element.44), channel_id=1, source_target_pairs={{0,2},{2,0},{1,3},{3,1},{4,6},{6,4},{5,7},{7,5},{8,10},{10,8},{9,1... | collective-permute-start | bytes 393224 | tf_op jit(solution)/shard_map/ppermute | solution.py:25
  102.1 9.6 %collective-permute-start.28 = (bf16[64,1024]{1,0:T(8,128)(2,1)S(1)}, bf16[64,1024]{1,0:T(8,128)(2,1)S(1)}, u32[]{:S(2)}, u32[]{:S(2)}) collective-permute-start(bf16[64,1024]{1,0:T(8,128)(2,1)S(1)} %get-tuple-element.46), channel_id=1, source_target_pairs={{0,2},{2,0},{1,3},{3,1},{4,6},{6,4},{5,7},{7,5},{8,10},{10,8},{9,1... | collective-permute-start | bytes 393224 | tf_op jit(solution)/shard_map/ppermute | solution.py:25
  103.6 10.1 %collective-permute-start.30 = (bf16[64,1024]{1,0:T(8,128)(2,1)S(1)}, bf16[64,1024]{1,0:T(8,128)(2,1)S(1)}, u32[]{:S(2)}, u32[]{:S(2)}) collective-permute-start(bf16[64,1024]{1,0:T(8,128)(2,1)S(1)} %get-tuple-element.48), channel_id=1, source_target_pairs={{0,2},{2,0},{1,3},{3,1},{4,6},{6,4},{5,7},{7,5},{8,10},{10,8},{9,1... | collective-permute-start | bytes 393224 | tf_op jit(solution)/shard_map/ppermute | solution.py:25
  106.2 7.6 %collective-permute-start.25 = (bf16[64,1024]{1,0:T(8,128)(2,1)S(1)}, bf16[64,1024]{1,0:T(8,128)(2,1)S(1)}, u32[]{:S(2)}, u32[]{:S(2)}) collective-permute-start(bf16[64,1024]{1,0:T(8,128)(2,1)S(1)} %add_convert_fusion.6), channel_id=1, source_target_pairs={{0,12},{4,0},{8,4},{12,8},{1,13},{5,1},{9,5},{13,9},{2,14},{6,2},{... | collective-permute-start | bytes 393224 | tf_op jit(solution)/shard_map/ppermute | solution.py:25
  109.0 8.3 %collective-permute-start.27 = (bf16[64,1024]{1,0:T(8,128)(2,1)S(1)}, bf16[64,1024]{1,0:T(8,128)(2,1)S(1)}, u32[]{:S(2)}, u32[]{:S(2)}) collective-permute-start(bf16[64,1024]{1,0:T(8,128)(2,1)S(1)} %add_convert_fusion.5), channel_id=1, source_target_pairs={{0,8},{4,12},{8,0},{12,4},{1,9},{5,13},{9,1},{13,5},{2,10},{6,14},... | collective-permute-start | bytes 393224 | tf_op jit(solution)/shard_map/ppermute | solution.py:25
  111.8 6.9 %collective-permute-start.29 = (bf16[64,1024]{1,0:T(8,128)(2,1)S(1)}, bf16[64,1024]{1,0:T(8,128)(2,1)S(1)}, u32[]{:S(2)}, u32[]{:S(2)}) collective-permute-start(bf16[64,1024]{1,0:T(8,128)(2,1)S(1)} %add_convert_fusion.4), channel_id=1, source_target_pairs={{0,4},{4,8},{8,12},{12,0},{1,5},{5,9},{9,13},{13,1},{2,6},{6,10},{... | collective-permute-start | bytes 393224 | tf_op jit(solution)/shard_map/ppermute | solution.py:25

commit v4 on v3

--- a/solution.py
+++ b/solution.py
@@ -17,6 +17,7 @@
 bf16, f32 = jnp.bfloat16, jnp.float32
 SMEM = pltpu.MemorySpace.SMEM
 VMEM = pltpu.MemorySpace.VMEM
+HBM = pltpu.MemorySpace.HBM
 
 
 def moved(value, axis, distance):
@@ -53,13 +54,38 @@
     return weight
 
 
-def state_kernel(keys_ref, values_ref, out_ref):
+def load_all(sources, targets, sems):
+    copies = [
+        pltpu.make_async_copy(source, target, sems.at[number])
+        for number, (source, target) in enumerate(zip(sources, targets))
+    ]
+    for copy in copies:
+        copy.start()
+    return copies
+
+
+def state_kernel(keys_hbm, values_hbm, out_ref, keys_ref, values_ref, sems):
+    for copy in load_all((keys_hbm, values_hbm), (keys_ref, values_ref), sems):
+        copy.wait()
     for head in range(out_ref.shape[0]):
         span = columns(head)
         out_ref[head] = dot(keys_ref[:, span], values_ref[:, span], ((0,), (0,))).astype(bf16)
 
 
-def within_kernel(table_ref, queries_ref, keys_ref, values_ref, index_ref, out_ref, weight_ref):
+def within_kernel(n_loads, table_ref, *rest):
+    sources = rest[:n_loads]
+    out_ref, weight_ref, route_ref = rest[n_loads : n_loads + 3]
+    kept_refs = rest[n_loads + 3 : n_loads + 6]
+    scratch_refs, sems = rest[n_loads + 6 : -1], rest[-1]
+    queries_ref = kept_refs[0]
+    keys_ref, index_ref, values_ref, ids_ref, slots_ref, share_ref = scratch_refs
+    targets = (queries_ref, *scratch_refs, *kept_refs[1:])
+    copies = load_all(sources, targets, sems)
+    for copy in copies[:7]:
+        copy.wait()
+    route_ref[0:TOPK, :] = ids_ref[...].astype(f32)
+    route_ref[TOPK : 2 * TOPK, :] = slots_ref[...].astype(f32)
+    route_ref[2 * TOPK : 3 * TOPK, :] = share_ref[...]
     block = queries_ref.shape[0]
     heads = queries_ref.shape[1] // HEAD_DIM
     levels = weight_ref.shape[1] // heads
@@ -81,35 +107,44 @@
             owned = (my_block >> level & 1).astype(f32)
             column, slot = LOCAL_LEVELS + level, head * levels + level
             weight_ref[:, slot : slot + 1] = weight[:, column : column + 1] * owned
-
-
-def project_kernel(n_levels, within_ref, queries_ref, level_ref, *rest):
+    for copy in copies[7:]:
+        copy.wait()
+
+
+def project_kernel(n_levels, weight_hbm, within_ref, queries_ref, level_ref, *rest):
     state_refs = rest[:n_levels]
-    weight_ref, own_ref, away_ref, attended_ref = rest[n_levels:]
-
-    @pl.when(pl.program_id(0) == 0)
-    def _():
-        for head in range(queries_ref.shape[1] // HEAD_DIM):
-            span = columns(head)
-            total = within_ref[:, span]
-            joined = jnp.concatenate([ref[head] for ref in state_refs], axis=1)
-            reads = dot(queries_ref[:, span], joined)
-            for level in range(n_levels):
-                slot = head * n_levels + level
-                total = total + level_ref[:, slot : slot + 1] * reads[:, columns(level)]
-            attended_ref[:, span] = (total * HEAD_DIM ** (-0.5)).astype(bf16)
-
+    own_ref, away_ref, attended_ref, weight_ref, sems = rest[n_levels:]
+    chunks = sems.shape[0]
+    step = weight_ref.shape[1] // chunks
+    spans = [slice(chunk * step, (chunk + 1) * step) for chunk in range(chunks)]
+    copies = load_all(
+        [weight_hbm.at[:, span] for span in spans], [weight_ref.at[:, span] for span in spans], sems
+    )
+    for head in range(queries_ref.shape[1] // HEAD_DIM):
+        span = columns(head)
+        total = within_ref[:, span]
+        joined = jnp.concatenate([ref[head] for ref in state_refs], axis=1)
+        reads = dot(queries_ref[:, span], joined)
+        for level in range(n_levels):
+            slot = head * n_levels + level
+            total = total + level_ref[:, slot : slot + 1] * reads[:, columns(level)]
+        attended_ref[:, span] = (total * HEAD_DIM ** (-0.5)).astype(bf16)
     tokens = own_ref.shape[0]
     n_sub = away_ref.shape[0] + 1
     my_sub = lax.axis_index("sub")
-    weight = weight_ref[...]
-    for hop in range(n_sub):
-        start = pl.multiple_of((my_sub + hop) % n_sub * tokens, tokens)
-        value = dot(attended_ref[pl.ds(start, tokens), :], weight)
-        if hop:
-            away_ref[hop - 1] = value.astype(bf16)
-        else:
-            own_ref[...] = value
+    for span, copy in zip(spans, copies):
+        copy.wait()
+        for hop in range(n_sub):
+            start = pl.multiple_of((my_sub + hop) % n_sub * tokens, tokens)
+            value = dot(attended_ref[pl.ds(start, tokens), :], weight_ref[:, span])
+            if hop:
+                away_ref[hop - 1, :, span] = value.astype(bf16)
+            else:
+                own_ref[:, span] = value
+
+
+def pinned(values):
+    return [pltpu.with_memory_space_constraint(value, HBM) for value in values]
 
 
 def grant(mebibytes):
@@ -124,26 +159,51 @@
     return pl.BlockSpec(memory_space=SMEM)
 
 
-def attention(queries, keys, values, level_index, level_table, out_weight, my_tokens, route):
+def attention(
+    queries,
+    keys,
+    values,
+    level_index,
+    level_table,
+    out_weight,
+    residual,
+    norm_gain,
+    expert_ids,
+    expert_slots,
+    route_weight,
+):
     block, width = queries.shape
     heads = width // HEAD_DIM
+    my_tokens = residual.shape[0]
     n_seq, n_sub = lax.axis_size("seq"), lax.axis_size("sub")
+    in_hbm = pl.BlockSpec(memory_space=HBM)
+    in_vmem = pl.BlockSpec(memory_space=VMEM)
     state = pl.pallas_call(
         state_kernel,
+        in_specs=[in_hbm] * 2,
+        out_specs=in_vmem,
         out_shape=jax.ShapeDtypeStruct((heads, HEAD_DIM, HEAD_DIM), bf16),
-        compiler_params=grant(8),
-    )(keys, values)
+        scratch_shapes=[pltpu.VMEM(keys.shape, bf16)] * 2 + [pltpu.SemaphoreType.DMA((2,))],
+        compiler_params=grant(4),
+    )(*pinned([keys, values]))
     levels = n_seq.bit_length() - 1
-    in_vmem = pl.BlockSpec(memory_space=VMEM)
-    within, level_weight = pl.pallas_call(
-        within_kernel,
-        in_specs=[scalars()] + [in_vmem] * 4,
+    scratch = [keys, level_index.T, values, expert_ids.T, expert_slots.T, route_weight.T]
+    kept = [residual, norm_gain]
+    loads = [queries, *scratch, *kept]
+    within, level_weight, route, queries, residual, norm_gain = pl.pallas_call(
+        functools.partial(within_kernel, len(loads)),
+        in_specs=[scalars()] + [in_hbm] * len(loads),
+        out_specs=[in_vmem] * 6,
         out_shape=[
             jax.ShapeDtypeStruct((block, width), f32),
             jax.ShapeDtypeStruct((block, heads * levels), f32),
-        ],
-        compiler_params=grant(8),
-    )(level_table.T, queries, keys, values, level_index.T)
+            jax.ShapeDtypeStruct((3 * TOPK, my_tokens), f32),
+        ]
+        + [jax.ShapeDtypeStruct(value.shape, value.dtype) for value in [queries, *kept]],
+        scratch_shapes=[pltpu.VMEM(value.shape, value.dtype) for value in scratch]
+        + [pltpu.SemaphoreType.DMA((len(loads),))],
+        compiler_params=grant(16),
+    )(level_table.T, *pinned(loads))
     running = state.astype(f32)
     found = []
     for level in range(levels):
@@ -161,25 +221,22 @@
     routes = jnp.concatenate([routes] + [moved(routes, "sub", hop) for hop in range(1, n_sub)], axis=1)
     found[-1], routes = lax.optimization_barrier((found[-1], routes))
     out_width = out_weight.shape[1]
-    step = out_width // 4
     own, away = pl.pallas_call(
         functools.partial(project_kernel, levels),
-        grid=(out_width // step,),
-        in_specs=[whole((block, width)), whole((block, width)), whole(level_weight.shape)]
-        + [whole((heads, HEAD_DIM, HEAD_DIM))] * levels
-        + [pl.BlockSpec((width, step), lambda i: (0, i))],
-        out_specs=[
-            pl.BlockSpec((my_tokens, step), lambda i: (0, i)),
-            pl.BlockSpec((n_sub - 1, my_tokens, step), lambda i: (0, 0, i)),
-        ],
+        in_specs=[in_hbm] + [in_vmem] * (3 + levels),
+        out_specs=[in_vmem] * 2,
         out_shape=[
             jax.ShapeDtypeStruct((my_tokens, out_width), f32),
             jax.ShapeDtypeStruct((n_sub - 1, my_tokens, out_width), bf16),
         ],
-        scratch_shapes=[pltpu.VMEM((block, width), bf16)],
+        scratch_shapes=[
+            pltpu.VMEM((block, width), bf16),
+            pltpu.VMEM((width, out_width), bf16),
+            pltpu.SemaphoreType.DMA((4,)),
+        ],
         compiler_params=grant(12),
-    )(within, queries, level_weight, *found, out_weight)
-    return own, away, routes
+    )(*pinned([out_weight]), within, queries, level_weight, *found)
+    return own, away, routes, residual, norm_gain
 
 
 def swiglu(gate, up):
@@ -217,25 +274,19 @@
     return place, share
 
 
-def fused_kernel(n_pieces, n_head, n_sub, capacity, routes_ref, *rest):
+def gate_kernel(n_pieces, n_sub, capacity, head_ref, routes_ref, *rest):
     piece_refs = rest[:n_pieces]
-    gate_up_ref, down_ref = rest[n_pieces : n_pieces + 2]
-    out_refs = rest[n_pieces + 2 : -5]
-    pick_ref, tokens_ref, rows_ref, scale_ref, result_ref = rest[-5:]
+    gate_up_ref, gate_ref, up_ref, pick_ref, scale_ref, tokens_ref, rows_ref = rest[n_pieces:]
     step = pl.program_id(0)
     experts, count = scale_ref.shape[0], scale_ref.shape[1]
-    width = tokens_ref.shape[2]
     all_tokens = routes_ref.shape[1]
-    my_head = lax.axis_index("head")
 
     @pl.when(step == 0)
     def _():
         first = (lax.axis_index("seq") * n_sub + lax.axis_index("sub")) * experts
         size = piece_refs[0].shape[0]
-        for number, ref in enumerate(piece_refs):
-            block, side = divmod(number, n_head)
-            part = (my_head + n_head - side) % n_head
-            tokens_ref[part, block * size : (block + 1) * size, :] = ref[...]
+        for block, ref in enumerate(piece_refs):
+            tokens_ref[block * size : (block + 1) * size, :] = ref[...]
         named = routes_ref[0:TOPK, :]
         slots = routes_ref[TOPK : 2 * TOPK, :]
         weights = routes_ref[2 * TOPK : 3 * TOPK, :]
@@ -250,24 +301,49 @@
             pick_ref[expert * count : (expert + 1) * count, :] = jnp.where(
                 chosen, 1.0, 0.0
             ).astype(bf16)
-        for part in range(n_head):
-            rows_ref[part] = dot(pick_ref[...], tokens_ref[part]).astype(bf16)
+        rows_ref[...] = dot(pick_ref[...], tokens_ref[...]).astype(bf16)
+
+    rows = rows_ref[pl.ds(pl.multiple_of(step * count, count), count), :]
+    pair = jnp.swapaxes(gate_up_ref[0], 0, 1)
+    gate_ref[0] = dot(rows, pair[0])
+    up_ref[0] = dot(rows, pair[1])
+
+
+def finish_kernel(n_head, n_sub, n_blocks, head_ref, *rest):
+    sides = n_head - 1
+    piece_refs = rest[: sides * n_blocks]
+    gate_up_refs = rest[sides * n_blocks : sides * (n_blocks + 1)]
+    gate_ref, up_ref, down_ref, pick_ref, scale_ref = rest[sides * (n_blocks + 1) :][:5]
+    out_refs = rest[sides * (n_blocks + 1) + 5 : -3]
+    tokens_ref, rows_ref, result_ref = rest[-3:]
+    step = pl.program_id(0)
+    experts, count = scale_ref.shape[0], scale_ref.shape[1]
+    width = tokens_ref.shape[1]
+    my_head = lax.axis_index("head")
+
+    @pl.when(step == 0)
+    def _():
+        size = piece_refs[0].shape[0]
+        for side in range(sides):
+            for block in range(n_blocks):
+                ref = piece_refs[side * n_blocks + block]
+                tokens_ref[block * size : (block + 1) * size, :] = ref[...]
+            rows_ref[side] = dot(pick_ref[...], tokens_ref[...]).astype(bf16)
 
     start = pl.multiple_of(step * count, count)
-    pair = jnp.swapaxes(gate_up_ref[0], 0, 1)
-    gate = up = 0.0
-    for part in range(n_head):
-        rows = rows_ref[part, pl.ds(start, count), :]
-        span = slice(part * width, (part + 1) * width)
-        gate = gate + dot(rows, pair[0, span, :])
-        up = up + dot(rows, pair[1, span, :])
+    gate, up = gate_ref[0], up_ref[0]
+    for side in range(sides):
+        pair = jnp.swapaxes(gate_up_refs[side][0], 0, 1)
+        rows = rows_ref[side, pl.ds(start, count), :]
+        gate = gate + dot(rows, pair[0])
+        up = up + dot(rows, pair[1])
     piece = (dot(swiglu(gate, up), down_ref[0]) * scale_ref[step]).astype(bf16)
     for part in range(n_head):
         result_ref[part, pl.ds(start, count), :] = piece[:, part * width : (part + 1) * width]
 
     @pl.when(step == experts - 1)
     def _():
-        tokens = all_tokens // n_sub
+        tokens = pick_ref.shape[1] // n_sub
         for number, ref in enumerate(out_refs):
             hop, side = divmod(number, n_head)
             part = (my_head + side) % n_head
@@ -275,33 +351,70 @@
             ref[...] = dot(pick, result_ref[part], ((0,), (0,))).astype(ref.dtype)
 
 
-def run_fused(routes, pieces, w_gate_up, w_down, n_head, n_sub, capacity):
+def run_split(routes, pieces, w_gate_up, w_down, n_head, n_sub, capacity):
     experts, full, _, hidden = w_gate_up.shape
     size, width = pieces[0].shape
+    blocks = len(pieces) // n_head
     all_tokens = routes.shape[1]
     tokens = all_tokens // n_sub
     count = all_tokens // size * capacity
+    sides = n_head - 1
+    head = lax.axis_index("head").astype(jnp.int32).reshape(1)
+
+    def columns_of(side):
+        return pl.BlockSpec(
+            (1, width, 2, hidden), lambda e, head_ref: (e, (head_ref[0] + n_head - side) % n_head, 0, 0)
+        )
+
+    w_gate_up, w_down = pinned([w_gate_up, w_down])
+    half = pl.BlockSpec((1, count, hidden), lambda e, head_ref: (e, 0, 0))
+    halves = jax.ShapeDtypeStruct((experts, count, hidden), f32)
+    gate, up, pick, scale = pl.pallas_call(
+        functools.partial(gate_kernel, blocks, n_sub, capacity),
+        grid_spec=pltpu.PrefetchScalarGridSpec(
+            num_scalar_prefetch=1,
+            grid=(experts,),
+            in_specs=[whole(routes.shape)] + [whole((size, width))] * blocks + [columns_of(0)],
+            out_specs=[half, half, whole((experts * count, all_tokens)), whole((experts, count, 1))],
+            scratch_shapes=[
+                pltpu.VMEM((all_tokens, width), bf16),
+                pltpu.VMEM((experts * count, width), bf16),
+            ],
+        ),
+        out_shape=[
+            halves,
+            halves,
+            jax.ShapeDtypeStruct((experts * count, all_tokens), bf16),
+            jax.ShapeDtypeStruct((experts, count, 1), f32),
+        ],
+        compiler_params=grant(24),
+    )(head, routes, *pieces[::n_head], w_gate_up)
+    others = [piece for side in range(1, n_head) for piece in pieces[side::n_head]]
     dtypes = [f32] * n_head + [bf16] * (n_head * (n_sub - 1))
     return pl.pallas_call(
-        functools.partial(fused_kernel, len(pieces), n_head, n_sub, capacity),
-        grid=(experts,),
-        in_specs=[whole(routes.shape)]
-        + [whole((size, width))] * len(pieces)
-        + [
-            pl.BlockSpec((1, full, 2, hidden), lambda e: (e, 0, 0, 0)),
-            pl.BlockSpec((1, hidden, full), lambda e: (e, 0, 0)),
-        ],
-        out_specs=[whole((tokens, width))] * len(dtypes),
+        functools.partial(finish_kernel, n_head, n_sub, blocks),
+        grid_spec=pltpu.PrefetchScalarGridSpec(
+            num_scalar_prefetch=1,
+            grid=(experts,),
+            in_specs=[whole((size, width))] * len(others)
+            + [columns_of(side) for side in range(1, n_head)]
+            + [
+                half,
+                half,
+                pl.BlockSpec((1, hidden, full), lambda e, head_ref: (e, 0, 0)),
+                whole((experts * count, all_tokens)),
+                whole((experts, count, 1)),
+            ],
+            out_specs=[whole((tokens, width))] * len(dtypes),
+            scratch_shapes=[
+                pltpu.VMEM((all_tokens, width), bf16),
+                pltpu.VMEM((sides, experts * count, width), bf16),
+                pltpu.VMEM((n_head, experts * count, width), bf16),
+            ],
+        ),
         out_shape=[jax.ShapeDtypeStruct((tokens, width), dtype) for dtype in dtypes],
-        scratch_shapes=[
-            pltpu.VMEM((experts * count, all_tokens), bf16),
-            pltpu.VMEM((n_head, all_tokens, width), bf16),
-            pltpu.VMEM((n_head, experts * count, width), bf16),
-            pltpu.VMEM((experts, count, 1), f32),
-            pltpu.VMEM((n_head, experts * count, width), bf16),
-        ],
-        compiler_params=grant(44),
-    )(routes, *pieces, w_gate_up, w_down)
+        compiler_params=grant(36),
+    )(head, *others, *[w_gate_up] * sides, gate, up, w_down, pick, scale)
 
 
 def on_device(
@@ -322,12 +435,18 @@
     n_seq, n_head, n_sub = (lax.axis_size(name) for name in ("seq", "head", "sub"))
     my_seq, my_head, my_sub = (lax.axis_index(name) for name in ("seq", "head", "sub"))
     my_tokens = residual.shape[0]
-    route = jnp.concatenate(
-        [expert_ids.astype(f32), expert_slots.astype(f32), route_weight], axis=1
-    ).T
-
-    my_rows, away, routes = attention(
-        queries, keys, values, level_index, level_table, out_weight, my_tokens, route
+    my_rows, away, routes, residual, norm_gain = attention(
+        queries,
+        keys,
+        values,
+        level_index,
+        level_table,
+        out_weight,
+        residual,
+        norm_gain,
+        expert_ids,
+        expert_slots,
+        route_weight,
     )
     for hop in range(1, n_sub):
         my_rows = my_rows + moved(away[hop - 1], "sub", hop).astype(f32)
@@ -359,7 +478,7 @@
         pieces = pieces + [
             moved(piece, "sub", hop) for hop in range(1, n_sub) for piece in pieces
         ]
-        results = run_fused(routes, pieces, w_gate_up, w_down, n_head, n_sub, capacity)
+        results = run_split(routes, pieces, w_gate_up, w_down, n_head, n_sub, capacity)
 
         def reduced(side):
             value = results[side]

time: 120 us -> 120 us (level)
  starting transfers between devices: 30.4 us -> 40.8 us
  local copies, waits for them, and re-layouts: 9.5 us -> 0.91 us
  Pallas kernels: 29 us -> 36.6 us
  waiting for transfers between devices: 44.9 us -> 39.3 us
  other arithmetic: 5.42 us -> 1.65 us
    ppermute x29, starting transfers between devices: 22.8 us -> 33 us  [moved(): return lax.ppermute(value, axis, pairs)]
    unnamed x18 -> x2, local copies, waits for them, and re-layouts: 9.28 us -> 0.69 us
    pallas_call x4 -> x5, Pallas kernels: 29 us -> 36.6 us  [the longest x1 17 us: run_split(): pl.pallas_call(functools.partial(finish_kernel, n_head, n_sub, blocks), g...]
    ppermute x29, waiting for transfers between devices: 44.9 us -> 37.4 us  [moved(): return lax.ppermute(value, axis, pairs)]
    ppermute x2, waiting for transfers between devices: 0.01 us -> 1.88 us  [swapped(): return lax.ppermute(value, axis, pairs)]
    convert_element_type x2 -> x0, other arithmetic: 1.38 us -> none  [the longest x1 0.69 us: on_device(): expert_ids.astype(f32)]
  transfers between devices with their start and end apart: 31 -> 31, of which waited for: 18 -> 16; matrix products, arithmetic and copies ran while one was open for 2% -> 1% of each run, Pallas kernels for 2% -> 13%
where the time goes in v4:
time: 120 us; the launch traced here: 119 us
  starting transfers between devices  40.8 us (34%)
  waiting for transfers between devices  39.3 us (33%)
  Pallas kernels  36.6 us (30%)
  other arithmetic  1.65 us (1%)
    ppermute x29, waiting for transfers between devices, moved(): return lax.ppermute(value, axis, pairs)  37.4 us
    ppermute x29, starting transfers between devices, moved(): return lax.ppermute(value, axis, pairs)  33 us
    pallas_call x1, Pallas kernels, run_split(): pl.pallas_call(functools.partial(finish_kernel, n_head, n_sub, blocks), g...  17 us
    pallas_call x1, Pallas kernels, run_split(): pl.pallas_call(functools.partial(gate_kernel, blocks, n_sub, capacity), g...  11.3 us
    ppermute x2, starting transfers between devices, swapped(): return lax.ppermute(value, axis, pairs)  7.79 us
    pallas_call x1, Pallas kernels, attention(): pl.pallas_call(functools.partial(within_kernel, len(loads)), in_specs=[sc...  3.73 us
    pallas_call x1, Pallas kernels, attention(): pl.pallas_call(functools.partial(project_kernel, levels), in_specs=[in_hb...  3.22 us
  transfers between devices with their start and end apart: 31, of which 16 were waited for; matrix products, arithmetic and copies ran while one was open for 1% of the time, Pallas kernels for 13%

profile of v4, /device:TPU:0, one launch (start us, length us, event | category | flops | bytes accessed | tf_op | source)
XLA Modules:
  0.0 119.4 jit_solution(15655701176062220108)
XLA Ops:
  0.0 1.3 %shard_map.128 = bf16[8,128,128]{2,1,0:T(8,128)(2,1)S(1)} custom-call(bf16[128,1024]{1,0:T(8,128)(2,1)} %keys_hbm.1, bf16[128,1024]{1,0:T(8,128)(2,1)} %values_hbm.1), custom_call_target="tpu_custom_call" | custom-call | tf_op jit(solution)/shard_map/pallas_call | solution.py:181
  1.3 3.1 %collective-permute-start = (bf16[8,128,128]{2,1,0:T(8,128)(2,1)S(1)}, bf16[8,128,128]{2,1,0:T(8,128)(2,1)S(1)}, u32[]{:S(2)}, u32[]{:S(2)}) collective-permute-start(bf16[8,128,128]{2,1,0:T(8,128)(2,1)S(1)} %shard_map.128), channel_id=1, source_target_pairs={{0,4},{4,0},{8,12},{12,8},{1,5},{5,1},{9,13},{13,9},{2,6},{6,2},{1... | collective-permute-start | bytes 786440 | tf_op jit(solution)/shard_map/ppermute | solution.py:32
  4.4 0.7 copy-done
  5.1 3.7 %shard_map.127 = (f32[128,1024]{1,0:T(8,128)S(1)}, f32[128,16]{1,0:T(8,128)S(1)}, f32[24,64]{1,0:T(8,128)S(1)}, bf16[128,1024]{1,0:T(8,128)(2,1)S(1)}, bf16[64,2048]{1,0:T(8,128)(2,1)S(1)}, /*index=5*/f32[2048]{0:T(1024)S(1)}) custom-call(f32[8,16]{1,0:T(8,128)S(1)} %bitcast.7, bf16[128,1024]{1,0:T(8,128)(2,1)} %rest_0_.1, bf16[128,1024]{1,0:T(8,128)(2,1)} %keys_hbm.1, ...), custom_call_target="tpu_custom_call" | custom-call | tf_op jit(solution)/shard_map/pallas_call | solution.py:193
  8.9 1.9 %collective-permute-done.rest_0_ = bf16[8,128,128]{2,1,0:T(8,128)(2,1)S(1)} collective-permute-done((bf16[8,128,128]{2,1,0:T(8,128)(2,1)S(1)}, bf16[8,128,128]{2,1,0:T(8,128)(2,1)S(1)}, u32[]{:S(2)}, u32[]{:S(2)}) %collective-permute-start) | collective-permute-done | bytes 262176 | tf_op jit(solution)/shard_map/ppermute | solution.py:32
  10.7 0.1 add_convert_fusion.2
  10.8 4.7 %collective-permute-start.1 = (bf16[8,128,128]{2,1,0:T(8,128)(2,1)S(1)}, bf16[8,128,128]{2,1,0:T(8,128)(2,1)S(1)}, u32[]{:S(2)}, u32[]{:S(2)}) collective-permute-start(bf16[8,128,128]{2,1,0:T(8,128)(2,1)S(1)} %add_convert_fusion.2), channel_id=1, source_target_pairs={{0,8},{4,12},{1,9},{5,13},{2,10},{6,14},{3,11},{7,15},{16,24},{20,... | collective-permute-start | bytes 786440 | tf_op jit(solution)/shard_map/ppermute | solution.py:32
  15.5 1.6 %collective-permute-start.2 = (f32[24,64]{1,0:T(8,128)S(1)}, f32[24,64]{1,0:T(8,128)S(1)}, u32[]{:S(2)}, u32[]{:S(2)}) collective-permute-start(f32[24,64]{1,0:T(8,128)S(1)} %get-tuple-element.43), channel_id=1, source_target_pairs={{0,4},{4,8},{8,12},{12,0},{1,5},{5,9},{9,13},{13,1},{2,6},{6,10},{... | collective-permute-start | bytes 18440 | tf_op jit(solution)/shard_map/ppermute | solution.py:26
  17.1 0.0 collective-permute-start.3
  17.1 2.4 %collective-permute-start.4 = (f32[24,64]{1,0:T(8,128)S(1)}, f32[24,64]{1,0:T(8,128)S(1)}, u32[]{:S(2)}, u32[]{:S(2)}) collective-permute-start(f32[24,64]{1,0:T(8,128)S(1)} %get-tuple-element.43), channel_id=1, source_target_pairs={{0,12},{4,0},{8,4},{12,8},{1,13},{5,1},{9,5},{13,9},{2,14},{6,2},{... | collective-permute-start | bytes 18440 | tf_op jit(solution)/shard_map/ppermute | solution.py:26
  19.6 1.5 %collective-permute-done.2 = f32[24,64]{1,0:T(8,128)S(1)} collective-permute-done((f32[24,64]{1,0:T(8,128)S(1)}, f32[24,64]{1,0:T(8,128)S(1)}, u32[]{:S(2)}, u32[]{:S(2)}) %collective-permute-start.2) | collective-permute-done | bytes 6176 | tf_op jit(solution)/shard_map/ppermute | solution.py:26
  21.0 0.7 collective-permute-done.3
  21.7 0.0 collective-permute-done.4
  21.7 0.1 pad_maximum_fusion
  21.8 0.0 collective-permute-start.5
  21.8 1.2 collective-permute-done.5
  23.0 0.1 concatenate.8.routes_ref
  23.1 3.2 %shard_map.129 = (f32[64,2048]{1,0:T(8,128)S(1)}, bf16[1,64,2048]{2,1,0:T(8,128)(2,1)S(1)}) custom-call(bf16[1024,2048]{1,0:T(8,128)(2,1)} %weight_hbm.1, f32[128,1024]{1,0:T(8,128)S(1)} %get-tuple-element.39.within_ref, bf16[128,1024]{1,0:T(8,128)(2,1)S(1)} %get-tuple-element.40.queries_ref, f32[128,16]{1,0:T(8,128)S(1)} %get-tuple-element.41.level_ref, ...), custom_call_target="tpu_custom_call" | custom-call | tf_op jit(solution)/shard_map/pallas_call | solution.py:224
  26.3 0.2 collective-permute-start.6
  26.6 1.4 %collective-permute-done.6 = bf16[64,2048]{1,0:T(8,128)(2,1)S(1)} collective-permute-done((bf16[64,2048]{1,0:T(8,128)(2,1)S(1)}, bf16[64,2048]{1,0:T(8,128)(2,1)S(1)}, u32[]{:S(2)}, u32[]{:S(2)}) %collective-permute-start.6) | collective-permute-done | bytes 262176 | tf_op jit(solution)/shard_map/ppermute | solution.py:26
  28.0 1.6 %collective-permute-start.7 = (bf16[64,2048]{1,0:T(8,128)(2,1)S(1)}, bf16[64,2048]{1,0:T(8,128)(2,1)S(1)}, u32[]{:S(2)}, u32[]{:S(2)}) collective-permute-start(bf16[64,2048]{1,0:T(8,128)(2,1)S(1)} %add_convert_fusion.1), channel_id=1, source_target_pairs={{0,2},{2,0},{1,3},{3,1},{4,6},{6,4},{5,7},{7,5},{8,10},{10,8},{9,1... | collective-permute-start | bytes 786440 | tf_op jit(solution)/shard_map/ppermute | solution.py:26
  29.6 6.9 %collective-permute-done.7 = bf16[64,2048]{1,0:T(8,128)(2,1)S(1)} collective-permute-done((bf16[64,2048]{1,0:T(8,128)(2,1)S(1)}, bf16[64,2048]{1,0:T(8,128)(2,1)S(1)}, u32[]{:S(2)}, u32[]{:S(2)}) %collective-permute-start.7) | collective-permute-done | bytes 262176 | tf_op jit(solution)/shard_map/ppermute | solution.py:26
  36.4 0.2 multiply_reduce_fusion
  36.7 0.1 multiply_convert_fusion
  36.8 6.6 %collective-permute-start.8 = (bf16[64,1024]{1,0:T(8,128)(2,1)S(1)}, bf16[64,1024]{1,0:T(8,128)(2,1)S(1)}, u32[]{:S(2)}, u32[]{:S(2)}) collective-permute-start(bf16[64,1024]{1,0:T(8,128)(2,1)S(1)} %get-tuple-element.75.rest_0_), channel_id=1, source_target_pairs={{0,4},{4,8},{8,12},{12,0},{1,5},{5,9},{9,13},{13,1},{2,6},{6,10},{... | collective-permute-start | bytes 393224 | tf_op jit(solution)/shard_map/ppermute | solution.py:26
  43.4 3.4 %collective-permute-start.10 = (bf16[64,1024]{1,0:T(8,128)(2,1)S(1)}, bf16[64,1024]{1,0:T(8,128)(2,1)S(1)}, u32[]{:S(2)}, u32[]{:S(2)}) collective-permute-start(bf16[64,1024]{1,0:T(8,128)(2,1)S(1)} %get-tuple-element.75.rest_0_), channel_id=1, source_target_pairs={{0,8},{4,12},{8,0},{12,4},{1,9},{5,13},{9,1},{13,5},{2,10},{6,14},... | collective-permute-start | bytes 393224 | tf_op jit(solution)/shard_map/ppermute | solution.py:26
  46.8 1.3 %collective-permute-start.12 = (bf16[64,1024]{1,0:T(8,128)(2,1)S(1)}, bf16[64,1024]{1,0:T(8,128)(2,1)S(1)}, u32[]{:S(2)}, u32[]{:S(2)}) collective-permute-start(bf16[64,1024]{1,0:T(8,128)(2,1)S(1)} %get-tuple-element.75.rest_0_), channel_id=1, source_target_pairs={{0,12},{4,0},{8,4},{12,8},{1,13},{5,1},{9,5},{13,9},{2,14},{6,2},{... | collective-permute-start | bytes 393224 | tf_op jit(solution)/shard_map/ppermute | solution.py:26
  48.1 2.6 %collective-permute-done.8.rest_1_ = bf16[64,1024]{1,0:T(8,128)(2,1)S(1)} collective-permute-done((bf16[64,1024]{1,0:T(8,128)(2,1)S(1)}, bf16[64,1024]{1,0:T(8,128)(2,1)S(1)}, u32[]{:S(2)}, u32[]{:S(2)}) %collective-permute-start.8) | collective-permute-done | bytes 131104 | tf_op jit(solution)/shard_map/ppermute | solution.py:26
  50.7 0.0 collective-permute-start.19
  50.7 4.3 %collective-permute-done.10.rest_2_ = bf16[64,1024]{1,0:T(8,128)(2,1)S(1)} collective-permute-done((bf16[64,1024]{1,0:T(8,128)(2,1)S(1)}, bf16[64,1024]{1,0:T(8,128)(2,1)S(1)}, u32[]{:S(2)}, u32[]{:S(2)}) %collective-permute-start.10) | collective-permute-done | bytes 131104 | tf_op jit(solution)/shard_map/ppermute | solution.py:26
  55.0 0.0 collective-permute-start.20
  55.0 1.5 %collective-permute-start.9 = (bf16[64,1024]{1,0:T(8,128)(2,1)S(1)}, bf16[64,1024]{1,0:T(8,128)(2,1)S(1)}, u32[]{:S(2)}, u32[]{:S(2)}) collective-permute-start(bf16[64,1024]{1,0:T(8,128)(2,1)S(1)} %collective-permute-done.8.rest_1_), channel_id=1, source_target_pairs={{0,2},{2,0},{1,3},{3,1},{4,6},{6,4},{5,7},{7,5},{8,10},{10,8},{9,1... | collective-permute-start | bytes 393224 | tf_op jit(solution)/shard_map/ppermute | solution.py:26
  56.5 0.5 collective-permute-start.11
  57.0 1.5 %collective-permute-start.13 = (bf16[64,1024]{1,0:T(8,128)(2,1)S(1)}, bf16[64,1024]{1,0:T(8,128)(2,1)S(1)}, u32[]{:S(2)}, u32[]{:S(2)}) collective-permute-start(bf16[64,1024]{1,0:T(8,128)(2,1)S(1)} %collective-permute-done.12.rest_3_), channel_id=1, source_target_pairs={{0,2},{2,0},{1,3},{3,1},{4,6},{6,4},{5,7},{7,5},{8,10},{10,8},{9,1... | collective-permute-start | bytes 393224 | tf_op jit(solution)/shard_map/ppermute | solution.py:26
  58.5 0.0 collective-permute-done.19.rest_5_
  58.5 0.0 collective-permute-start.21
  58.5 0.0 collective-permute-done.20.rest_6_
  58.5 0.5 collective-permute-start.14
  59.0 2.3 %collective-permute-done.9.rest_1_ = bf16[64,1024]{1,0:T(8,128)(2,1)S(1)} collective-permute-done((bf16[64,1024]{1,0:T(8,128)(2,1)S(1)}, bf16[64,1024]{1,0:T(8,128)(2,1)S(1)}, u32[]{:S(2)}, u32[]{:S(2)}) %collective-permute-start.9) | collective-permute-done | bytes 131104 | tf_op jit(solution)/shard_map/ppermute | solution.py:26
  61.4 2.8 %collective-permute-done.11.rest_2_ = bf16[64,1024]{1,0:T(8,128)(2,1)S(1)} collective-permute-done((bf16[64,1024]{1,0:T(8,128)(2,1)S(1)}, bf16[64,1024]{1,0:T(8,128)(2,1)S(1)}, u32[]{:S(2)}, u32[]{:S(2)}) %collective-permute-start.11) | collective-permute-done | bytes 131104 | tf_op jit(solution)/shard_map/ppermute | solution.py:26
  64.2 2.3 %collective-permute-done.13.rest_3_ = bf16[64,1024]{1,0:T(8,128)(2,1)S(1)} collective-permute-done((bf16[64,1024]{1,0:T(8,128)(2,1)S(1)}, bf16[64,1024]{1,0:T(8,128)(2,1)S(1)}, u32[]{:S(2)}, u32[]{:S(2)}) %collective-permute-start.13) | collective-permute-done | bytes 131104 | tf_op jit(solution)/shard_map/ppermute | solution.py:26
  66.5 11.3 %shard_map.130 = (f32[8,96,384]{2,1,0:T(8,128)S(1)}, f32[8,96,384]{2,1,0:T(8,128)S(1)}, bf16[768,512]{1,0:T(8,128)(2,1)S(1)}, f32[8,96,1]{2,1,0:T(8,128)S(1)}) custom-call(s32[1]{0:T(128)} %bitcast.6.head_ref, f32[24,512]{1,0:T(8,128)S(1)} %concatenate.8.routes_ref, bf16[64,1024]{1,0:T(8,128)(2,1)S(1)} %get-tuple-element.75.rest_0_, ...), custom_call_target="tpu_custom_call" | custom-call | tf_op jit(solution)/shard_map/pallas_call | solution.py:372
  77.9 0.0 collective-permute-done.14.rest_4_
  77.9 0.0 collective-permute-done.16.rest_6_
  77.9 0.0 collective-permute-done.17.rest_7_
  77.9 17.0 %shard_map.131 = (f32[256,1024]{1,0:T(8,128)S(1)}, f32[256,1024]{1,0:T(8,128)S(1)}, bf16[256,1024]{1,0:T(8,128)(2,1)S(1)}, bf16[256,1024]{1,0:T(8,128)(2,1)S(1)}) custom-call(s32[1]{0:T(128)} %bitcast.6.head_ref, bf16[64,1024]{1,0:T(8,128)(2,1)S(1)} %get-tuple-element.76.rest_0_, bf16[64,1024]{1,0:T(8,128)(2,1)S(1)} %collective-permute-done.9.rest_1_, ...), custom_call_target="tpu_custom_call" | custom-call | tf_op jit(solution)/shard_map/pallas_call | solution.py:394
  94.9 0.6 collective-permute-start.23
  95.5 0.1 collective-permute-start.22
  95.5 1.5 %collective-permute-done.23 = bf16[256,1024]{1,0:T(8,128)(2,1)S(1)} collective-permute-done((bf16[256,1024]{1,0:T(8,128)(2,1)S(1)}, bf16[256,1024]{1,0:T(8,128)(2,1)S(1)}, u32[]{:S(2)}, u32[]{:S(2)}) %collective-permute-start.23) | collective-permute-done | bytes 524320 | tf_op jit(solution)/shard_map/ppermute | solution.py:26
  97.0 0.1 add_convert_fusion
  97.2 1.6 %collective-permute-start.24 = (bf16[64,1024]{1,0:T(8,128)(2,1)S(1)}, bf16[64,1024]{1,0:T(8,128)(2,1)S(1)}, u32[]{:S(2)}, u32[]{:S(2)}) collective-permute-start(bf16[64,1024]{1,0:T(8,128)(2,1)S(1)} %get-tuple-element.58), channel_id=1, source_target_pairs={{0,2},{2,0},{1,3},{3,1},{4,6},{6,4},{5,7},{7,5},{8,10},{10,8},{9,1... | collective-permute-start | bytes 393224 | tf_op jit(solution)/shard_map/ppermute | solution.py:26
  98.8 0.1 convert_add_fusion
  99.0 0.1 fusion
  99.1 0.5 collective-permute-start.26
  99.6 1.5 %collective-permute-start.28 = (bf16[64,1024]{1,0:T(8,128)(2,1)S(1)}, bf16[64,1024]{1,0:T(8,128)(2,1)S(1)}, u32[]{:S(2)}, u32[]{:S(2)}) collective-permute-start(bf16[64,1024]{1,0:T(8,128)(2,1)S(1)} %get-tuple-element.62), channel_id=1, source_target_pairs={{0,2},{2,0},{1,3},{3,1},{4,6},{6,4},{5,7},{7,5},{8,10},{10,8},{9,1... | collective-permute-start | bytes 393224 | tf_op jit(solution)/shard_map/ppermute | solution.py:26
  101.2 0.5 collective-permute-start.30
  101.6 2.0 %collective-permute-done.24 = bf16[64,1024]{1,0:T(8,128)(2,1)S(1)} collective-permute-done((bf16[64,1024]{1,0:T(8,128)(2,1)S(1)}, bf16[64,1024]{1,0:T(8,128)(2,1)S(1)}, u32[]{:S(2)}, u32[]{:S(2)}) %collective-permute-start.24) | collective-permute-done | bytes 131104 | tf_op jit(solution)/shard_map/ppermute | solution.py:26
  103.7 4.4 %collective-permute-start.25 = (bf16[64,1024]{1,0:T(8,128)(2,1)S(1)}, bf16[64,1024]{1,0:T(8,128)(2,1)S(1)}, u32[]{:S(2)}, u32[]{:S(2)}) collective-permute-start(bf16[64,1024]{1,0:T(8,128)(2,1)S(1)} %add_convert_fusion.6), channel_id=1, source_target_pairs={{0,12},{4,0},{8,4},{12,8},{1,13},{5,1},{9,5},{13,9},{2,14},{6,2},{... | collective-permute-start | bytes 393224 | tf_op jit(solution)/shard_map/ppermute | solution.py:26
  108.1 0.4 collective-permute-start.27
  108.5 0.8 collective-permute-done.28
  109.3 2.2 %collective-permute-start.29 = (bf16[64,1024]{1,0:T(8,128)(2,1)S(1)}, bf16[64,1024]{1,0:T(8,128)(2,1)S(1)}, u32[]{:S(2)}, u32[]{:S(2)}) collective-permute-start(bf16[64,1024]{1,0:T(8,128)(2,1)S(1)} %add_convert_fusion.4), channel_id=1, source_target_pairs={{0,4},{4,8},{8,12},{12,0},{1,5},{5,9},{9,13},{13,1},{2,6},{6,10},{... | collective-permute-start | bytes 393224 | tf_op jit(solution)/shard_map/ppermute | solution.py:26
  111.5 0.4 collective-permute-done.25
  111.9 6.8 %collective-permute-done.27 = bf16[64,1024]{1,0:T(8,128)(2,1)S(1)} collective-permute-done((bf16[64,1024]{1,0:T(8,128)(2,1)S(1)}, bf16[64,1024]{1,0:T(8,128)(2,1)S(1)}, u32[]{:S(2)}, u32[]{:S(2)}) %collective-permute-start.27) | collective-permute-done | bytes 131104 | tf_op jit(solution)/shard_map/ppermute | solution.py:26
  118.7 0.7 add_convert_fusion.3
  (21 shorter events, 0.2 us)
Async XLA Ops:
  1.3 9.4 %collective-permute-start = (bf16[8,128,128]{2,1,0:T(8,128)(2,1)S(1)}, bf16[8,128,128]{2,1,0:T(8,128)(2,1)S(1)}, u32[]{:S(2)}, u32[]{:S(2)}) collective-permute-start(bf16[8,128,128]{2,1,0:T(8,128)(2,1)S(1)} %shard_map.128), channel_id=1, source_target_pairs={{0,4},{4,0},{8,12},{12,8},{1,5},{5,1},{9,13},{13,9},{2,6},{6,2},{1... | collective-permute-start | bytes 786440 | tf_op jit(solution)/shard_map/ppermute | solution.py:32
  4.4 0.7 copy-start
  10.8 12.3 %collective-permute-start.1 = (bf16[8,128,128]{2,1,0:T(8,128)(2,1)S(1)}, bf16[8,128,128]{2,1,0:T(8,128)(2,1)S(1)}, u32[]{:S(2)}, u32[]{:S(2)}) collective-permute-start(bf16[8,128,128]{2,1,0:T(8,128)(2,1)S(1)} %add_convert_fusion.2), channel_id=1, source_target_pairs={{0,8},{4,12},{1,9},{5,13},{2,10},{6,14},{3,11},{7,15},{16,24},{20,... | collective-permute-start | bytes 786440 | tf_op jit(solution)/shard_map/ppermute | solution.py:32
  15.5 5.5 %collective-permute-start.2 = (f32[24,64]{1,0:T(8,128)S(1)}, f32[24,64]{1,0:T(8,128)S(1)}, u32[]{:S(2)}, u32[]{:S(2)}) collective-permute-start(f32[24,64]{1,0:T(8,128)S(1)} %get-tuple-element.43), channel_id=1, source_target_pairs={{0,4},{4,8},{8,12},{12,0},{1,5},{5,9},{9,13},{13,1},{2,6},{6,10},{... | collective-permute-start | bytes 18440 | tf_op jit(solution)/shard_map/ppermute | solution.py:26
  17.1 4.6 %collective-permute-start.3 = (f32[24,64]{1,0:T(8,128)S(1)}, f32[24,64]{1,0:T(8,128)S(1)}, u32[]{:S(2)}, u32[]{:S(2)}) collective-permute-start(f32[24,64]{1,0:T(8,128)S(1)} %get-tuple-element.43), channel_id=1, source_target_pairs={{0,8},{4,12},{8,0},{12,4},{1,9},{5,13},{9,1},{13,5},{2,10},{6,14},... | collective-permute-start | bytes 18440 | tf_op jit(solution)/shard_map/ppermute | solution.py:26
  17.1 4.6 %collective-permute-start.4 = (f32[24,64]{1,0:T(8,128)S(1)}, f32[24,64]{1,0:T(8,128)S(1)}, u32[]{:S(2)}, u32[]{:S(2)}) collective-permute-start(f32[24,64]{1,0:T(8,128)S(1)} %get-tuple-element.43), channel_id=1, source_target_pairs={{0,12},{4,0},{8,4},{12,8},{1,13},{5,1},{9,5},{13,9},{2,14},{6,2},{... | collective-permute-start | bytes 18440 | tf_op jit(solution)/shard_map/ppermute | solution.py:26
  21.8 1.2 %collective-permute-start.5 = (f32[24,256]{1,0:T(8,128)S(1)}, f32[24,256]{1,0:T(8,128)S(1)}, u32[]{:S(2)}, u32[]{:S(2)}) collective-permute-start(f32[24,256]{1,0:T(8,128)S(1)} %pad_maximum_fusion), channel_id=1, source_target_pairs={{0,1},{1,0},{2,3},{3,2},{4,5},{5,4},{6,7},{7,6},{8,9},{9,8},{10,11... | collective-permute-start | bytes 73736 | tf_op jit(solution)/shard_map/ppermute | solution.py:26
  26.3 1.6 %collective-permute-start.6 = (bf16[64,2048]{1,0:T(8,128)(2,1)S(1)}, bf16[64,2048]{1,0:T(8,128)(2,1)S(1)}, u32[]{:S(2)}, u32[]{:S(2)}) collective-permute-start(bf16[64,2048]{1,0:T(8,128)(2,1)S(1)} %bitcast.8), channel_id=1, source_target_pairs={{0,1},{1,0},{2,3},{3,2},{4,5},{5,4},{6,7},{7,6},{8,9},{9,8},{10,11... | collective-permute-start | bytes 786440 | tf_op jit(solution)/shard_map/ppermute | solution.py:26
  28.0 8.4 %collective-permute-start.7 = (bf16[64,2048]{1,0:T(8,128)(2,1)S(1)}, bf16[64,2048]{1,0:T(8,128)(2,1)S(1)}, u32[]{:S(2)}, u32[]{:S(2)}) collective-permute-start(bf16[64,2048]{1,0:T(8,128)(2,1)S(1)} %add_convert_fusion.1), channel_id=1, source_target_pairs={{0,2},{2,0},{1,3},{3,1},{4,6},{6,4},{5,7},{7,5},{8,10},{10,8},{9,1... | collective-permute-start | bytes 786440 | tf_op jit(solution)/shard_map/ppermute | solution.py:26
  36.8 13.9 %collective-permute-start.8 = (bf16[64,1024]{1,0:T(8,128)(2,1)S(1)}, bf16[64,1024]{1,0:T(8,128)(2,1)S(1)}, u32[]{:S(2)}, u32[]{:S(2)}) collective-permute-start(bf16[64,1024]{1,0:T(8,128)(2,1)S(1)} %get-tuple-element.75.rest_0_), channel_id=1, source_target_pairs={{0,4},{4,8},{8,12},{12,0},{1,5},{5,9},{9,13},{13,1},{2,6},{6,10},{... | collective-permute-start | bytes 393224 | tf_op jit(solution)/shard_map/ppermute | solution.py:26
  43.4 11.5 %collective-permute-start.10 = (bf16[64,1024]{1,0:T(8,128)(2,1)S(1)}, bf16[64,1024]{1,0:T(8,128)(2,1)S(1)}, u32[]{:S(2)}, u32[]{:S(2)}) collective-permute-start(bf16[64,1024]{1,0:T(8,128)(2,1)S(1)} %get-tuple-element.75.rest_0_), channel_id=1, source_target_pairs={{0,8},{4,12},{8,0},{12,4},{1,9},{5,13},{9,1},{13,5},{2,10},{6,14},... | collective-permute-start | bytes 393224 | tf_op jit(solution)/shard_map/ppermute | solution.py:26
  46.8 9.7 %collective-permute-start.12 = (bf16[64,1024]{1,0:T(8,128)(2,1)S(1)}, bf16[64,1024]{1,0:T(8,128)(2,1)S(1)}, u32[]{:S(2)}, u32[]{:S(2)}) collective-permute-start(bf16[64,1024]{1,0:T(8,128)(2,1)S(1)} %get-tuple-element.75.rest_0_), channel_id=1, source_target_pairs={{0,12},{4,0},{8,4},{12,8},{1,13},{5,1},{9,5},{13,9},{2,14},{6,2},{... | collective-permute-start | bytes 393224 | tf_op jit(solution)/shard_map/ppermute | solution.py:26
  48.1 8.9 %collective-permute-start.18 = (bf16[64,1024]{1,0:T(8,128)(2,1)S(1)}, bf16[64,1024]{1,0:T(8,128)(2,1)S(1)}, u32[]{:S(2)}, u32[]{:S(2)}) collective-permute-start(bf16[64,1024]{1,0:T(8,128)(2,1)S(1)} %get-tuple-element.75.rest_0_), channel_id=1, source_target_pairs={{0,1},{1,0},{2,3},{3,2},{4,5},{5,4},{6,7},{7,6},{8,9},{9,8},{10,11... | collective-permute-start | bytes 393224 | tf_op jit(solution)/shard_map/ppermute | solution.py:26
  50.7 7.8 %collective-permute-start.19 = (bf16[64,1024]{1,0:T(8,128)(2,1)S(1)}, bf16[64,1024]{1,0:T(8,128)(2,1)S(1)}, u32[]{:S(2)}, u32[]{:S(2)}) collective-permute-start(bf16[64,1024]{1,0:T(8,128)(2,1)S(1)} %collective-permute-done.8.rest_1_), channel_id=1, source_target_pairs={{0,1},{1,0},{2,3},{3,2},{4,5},{5,4},{6,7},{7,6},{8,9},{9,8},{10,11... | collective-permute-start | bytes 393224 | tf_op jit(solution)/shard_map/ppermute | solution.py:26
  55.0 3.5 %collective-permute-start.20 = (bf16[64,1024]{1,0:T(8,128)(2,1)S(1)}, bf16[64,1024]{1,0:T(8,128)(2,1)S(1)}, u32[]{:S(2)}, u32[]{:S(2)}) collective-permute-start(bf16[64,1024]{1,0:T(8,128)(2,1)S(1)} %collective-permute-done.10.rest_2_), channel_id=1, source_target_pairs={{0,1},{1,0},{2,3},{3,2},{4,5},{5,4},{6,7},{7,6},{8,9},{9,8},{10,11... | collective-permute-start | bytes 393224 | tf_op jit(solution)/shard_map/ppermute | solution.py:26
  55.0 6.4 %collective-permute-start.9 = (bf16[64,1024]{1,0:T(8,128)(2,1)S(1)}, bf16[64,1024]{1,0:T(8,128)(2,1)S(1)}, u32[]{:S(2)}, u32[]{:S(2)}) collective-permute-start(bf16[64,1024]{1,0:T(8,128)(2,1)S(1)} %collective-permute-done.8.rest_1_), channel_id=1, source_target_pairs={{0,2},{2,0},{1,3},{3,1},{4,6},{6,4},{5,7},{7,5},{8,10},{10,8},{9,1... | collective-permute-start | bytes 393224 | tf_op jit(solution)/shard_map/ppermute | solution.py:26
  56.5 7.7 %collective-permute-start.11 = (bf16[64,1024]{1,0:T(8,128)(2,1)S(1)}, bf16[64,1024]{1,0:T(8,128)(2,1)S(1)}, u32[]{:S(2)}, u32[]{:S(2)}) collective-permute-start(bf16[64,1024]{1,0:T(8,128)(2,1)S(1)} %collective-permute-done.10.rest_2_), channel_id=1, source_target_pairs={{0,2},{2,0},{1,3},{3,1},{4,6},{6,4},{5,7},{7,5},{8,10},{10,8},{9,1... | collective-permute-start | bytes 393224 | tf_op jit(solution)/shard_map/ppermute | solution.py:26
  57.0 9.5 %collective-permute-start.13 = (bf16[64,1024]{1,0:T(8,128)(2,1)S(1)}, bf16[64,1024]{1,0:T(8,128)(2,1)S(1)}, u32[]{:S(2)}, u32[]{:S(2)}) collective-permute-start(bf16[64,1024]{1,0:T(8,128)(2,1)S(1)} %collective-permute-done.12.rest_3_), channel_id=1, source_target_pairs={{0,2},{2,0},{1,3},{3,1},{4,6},{6,4},{5,7},{7,5},{8,10},{10,8},{9,1... | collective-permute-start | bytes 393224 | tf_op jit(solution)/shard_map/ppermute | solution.py:26
  58.5 8.0 %collective-permute-start.21 = (bf16[64,1024]{1,0:T(8,128)(2,1)S(1)}, bf16[64,1024]{1,0:T(8,128)(2,1)S(1)}, u32[]{:S(2)}, u32[]{:S(2)}) collective-permute-start(bf16[64,1024]{1,0:T(8,128)(2,1)S(1)} %collective-permute-done.12.rest_3_), channel_id=1, source_target_pairs={{0,1},{1,0},{2,3},{3,2},{4,5},{5,4},{6,7},{7,6},{8,9},{9,8},{10,11... | collective-permute-start | bytes 393224 | tf_op jit(solution)/shard_map/ppermute | solution.py:26
  58.5 19.3 %collective-permute-start.14 = (bf16[64,1024]{1,0:T(8,128)(2,1)S(1)}, bf16[64,1024]{1,0:T(8,128)(2,1)S(1)}, u32[]{:S(2)}, u32[]{:S(2)}) collective-permute-start(bf16[64,1024]{1,0:T(8,128)(2,1)S(1)} %get-tuple-element.76.rest_0_), channel_id=1, source_target_pairs={{0,1},{1,0},{2,3},{3,2},{4,5},{5,4},{6,7},{7,6},{8,9},{9,8},{10,11... | collective-permute-start | bytes 393224 | tf_op jit(solution)/shard_map/ppermute | solution.py:26
  61.4 16.5 %collective-permute-start.15 = (bf16[64,1024]{1,0:T(8,128)(2,1)S(1)}, bf16[64,1024]{1,0:T(8,128)(2,1)S(1)}, u32[]{:S(2)}, u32[]{:S(2)}) collective-permute-start(bf16[64,1024]{1,0:T(8,128)(2,1)S(1)} %collective-permute-done.9.rest_1_), channel_id=1, source_target_pairs={{0,1},{1,0},{2,3},{3,2},{4,5},{5,4},{6,7},{7,6},{8,9},{9,8},{10,11... | collective-permute-start | bytes 393224 | tf_op jit(solution)/shard_map/ppermute | solution.py:26
  64.2 13.7 %collective-permute-start.16 = (bf16[64,1024]{1,0:T(8,128)(2,1)S(1)}, bf16[64,1024]{1,0:T(8,128)(2,1)S(1)}, u32[]{:S(2)}, u32[]{:S(2)}) collective-permute-start(bf16[64,1024]{1,0:T(8,128)(2,1)S(1)} %collective-permute-done.11.rest_2_), channel_id=1, source_target_pairs={{0,1},{1,0},{2,3},{3,2},{4,5},{5,4},{6,7},{7,6},{8,9},{9,8},{10,11... | collective-permute-start | bytes 393224 | tf_op jit(solution)/shard_map/ppermute | solution.py:26
  66.5 11.4 %collective-permute-start.17 = (bf16[64,1024]{1,0:T(8,128)(2,1)S(1)}, bf16[64,1024]{1,0:T(8,128)(2,1)S(1)}, u32[]{:S(2)}, u32[]{:S(2)}) collective-permute-start(bf16[64,1024]{1,0:T(8,128)(2,1)S(1)} %collective-permute-done.13.rest_3_), channel_id=1, source_target_pairs={{0,1},{1,0},{2,3},{3,2},{4,5},{5,4},{6,7},{7,6},{8,9},{9,8},{10,11... | collective-permute-start | bytes 393224 | tf_op jit(solution)/shard_map/ppermute | solution.py:26
  94.9 2.1 %collective-permute-start.23 = (bf16[256,1024]{1,0:T(8,128)(2,1)S(1)}, bf16[256,1024]{1,0:T(8,128)(2,1)S(1)}, u32[]{:S(2)}, u32[]{:S(2)}) collective-permute-start(bf16[256,1024]{1,0:T(8,128)(2,1)S(1)} %get-tuple-element.57), channel_id=1, source_target_pairs={{0,1},{1,0},{2,3},{3,2},{4,5},{5,4},{6,7},{7,6},{8,9},{9,8},{10,11... | collective-permute-start | bytes 1572872 | tf_op jit(solution)/shard_map/ppermute | solution.py:26
  95.5 3.4 %collective-permute-start.22 = (bf16[256,1024]{1,0:T(8,128)(2,1)S(1)}, bf16[256,1024]{1,0:T(8,128)(2,1)S(1)}, u32[]{:S(2)}, u32[]{:S(2)}) collective-permute-start(bf16[256,1024]{1,0:T(8,128)(2,1)S(1)} %get-tuple-element.54), channel_id=1, source_target_pairs={{0,1},{1,0},{2,3},{3,2},{4,5},{5,4},{6,7},{7,6},{8,9},{9,8},{10,11... | collective-permute-start | bytes 1572872 | tf_op jit(solution)/shard_map/ppermute | solution.py:26
  97.2 6.4 %collective-permute-start.24 = (bf16[64,1024]{1,0:T(8,128)(2,1)S(1)}, bf16[64,1024]{1,0:T(8,128)(2,1)S(1)}, u32[]{:S(2)}, u32[]{:S(2)}) collective-permute-start(bf16[64,1024]{1,0:T(8,128)(2,1)S(1)} %get-tuple-element.58), channel_id=1, source_target_pairs={{0,2},{2,0},{1,3},{3,1},{4,6},{6,4},{5,7},{7,5},{8,10},{10,8},{9,1... | collective-permute-start | bytes 393224 | tf_op jit(solution)/shard_map/ppermute | solution.py:26
  99.1 9.0 %collective-permute-start.26 = (bf16[64,1024]{1,0:T(8,128)(2,1)S(1)}, bf16[64,1024]{1,0:T(8,128)(2,1)S(1)}, u32[]{:S(2)}, u32[]{:S(2)}) collective-permute-start(bf16[64,1024]{1,0:T(8,128)(2,1)S(1)} %get-tuple-element.60), channel_id=1, source_target_pairs={{0,2},{2,0},{1,3},{3,1},{4,6},{6,4},{5,7},{7,5},{8,10},{10,8},{9,1... | collective-permute-start | bytes 393224 | tf_op jit(solution)/shard_map/ppermute | solution.py:26
  99.6 9.7 %collective-permute-start.28 = (bf16[64,1024]{1,0:T(8,128)(2,1)S(1)}, bf16[64,1024]{1,0:T(8,128)(2,1)S(1)}, u32[]{:S(2)}, u32[]{:S(2)}) collective-permute-start(bf16[64,1024]{1,0:T(8,128)(2,1)S(1)} %get-tuple-element.62), channel_id=1, source_target_pairs={{0,2},{2,0},{1,3},{3,1},{4,6},{6,4},{5,7},{7,5},{8,10},{10,8},{9,1... | collective-permute-start | bytes 393224 | tf_op jit(solution)/shard_map/ppermute | solution.py:26
  101.2 10.3 %collective-permute-start.30 = (bf16[64,1024]{1,0:T(8,128)(2,1)S(1)}, bf16[64,1024]{1,0:T(8,128)(2,1)S(1)}, u32[]{:S(2)}, u32[]{:S(2)}) collective-permute-start(bf16[64,1024]{1,0:T(8,128)(2,1)S(1)} %get-tuple-element.64), channel_id=1, source_target_pairs={{0,2},{2,0},{1,3},{3,1},{4,6},{6,4},{5,7},{7,5},{8,10},{10,8},{9,1... | collective-permute-start | bytes 393224 | tf_op jit(solution)/shard_map/ppermute | solution.py:26
  103.7 8.3 %collective-permute-start.25 = (bf16[64,1024]{1,0:T(8,128)(2,1)S(1)}, bf16[64,1024]{1,0:T(8,128)(2,1)S(1)}, u32[]{:S(2)}, u32[]{:S(2)}) collective-permute-start(bf16[64,1024]{1,0:T(8,128)(2,1)S(1)} %add_convert_fusion.6), channel_id=1, source_target_pairs={{0,12},{4,0},{8,4},{12,8},{1,13},{5,1},{9,5},{13,9},{2,14},{6,2},{... | collective-permute-start | bytes 393224 | tf_op jit(solution)/shard_map/ppermute | solution.py:26
  108.1 10.6 %collective-permute-start.27 = (bf16[64,1024]{1,0:T(8,128)(2,1)S(1)}, bf16[64,1024]{1,0:T(8,128)(2,1)S(1)}, u32[]{:S(2)}, u32[]{:S(2)}) collective-permute-start(bf16[64,1024]{1,0:T(8,128)(2,1)S(1)} %add_convert_fusion.5), channel_id=1, source_target_pairs={{0,8},{4,12},{8,0},{12,4},{1,9},{5,13},{9,1},{13,5},{2,10},{6,14},... | collective-permute-start | bytes 393224 | tf_op jit(solution)/shard_map/ppermute | solution.py:26
  109.3 9.4 %collective-permute-start.29 = (bf16[64,1024]{1,0:T(8,128)(2,1)S(1)}, bf16[64,1024]{1,0:T(8,128)(2,1)S(1)}, u32[]{:S(2)}, u32[]{:S(2)}) collective-permute-start(bf16[64,1024]{1,0:T(8,128)(2,1)S(1)} %add_convert_fusion.4), channel_id=1, source_target_pairs={{0,4},{4,8},{8,12},{12,0},{1,5},{5,9},{9,13},{13,1},{2,6},{6,10},{... | collective-permute-start | bytes 393224 | tf_op jit(solution)/shard_map/ppermute | solution.py:26
